TPU v7x, 256 devices: a whole 4x4x8 slice. The times are simulated.
256 devices in a mesh: seq: 32 (over z, y), head: 8 (over x, core).
Axes of the slice: x: 4, y: 4, z: 8, core: 2. Of those that a mesh axis runs over, the one named last changes fastest.
Arguments:
- queries: bfloat16 [4096, 24576], P('seq', 'head'), may hold values from -325 to 325
- latents: bfloat16 [4096, 576], P('seq'), may hold values from -5 to 5
- doc_ids: int32 [4096], P('seq'), may hold values from 0 to 15, never falling along the last dimension, each value on 1 to 512 neighbouring positions
- key_weight: bfloat16 [512, 16384], P(None, 'head'), may hold values from -0.25 to 0.25
- value_weight: bfloat16 [512, 16384], P(None, 'head'), may hold values from -0.25 to 0.25
- out_grad: bfloat16 [4096, 16384], P('seq', 'head'), may hold values from -6 to 6
Outputs:
- attended: bfloat16 [4096, 16384], P('seq', 'head')
- latent_grad: float32 [4096, 576], P('seq')
- key_weight_grad: float32 [512, 16384], P('seq', 'head')
- value_weight_grad: float32 [512, 16384], P('seq', 'head')
Inputs may be any that keep to these rules, and one draw needn't show every extreme that they name: `doc_ids`: ids never fall along the sequence; every document holds 1 to 512 tokens, and one holds exactly that many.
All inputs are finite; a program needn't handle non-finite values.
Results may differ from a plain program's by a relative error of at most 0.028.
Values may be sent and summed in bfloat16 or wider, within the bound.
No kernel may reach another device: no remote copies, remote signals or barrier semaphores. Data moves between devices by JAX's collectives and lax.ppermute only.
A program may use at most 128 MiB of HBM per device.

v0:
```python
import math

import jax
import jax.numpy as jnp
from jax import lax
from jax.sharding import Mesh
from jax.sharding import PartitionSpec as P

NOPE = 128
ROPE = 64
VDIM = 128
LATENT = 512
REACH = 4
SEQ = ("seq_0", "seq_1")


def shifted(shard, axis, by):
    devices = lax.axis_size(axis)
    pairs = [(i, i + by) for i in range(devices) if 0 <= i + by < devices]
    return lax.ppermute(shard, axis, pairs)


def summed_rows(terms, axes):
    total = terms.astype(jnp.bfloat16)
    for axis in axes:
        total = lax.psum_scatter(total, axis, scatter_dimension=0, tiled=True)
    return total.astype(jnp.float32)


def sent_to_all(shard, axis):
    copies = jnp.broadcast_to(shard, (lax.axis_size(axis), *shard.shape))
    return lax.all_to_all(copies, axis, split_axis=0, concat_axis=0, tiled=True)


def taken_together(shard, axis):
    return sent_to_all(shard, axis).sum(axis=0)


def attend(
    query_block, grad_block, key_nope, value_up, key_rope, key_ids, key_pos, query_ids, query_pos
):
    query_rows = query_block.shape[0]
    key_rows = key_nope.shape[0]
    head_count = key_nope.shape[1] // NOPE
    score_scale = 1.0 / math.sqrt(NOPE + ROPE)
    query_heads = query_block.reshape(query_rows, head_count, NOPE + ROPE)
    grad_heads = grad_block.reshape(query_rows, head_count, VDIM)
    key_heads = key_nope.reshape(key_rows, head_count, NOPE)
    value_heads = value_up.reshape(key_rows, head_count, VDIM)
    scores = jnp.einsum(
        "phd,thd->hpt", query_heads[:, :, :NOPE], key_heads, preferred_element_type=jnp.float32
    )
    scores = scores + jnp.einsum(
        "phr,tr->hpt", query_heads[:, :, NOPE:], key_rope, preferred_element_type=jnp.float32
    )
    scores = scores * score_scale
    visible = (
        (key_pos[None, :] <= query_pos[:, None])
        & (key_pos[None, :] >= 0)
        & (key_ids[None, :] == query_ids[:, None])
    )
    scores = jnp.where(visible[None], scores, -jnp.inf)
    row_top = jnp.max(scores, axis=-1, keepdims=True)
    row_lse = row_top + jnp.log(jnp.sum(jnp.exp(scores - row_top), axis=-1, keepdims=True))
    weight_f = jnp.exp(scores - row_lse)
    weight_b = weight_f.astype(jnp.bfloat16)
    output = jnp.einsum(
        "hpt,thd->phd", weight_b, value_heads, preferred_element_type=jnp.float32
    ).astype(jnp.bfloat16)
    d_weight = jnp.einsum(
        "phd,thd->hpt", grad_heads, value_heads, preferred_element_type=jnp.float32
    )
    row_delta = jnp.sum(grad_heads.astype(jnp.float32) * output.astype(jnp.float32), axis=-1)
    d_score = (weight_f * (d_weight - jnp.transpose(row_delta)[:, :, None]) * score_scale).astype(
        jnp.bfloat16
    )
    d_key = jnp.einsum(
        "hpt,phd->thd", d_score, query_heads, preferred_element_type=jnp.float32
    ).astype(jnp.bfloat16)
    d_value = jnp.einsum(
        "hpt,phd->thd", weight_b, grad_heads, preferred_element_type=jnp.float32
    ).astype(jnp.bfloat16)
    key_grads = jnp.concatenate(
        [
            d_key[:, :, :NOPE].reshape(key_rows, head_count * NOPE),
            d_value.reshape(key_rows, head_count * VDIM),
        ],
        axis=1,
    )
    rope_grads = d_key[:, :, NOPE:].reshape(key_rows, head_count * ROPE)
    return (output.reshape(query_rows, head_count * VDIM), key_grads, rope_grads)


def fetch_blocks(main_part, rope_part, id_part):
    gathered = [(main_part, rope_part, id_part)]
    for distance in range(1, REACH + 1):
        gathered.append(shifted((main_part, rope_part, id_part), SEQ, distance))
    ordered = gathered[::-1]
    stacked_main = jnp.concatenate([entry[0] for entry in ordered], axis=0)
    stacked_rope = jnp.concatenate([entry[1] for entry in ordered], axis=0)
    stacked_ids = jnp.concatenate([entry[2] for entry in ordered], axis=0)
    return (stacked_main, stacked_rope, stacked_ids)


def per_device(queries, latents, doc_ids, key_weight, value_weight, out_grad):
    tok_rows = latents.shape[0]
    head_count = key_weight.shape[1] // NOPE
    nope_cols = head_count * NOPE
    seq_index = lax.axis_index(SEQ)
    weight_both = jnp.concatenate([key_weight, value_weight], axis=1)
    query_pos = seq_index * tok_rows + jnp.arange(tok_rows, dtype=jnp.int32)
    own_latent = latents[:, :LATENT]
    own_rope = latents[:, LATENT:]
    stacked_main, stacked_rope, key_ids = fetch_blocks(own_latent, own_rope, doc_ids)
    upward = jnp.dot(stacked_main, weight_both, preferred_element_type=jnp.float32).astype(
        jnp.bfloat16
    )
    key_nope = upward[:, :nope_cols]
    value_up = upward[:, nope_cols:]
    key_rows = stacked_main.shape[0]
    key_pos = (seq_index - REACH) * tok_rows + jnp.arange(key_rows, dtype=jnp.int32)
    attended, key_grads, rope_grads = attend(
        queries, out_grad, key_nope, value_up, stacked_rope, key_ids, key_pos, doc_ids, query_pos
    )
    own_start = REACH * tok_rows
    latent_term = jnp.einsum(
        "tc,lc->tl", key_grads, weight_both, preferred_element_type=jnp.float32
    )
    rope_term = jnp.sum(rope_grads.astype(jnp.float32).reshape(key_rows, head_count, ROPE), axis=1)
    partial_grad = jnp.concatenate([latent_term, rope_term], axis=1)
    own_grad = partial_grad[own_start:]
    for distance in range(1, REACH + 1):
        slice_start = (REACH - distance) * tok_rows
        own_grad = own_grad + shifted(
            partial_grad[slice_start : slice_start + tok_rows].astype(jnp.bfloat16), SEQ, -distance
        ).astype(jnp.float32)
    weight_grad = summed_rows(
        jnp.einsum("tl,tc->lc", stacked_main, key_grads, preferred_element_type=jnp.float32), SEQ
    )
    latent_grad = taken_together(own_grad, "head")
    return (attended, latent_grad, weight_grad[:, :nope_cols], weight_grad[:, nope_cols:])


def solution(mesh):
    split = Mesh(mesh.devices.reshape(8, 4, mesh.shape["head"]), ("seq_0", "seq_1", "head"))
    in_specs = (
        P(SEQ, "head"),
        P(SEQ, None),
        P(SEQ),
        P(None, "head"),
        P(None, "head"),
        P(SEQ, "head"),
    )
    out_specs = (P(SEQ, "head"), P(SEQ, None), P(SEQ, "head"), P(SEQ, "head"))
    return jax.shard_map(
        per_device, mesh=split, in_specs=in_specs, out_specs=out_specs, check_vma=False
    )
```

profile of v0, /device:TPU:1, one launch (start us, length us, event | category | flops | bytes accessed | tf_op | source)
XLA Modules:
  0.0 197.5 jit_solution(7285480908923297337)
XLA Ops:
  7.2 4.7 %collective-permute-start.7 = (s32[128]{0:T(128)}, s32[128]{0:T(128)}, u32[]{:S(2)}, u32[]{:S(2)}) collective-permute-start(s32[128]{0:T(128)} %param.8), channel_id=1, source_target_pairs={{0,8},{8,16},{16,24},{24,32},{32,40},{40,48},{48,56},{56,64},{64,7... | collective-permute-start | bytes 1544 | tf_op jit(solution)/shard_map/ppermute | solution.py:20
  11.9 4.6 %collective-permute-start.6 = (s32[128]{0:T(128)}, s32[128]{0:T(128)}, u32[]{:S(2)}, u32[]{:S(2)}) collective-permute-start(s32[128]{0:T(128)} %param.8), channel_id=1, source_target_pairs={{0,16},{8,24},{16,32},{24,40},{32,48},{40,56},{48,64},{56,72},{64,... | collective-permute-start | bytes 1544 | tf_op jit(solution)/shard_map/ppermute | solution.py:20
  16.5 4.3 %collective-permute-start.5 = (s32[128]{0:T(128)}, s32[128]{0:T(128)}, u32[]{:S(2)}, u32[]{:S(2)}) collective-permute-start(s32[128]{0:T(128)} %param.8), channel_id=1, source_target_pairs={{0,24},{8,32},{16,40},{24,48},{32,56},{40,64},{48,72},{56,80},{64,... | collective-permute-start | bytes 1544 | tf_op jit(solution)/shard_map/ppermute | solution.py:20
  20.8 3.6 %collective-permute-start.4 = (s32[128]{0:T(128)}, s32[128]{0:T(128)}, u32[]{:S(2)}, u32[]{:S(2)}) collective-permute-start(s32[128]{0:T(128)} %param.8), channel_id=1, source_target_pairs={{0,32},{8,40},{16,48},{24,56},{32,64},{40,72},{48,80},{56,88},{64,... | collective-permute-start | bytes 1544 | tf_op jit(solution)/shard_map/ppermute | solution.py:20
  25.7 2.9 %collective-permute-start.11 = (bf16[128,64]{0,1:T(8,128)(2,1)}, bf16[128,64]{0,1:T(8,128)(2,1)}, u32[]{:S(2)}, u32[]{:S(2)}) collective-permute-start(bf16[128,64]{0,1:T(8,128)(2,1)} %slice.53), channel_id=1, source_target_pairs={{0,8},{8,16},{16,24},{24,32},{32,40},{40,48},{48,56},{56,64},{64,7... | collective-permute-start | bytes 49160 | tf_op jit(solution)/shard_map/ppermute | solution.py:20
  29.7 3.3 %constant_dynamic-update-slice_fusion.6 = bf16[512,4096]{1,0:T(8,128)(2,1)} fusion(bf16[512,2048]{1,0:T(8,128)(2,1)} %param.9), kind=kLoop, calls=%fused_computation.52 | loop fusion | bytes 4194304
  36.0 3.0 %collective-permute-start.10 = (bf16[128,64]{0,1:T(8,128)(2,1)}, bf16[128,64]{0,1:T(8,128)(2,1)S(1)}, u32[]{:S(2)}, u32[]{:S(2)}) collective-permute-start(bf16[128,64]{0,1:T(8,128)(2,1)} %slice.53), channel_id=1, source_target_pairs={{0,16},{8,24},{16,32},{24,40},{32,48},{40,56},{48,64},{56,72},{64,... | collective-permute-start | bytes 49160 | tf_op jit(solution)/shard_map/ppermute | solution.py:20
  39.6 5.3 %collective-permute-start.9 = (bf16[128,64]{0,1:T(8,128)(2,1)}, bf16[128,64]{0,1:T(8,128)(2,1)S(1)}, u32[]{:S(2)}, u32[]{:S(2)}) collective-permute-start(bf16[128,64]{0,1:T(8,128)(2,1)} %slice.53), channel_id=1, source_target_pairs={{0,24},{8,32},{16,40},{24,48},{32,56},{40,64},{48,72},{56,80},{64,... | collective-permute-start | bytes 49160 | tf_op jit(solution)/shard_map/ppermute | solution.py:20
  45.6 2.9 %collective-permute-start.8 = (bf16[128,64]{0,1:T(8,128)(2,1)}, bf16[128,64]{0,1:T(8,128)(2,1)S(1)}, u32[]{:S(2)}, u32[]{:S(2)}) collective-permute-start(bf16[128,64]{0,1:T(8,128)(2,1)} %slice.53), channel_id=1, source_target_pairs={{0,32},{8,40},{16,48},{24,56},{32,64},{40,72},{48,80},{56,88},{64,... | collective-permute-start | bytes 49160 | tf_op jit(solution)/shard_map/ppermute | solution.py:20
  49.1 2.4 %collective-permute-start.3 = (bf16[128,512]{0,1:T(8,128)(2,1)S(1)}, bf16[128,512]{0,1:T(8,128)(2,1)S(1)}, u32[]{:S(2)}, u32[]{:S(2)}) collective-permute-start(bf16[128,512]{0,1:T(8,128)(2,1)S(1)} %slice.49), channel_id=1, source_target_pairs={{0,8},{8,16},{16,24},{24,32},{32,40},{40,48},{48,56},{56,64},{64,7... | collective-permute-start | bytes 393224 | tf_op jit(solution)/shard_map/ppermute | solution.py:20
  53.8 4.2 %collective-permute-start.2 = (bf16[128,512]{0,1:T(8,128)(2,1)S(1)}, bf16[128,512]{0,1:T(8,128)(2,1)S(1)}, u32[]{:S(2)}, u32[]{:S(2)}) collective-permute-start(bf16[128,512]{0,1:T(8,128)(2,1)S(1)} %slice.49), channel_id=1, source_target_pairs={{0,16},{8,24},{16,32},{24,40},{32,48},{40,56},{48,64},{56,72},{64,... | collective-permute-start | bytes 393224 | tf_op jit(solution)/shard_map/ppermute | solution.py:20
  58.0 4.4 %collective-permute-start.1 = (bf16[128,512]{0,1:T(8,128)(2,1)S(1)}, bf16[128,512]{0,1:T(8,128)(2,1)S(1)}, u32[]{:S(2)}, u32[]{:S(2)}) collective-permute-start(bf16[128,512]{0,1:T(8,128)(2,1)S(1)} %slice.49), channel_id=1, source_target_pairs={{0,24},{8,32},{16,40},{24,48},{32,56},{40,64},{48,72},{56,80},{64,... | collective-permute-start | bytes 393224 | tf_op jit(solution)/shard_map/ppermute | solution.py:20
  62.5 2.6 %collective-permute-start = (bf16[128,512]{0,1:T(8,128)(2,1)S(1)}, bf16[128,512]{0,1:T(8,128)(2,1)S(1)}, u32[]{:S(2)}, u32[]{:S(2)}) collective-permute-start(bf16[128,512]{0,1:T(8,128)(2,1)S(1)} %slice.49), channel_id=1, source_target_pairs={{0,32},{8,40},{16,48},{24,56},{32,64},{40,72},{48,80},{56,88},{64,... | collective-permute-start | bytes 393224 | tf_op jit(solution)/shard_map/ppermute | solution.py:20
  68.1 5.1 %convolution_convert_fusion = bf16[640,4096]{1,0:T(8,128)(2,1)S(1)} fusion(bf16[640,512]{0,1:T(8,128)(2,1)S(1)} %constant_dynamic-update-slice_fusion, bf16[512,4096]{1,0:T(8,128)(2,1)} %constant_dynamic-update-slice_fusion.5), kind=kOutput, calls=%fused_computation | convolution fusion | flops 2686976000 | bytes 10092544 | tf_op jit(solution)/shard_map/dot_general | solution.py:115
  77.4 2.6 %multiply_reduce_fusion = (f32[128,16]{0,1:T(8,128)S(1)}, bf16[16,128,128]{2,1,0:T(8,128)(2,1)}) fusion(bf16[128,2048]{0,1:T(8,128)(2,1)S(1)} %copy.35, f32[16,128,640]{1,2,0:T(8,128)S(1)} %get-tuple-element.25, f32[16,128]{1,0:T(8,128)S(1)} %log_add_fusion, bf16[80,16,8,128]{3,2,1,0:T(8,128)(2,1)S(1)} %get-tuple-element.17), kind=kOutput, calls=%fused_computation.36 | convolution fusion | flops 339474432 | bytes 8929280 | tf_op jit(solution)/shard_map/hpt,thd->phd/dot_general | solution.py:67
  80.0 2.5 %convolution_convert_fusion.2 = bf16[16,640,128]{1,2,0:T(8,128)(2,1)} fusion(bf16[128,16,128]{0,2,1:T(8,128)(2,1)S(1)} %bitcast.63, f32[16,128,640]{1,2,0:T(8,128)S(1)} %get-tuple-element.25, f32[16,128]{1,0:T(8,128)S(1)} %log_add_fusion), kind=kOutput, calls=%fused_computation.30 | convolution fusion | flops 339476480 | bytes 8396800 | tf_op jit(solution)/shard_map/hpt,phd->thd/dot_general | solution.py:80
  82.6 7.2 %convert_bitcast_fusion = bf16[640,16,192]{0,2,1:T(8,128)(2,1)} fusion(bf16[128,16,192]{0,2,1:T(8,128)(2,1)} %bitcast.65, f32[16,128,640]{1,2,0:T(8,128)} %copy-done, f32[16,128]{1,0:T(8,128)S(1)} %bitcast.73, f32[16,128]{1,0:T(8,128)S(1)} %log_add_fusion, bf16[128,16,128]{0,2,1:T(8,128)(2,1)S(1)} %bitcast.64, ...), kind=kOutput, calls=%fused_computation.12 | convolution fusion | flops 847380480 | bytes 13123584 | tf_op jit(solution)/shard_map/hpt,phd->thd/dot_general | solution.py:77
  89.7 2.1 %slice.68 = bf16[640,16,128]{0,2,1:T(8,128)(2,1)S(1)} slice(bf16[640,16,192]{0,2,1:T(8,128)(2,1)} %convert_bitcast_fusion), slice={[0:640], [0:16], [0:128]} | slice | bytes 5242880 | tf_op jit(solution)/shard_map/slice | solution.py:85
  93.4 8.0 %convolution_convert_fusion.1 = bf16[512,4096]{1,0:T(8,128)(2,1)} fusion(bf16[640,512]{0,1:T(8,128)(2,1)S(1)} %copy-done.7, bf16[640,2048]{0,1:T(8,128)(2,1)S(1)} %bitcast.68, bf16[640,2048]{0,1:T(8,128)(2,1)S(1)} %bitcast.70), kind=kOutput, calls=%fused_computation.1 | convolution fusion | flops 2696937472 | bytes 10092544 | tf_op jit(solution)/shard_map/tl,tc->lc/dot_general | solution.py:138
  102.9 6.4 %fusion.5 = f32[640,512]{0,1:T(8,128)S(1)} fusion(bf16[512,4096]{1,0:T(8,128)(2,1)} %constant_dynamic-update-slice_fusion.5, bf16[640,2048]{0,1:T(8,128)(2,1)S(1)} %bitcast.69, bf16[640,2048]{0,1:T(8,128)(2,1)} %bitcast.71), kind=kOutput, calls=%fused_computation.13 | convolution fusion | flops 2694840320 | bytes 10747904 | tf_op jit(solution)/shard_map/tc,lc->tl/dot_general | solution.py:126
  115.8 10.2 %collective-permute-done.15 = bf16[128,576]{0,1:T(8,128)(2,1)S(1)} collective-permute-done((bf16[128,576]{0,1:T(8,128)(2,1)S(1)}, bf16[128,576]{0,1:T(8,128)(2,1)S(1)}, u32[]{:S(2)}, u32[]{:S(2)}) %collective-permute-start.15) | collective-permute-done | bytes 147488 | tf_op jit(solution)/shard_map/ppermute | solution.py:20
  127.8 10.9 %all-to-all-start = ((f32[8,128,576]{1,2,0:T(8,128)}), f32[8,128,576]{1,2,0:T(8,128)S(1)}, u32[]{:S(2)}, u32[]{:S(2)}) async-start(f32[8,128,576]{1,2,0:T(8,128)} %broadcast_in_dim.16), calls=%async_computation | async-start | bytes 4718592 | tf_op jit(solution)/shard_map/all_to_all | solution.py:32
  138.6 28.8 %reduce-scatter.3.cloned.1.call-done = bf16[64,4096]{1,0:T(8,128)(2,1)} async-done(((bf16[512,4096]{1,0:T(8,128)(2,1)}), bf16[64,4096]{1,0:T(8,128)(2,1)}) %reduce-scatter.3.cloned.1.call-update) | async-done | bytes 524304 | tf_op jit(solution)/shard_map/reduce_scatter | solution.py:26
  169.3 19.7 %reduce-scatter.5.cloned.1.call-done = bf16[16,4096]{1,0:T(8,128)(2,1)} async-done(((bf16[64,4096]{1,0:T(8,128)(2,1)}), bf16[16,4096]{1,0:T(8,128)(2,1)}) %reduce-scatter.5.cloned.1.call-update) | async-done | bytes 131088 | tf_op jit(solution)/shard_map/reduce_scatter | solution.py:26
  (84 shorter events, 31.4 us)
Async XLA Ops:
  7.2 25.8 %copy-start.5 = (bf16[512,2048]{1,0:T(8,128)(2,1)S(1)}, bf16[512,2048]{1,0:T(8,128)(2,1)}, u32[]{:S(2)}) copy-start(bf16[512,2048]{1,0:T(8,128)(2,1)} %param.10) | copy-start | bytes 6291460
  7.2 160.3 %reduce-scatter.3.cloned.1.call-start = ((), (), s32[]{:S(2)}) async-start(), calls=%async_computation.3 | async-start | bytes 4718592 | tf_op jit(solution)/shard_map/reduce_scatter | solution.py:26
  7.2 41.9 %collective-permute-start.7 = (s32[128]{0:T(128)}, s32[128]{0:T(128)}, u32[]{:S(2)}, u32[]{:S(2)}) collective-permute-start(s32[128]{0:T(128)} %param.8), channel_id=1, source_target_pairs={{0,8},{8,16},{16,24},{24,32},{32,40},{40,48},{48,56},{56,64},{64,7... | collective-permute-start | bytes 1544 | tf_op jit(solution)/shard_map/ppermute | solution.py:20
  11.9 33.7 %collective-permute-start.6 = (s32[128]{0:T(128)}, s32[128]{0:T(128)}, u32[]{:S(2)}, u32[]{:S(2)}) collective-permute-start(s32[128]{0:T(128)} %param.8), channel_id=1, source_target_pairs={{0,16},{8,24},{16,32},{24,40},{32,48},{40,56},{48,64},{56,72},{64,... | collective-permute-start | bytes 1544 | tf_op jit(solution)/shard_map/ppermute | solution.py:20
  16.5 23.2 %collective-permute-start.5 = (s32[128]{0:T(128)}, s32[128]{0:T(128)}, u32[]{:S(2)}, u32[]{:S(2)}) collective-permute-start(s32[128]{0:T(128)} %param.8), channel_id=1, source_target_pairs={{0,24},{8,32},{16,40},{24,48},{32,56},{40,64},{48,72},{56,80},{64,... | collective-permute-start | bytes 1544 | tf_op jit(solution)/shard_map/ppermute | solution.py:20
  20.8 15.2 %collective-permute-start.4 = (s32[128]{0:T(128)}, s32[128]{0:T(128)}, u32[]{:S(2)}, u32[]{:S(2)}) collective-permute-start(s32[128]{0:T(128)} %param.8), channel_id=1, source_target_pairs={{0,32},{8,40},{16,48},{24,56},{32,64},{40,72},{48,80},{56,88},{64,... | collective-permute-start | bytes 1544 | tf_op jit(solution)/shard_map/ppermute | solution.py:20
  25.7 39.5 %collective-permute-start.11 = (bf16[128,64]{0,1:T(8,128)(2,1)}, bf16[128,64]{0,1:T(8,128)(2,1)}, u32[]{:S(2)}, u32[]{:S(2)}) collective-permute-start(bf16[128,64]{0,1:T(8,128)(2,1)} %slice.53), channel_id=1, source_target_pairs={{0,8},{8,16},{16,24},{24,32},{32,40},{40,48},{48,56},{56,64},{64,7... | collective-permute-start | bytes 49160 | tf_op jit(solution)/shard_map/ppermute | solution.py:20
  29.7 4.8 %copy-start.9 = (bf16[128,576]{0,1:T(8,128)(2,1)S(1)}, bf16[128,576]{0,1:T(8,128)(2,1)}, u32[]{:S(2)}) copy-start(bf16[128,576]{0,1:T(8,128)(2,1)} %param.7) | copy-start | bytes 442372
  29.7 4.8 %copy-start.10 = (bf16[128,2048]{1,0:T(8,128)(2,1)S(1)}, bf16[128,2048]{1,0:T(8,128)(2,1)}, u32[]{:S(2)}) copy-start(bf16[128,2048]{1,0:T(8,128)(2,1)} %param.11) | copy-start | bytes 1572868
  29.7 5.1 %copy-start.8 = (bf16[128,3072]{1,0:T(8,128)(2,1)S(1)}, bf16[128,3072]{1,0:T(8,128)(2,1)}, u32[]{:S(2)}) copy-start(bf16[128,3072]{1,0:T(8,128)(2,1)} %param.6) | copy-start | bytes 2359300
  36.0 26.5 %collective-permute-start.10 = (bf16[128,64]{0,1:T(8,128)(2,1)}, bf16[128,64]{0,1:T(8,128)(2,1)S(1)}, u32[]{:S(2)}, u32[]{:S(2)}) collective-permute-start(bf16[128,64]{0,1:T(8,128)(2,1)} %slice.53), channel_id=1, source_target_pairs={{0,16},{8,24},{16,32},{24,40},{32,48},{40,56},{48,64},{56,72},{64,... | collective-permute-start | bytes 49160 | tf_op jit(solution)/shard_map/ppermute | solution.py:20
  39.6 18.3 %collective-permute-start.9 = (bf16[128,64]{0,1:T(8,128)(2,1)}, bf16[128,64]{0,1:T(8,128)(2,1)S(1)}, u32[]{:S(2)}, u32[]{:S(2)}) collective-permute-start(bf16[128,64]{0,1:T(8,128)(2,1)} %slice.53), channel_id=1, source_target_pairs={{0,24},{8,32},{16,40},{24,48},{32,56},{40,64},{48,72},{56,80},{64,... | collective-permute-start | bytes 49160 | tf_op jit(solution)/shard_map/ppermute | solution.py:20
  45.6 8.2 %collective-permute-start.8 = (bf16[128,64]{0,1:T(8,128)(2,1)}, bf16[128,64]{0,1:T(8,128)(2,1)S(1)}, u32[]{:S(2)}, u32[]{:S(2)}) collective-permute-start(bf16[128,64]{0,1:T(8,128)(2,1)} %slice.53), channel_id=1, source_target_pairs={{0,32},{8,40},{16,48},{24,56},{32,64},{40,72},{48,80},{56,88},{64,... | collective-permute-start | bytes 49160 | tf_op jit(solution)/shard_map/ppermute | solution.py:20
  49.1 18.0 %collective-permute-start.3 = (bf16[128,512]{0,1:T(8,128)(2,1)S(1)}, bf16[128,512]{0,1:T(8,128)(2,1)S(1)}, u32[]{:S(2)}, u32[]{:S(2)}) collective-permute-start(bf16[128,512]{0,1:T(8,128)(2,1)S(1)} %slice.49), channel_id=1, source_target_pairs={{0,8},{8,16},{16,24},{24,32},{32,40},{40,48},{48,56},{56,64},{64,7... | collective-permute-start | bytes 393224 | tf_op jit(solution)/shard_map/ppermute | solution.py:20
  53.8 13.3 %collective-permute-start.2 = (bf16[128,512]{0,1:T(8,128)(2,1)S(1)}, bf16[128,512]{0,1:T(8,128)(2,1)S(1)}, u32[]{:S(2)}, u32[]{:S(2)}) collective-permute-start(bf16[128,512]{0,1:T(8,128)(2,1)S(1)} %slice.49), channel_id=1, source_target_pairs={{0,16},{8,24},{16,32},{24,40},{32,48},{40,56},{48,64},{56,72},{64,... | collective-permute-start | bytes 393224 | tf_op jit(solution)/shard_map/ppermute | solution.py:20
  58.0 9.1 %collective-permute-start.1 = (bf16[128,512]{0,1:T(8,128)(2,1)S(1)}, bf16[128,512]{0,1:T(8,128)(2,1)S(1)}, u32[]{:S(2)}, u32[]{:S(2)}) collective-permute-start(bf16[128,512]{0,1:T(8,128)(2,1)S(1)} %slice.49), channel_id=1, source_target_pairs={{0,24},{8,32},{16,40},{24,48},{32,56},{40,64},{48,72},{56,80},{64,... | collective-permute-start | bytes 393224 | tf_op jit(solution)/shard_map/ppermute | solution.py:20
  62.5 4.6 %collective-permute-start = (bf16[128,512]{0,1:T(8,128)(2,1)S(1)}, bf16[128,512]{0,1:T(8,128)(2,1)S(1)}, u32[]{:S(2)}, u32[]{:S(2)}) collective-permute-start(bf16[128,512]{0,1:T(8,128)(2,1)S(1)} %slice.49), channel_id=1, source_target_pairs={{0,32},{8,40},{16,48},{24,56},{32,64},{40,72},{48,80},{56,88},{64,... | collective-permute-start | bytes 393224 | tf_op jit(solution)/shard_map/ppermute | solution.py:20
  109.5 6.3 %collective-permute-start.12 = (bf16[128,576]{0,1:T(8,128)(2,1)S(1)}, bf16[128,576]{0,1:T(8,128)(2,1)S(1)}, u32[]{:S(2)}, u32[]{:S(2)}) collective-permute-start(bf16[128,576]{0,1:T(8,128)(2,1)S(1)} %get-tuple-element.18), channel_id=1, source_target_pairs={{8,0},{16,8},{24,16},{32,24},{40,32},{48,40},{56,48},{64,56},{72,6... | collective-permute-start | bytes 442376 | tf_op jit(solution)/shard_map/ppermute | solution.py:20
  110.8 15.2 %collective-permute-start.15 = (bf16[128,576]{0,1:T(8,128)(2,1)S(1)}, bf16[128,576]{0,1:T(8,128)(2,1)S(1)}, u32[]{:S(2)}, u32[]{:S(2)}) collective-permute-start(bf16[128,576]{0,1:T(8,128)(2,1)S(1)} %get-tuple-element.19), channel_id=1, source_target_pairs={{32,0},{40,8},{48,16},{56,24},{64,32},{72,40},{80,48},{88,56},{96,... | collective-permute-start | bytes 442376 | tf_op jit(solution)/shard_map/ppermute | solution.py:20
  112.1 13.9 %collective-permute-start.14 = (bf16[128,576]{0,1:T(8,128)(2,1)S(1)}, bf16[128,576]{0,1:T(8,128)(2,1)S(1)}, u32[]{:S(2)}, u32[]{:S(2)}) collective-permute-start(bf16[128,576]{0,1:T(8,128)(2,1)S(1)} %get-tuple-element.20), channel_id=1, source_target_pairs={{24,0},{32,8},{40,16},{48,24},{56,32},{64,40},{72,48},{80,56},{88,... | collective-permute-start | bytes 442376 | tf_op jit(solution)/shard_map/ppermute | solution.py:20
  113.4 12.6 %collective-permute-start.13 = (bf16[128,576]{0,1:T(8,128)(2,1)S(1)}, bf16[128,576]{0,1:T(8,128)(2,1)S(1)}, u32[]{:S(2)}, u32[]{:S(2)}) collective-permute-start(bf16[128,576]{0,1:T(8,128)(2,1)S(1)} %get-tuple-element.21), channel_id=1, source_target_pairs={{16,0},{24,8},{32,16},{40,24},{48,32},{56,40},{64,48},{72,56},{80,... | collective-permute-start | bytes 442376 | tf_op jit(solution)/shard_map/ppermute | solution.py:20
  126.2 41.3 %copy-start.4 = (bf16[16,128,128]{2,1,0:T(8,128)(2,1)S(1)}, bf16[16,128,128]{2,1,0:T(8,128)(2,1)}, u32[]{:S(2)}) copy-start(bf16[16,128,128]{2,1,0:T(8,128)(2,1)} %get-tuple-element.27) | copy-start | bytes 1572868
  127.8 40.7 %all-to-all-start = ((f32[8,128,576]{1,2,0:T(8,128)}), f32[8,128,576]{1,2,0:T(8,128)S(1)}, u32[]{:S(2)}, u32[]{:S(2)}) async-start(f32[8,128,576]{1,2,0:T(8,128)} %broadcast_in_dim.16), calls=%async_computation | async-start | bytes 4718592 | tf_op jit(solution)/shard_map/all_to_all | solution.py:32
  138.6 50.5 %reduce-scatter.5.cloned.1.call-start = ((), (), s32[]{:S(2)}) async-start(), calls=%async_computation.4 | async-start | bytes 655360 | tf_op jit(solution)/shard_map/reduce_scatter | solution.py:26
  (6 other events, 14.5 us)
Sparse Core Ops, SparseCore 0:
  101.5 65.9 reduce-scatter.2
  170.0 19.0 reduce-scatter.4
where the time goes:
time: 199 us; the launch traced here: 198 us
  waiting for transfers between devices  61.1 us (31%)
  starting transfers between devices  60.9 us (31%)
  matrix products  33.7 us (17%)
  local copies, waits for them, and re-layouts  22 us (11%)
  between operations  14.4 us (7%)
  other arithmetic  5.43 us (3%)
    ppermute x16, starting transfers between devices, shifted(): return lax.ppermute(shard, axis, pairs)  50 us
    reduce_scatter x2, waiting for transfers between devices, summed_rows(): total = lax.psum_scatter(total, axis, scatter_dimension=0, tiled=True)  48.6 us
    unnamed x39, local copies, waits for them, and re-layouts  13 us
    ppermute x16, waiting for transfers between devices, shifted(): return lax.ppermute(shard, axis, pairs)  12.5 us
    all_to_all x1, starting transfers between devices, sent_to_all(): return lax.all_to_all(copies, axis, split_axis=0, concat_axis=0, tiled=True)  10.9 us
    dot_general x1, matrix products, per_device(): jnp.einsum('tl,tc->lc', stacked_main, key_grads, preferred_element_type=j...  8 us
    dot_general x1, matrix products, attend(): jnp.einsum('hpt,phd->thd', d_score, query_heads, preferred_element_type=j...  7.19 us
    dot_general x1, matrix products, per_device(): jnp.einsum('tc,lc->tl', key_grads, weight_both, preferred_element_type=jn...  6.42 us
  transfers between devices with their start and end apart: 19, of which 5 were waited for; matrix products, arithmetic and copies ran while one was open for 13% of the time, Pallas kernels for 0%

commit v1 on v0

v1 whole, which is shorter than its diff:
```python
import functools
import math

import jax
import jax.numpy as jnp
from jax import lax
from jax.experimental import pallas as pl
from jax.experimental.pallas import tpu as pltpu
from jax.sharding import Mesh
from jax.sharding import PartitionSpec as P

NOPE = 128
ROPE = 64
VDIM = 128
LATENT = 512
TOK = 128
ROWS = 4 * TOK
KEYS = 2 * ROWS
TILE = 256
SPAN = ROWS + TILE
PAY = 640
SCALE = 1.0 / math.sqrt(NOPE + ROPE)
LOG2E = math.log2(math.e)
HIDDEN = -1e30
GROUPS = 8
F32 = jnp.float32
BF16 = jnp.bfloat16


def nt(a, b):
    return lax.dot_general(a, b, (((1,), (1,)), ((), ())), preferred_element_type=F32)


def nn(a, b):
    return lax.dot_general(a, b, (((1,), (0,)), ((), ())), preferred_element_type=F32)


def tn(a, b):
    return lax.dot_general(a, b, (((0,), (0,)), ((), ())), preferred_element_type=F32)


def pair_kernel(first, where_ref, x_ref, l_ref, wk_ref, wv_ref, *refs):
    if first:
        out_ref, dw_ref, dl_ref, kcat, vals, bias, dk_acc, dv_acc, grads = refs
        before_ref = None
    else:
        before_ref, out_ref, dw_ref, dl_ref, kcat, vals, bias, dk_acc, dv_acc, grads = refs
    group = where_ref[0]
    lat = l_ref[:, :LATENT]
    tail = l_ref[:, LATENT:].astype(F32)
    lane = lax.broadcasted_iota(jnp.int32, (KEYS, 128), 1)
    low = lane < ROPE

    key_id = tail[:, ROPE : ROPE + 1]
    key_row = lax.broadcasted_iota(jnp.int32, (KEYS, 1), 0)
    key_id = jnp.where((key_row < ROWS) & (group == 0), -1.0, key_id)
    query_id = jnp.transpose(tail[ROWS:])[ROPE : ROPE + 1, :]
    for i in range(2):
        start = i * TILE
        at = lax.broadcasted_iota(jnp.int32, (SPAN, TILE), 0)
        by = lax.broadcasted_iota(jnp.int32, (SPAN, TILE), 1)
        seen = (key_id[start : start + SPAN] == query_id[:, start : start + TILE]) & (
            at <= by + ROWS
        )
        bias[i] = jnp.where(seen, 0.0, HIDDEN)

    keys_up = nn(lat, wk_ref[...])
    vals_up = nn(lat, wv_ref[...])
    vals[...] = vals_up.astype(BF16)
    rope_low = jnp.where(low, tail, 0.0)
    rope_high = pltpu.roll(rope_low, ROPE, 1)
    turned = pltpu.roll(keys_up[:, NOPE:], ROPE, 1)
    kcat[0, :, :NOPE] = keys_up[:, :NOPE].astype(BF16)
    kcat[0, :, NOPE:] = rope_low.astype(BF16)
    kcat[1, :, :NOPE] = jnp.where(low, 0.0, turned).astype(BF16)
    kcat[1, :, NOPE:] = jnp.where(low, turned, rope_high).astype(BF16)

    for h in range(2):
        v_turned = jnp.transpose(vals_up[:, h * VDIM : (h + 1) * VDIM]).astype(BF16)
        for i in range(2):
            start = i * TILE
            span = slice(start, start + SPAN)
            rows = slice(start, start + TILE)
            qc = x_ref[rows, h * NOPE : h * NOPE + 256]
            og = x_ref[rows, 384 + h * VDIM : 384 + (h + 1) * VDIM]
            s = nt(kcat[h, span, :], qc) * (SCALE * LOG2E) + bias[i]
            top = jnp.max(s, axis=0, keepdims=True)
            e = jnp.exp2(s - top)
            p = e * (1.0 / jnp.sum(e, axis=0, keepdims=True))
            pb = p.astype(BF16)
            out_t = nn(v_turned[:, span], pb).astype(BF16).astype(F32)
            out_ref[rows, h * VDIM : (h + 1) * VDIM] = jnp.transpose(out_t).astype(BF16)
            og_t = jnp.transpose(og.astype(F32))
            delta = jnp.sum(og_t * out_t, axis=0, keepdims=True)
            dp = nn(vals[span, h * VDIM : (h + 1) * VDIM], og_t.astype(BF16))
            ds = (p * (dp - delta) * SCALE).astype(BF16)
            dk = nn(ds, qc)
            dv = nn(pb, og)
            if i == 0:
                dk_acc[h, :SPAN, :] = dk
                dv_acc[:SPAN, :] = dv
            else:
                dk_acc[h, TILE:ROWS + TILE, :] += dk[:ROWS]
                dv_acc[TILE:ROWS + TILE, :] += dv[:ROWS]
                dk_acc[h, SPAN:, :] = dk[ROWS:]
                dv_acc[SPAN:, :] = dv[ROWS:]
        grads[:, 256 + h * VDIM : 256 + (h + 1) * VDIM] = dv_acc[...].astype(BF16)
    grads[:, :NOPE] = dk_acc[0, :, :NOPE].astype(BF16)
    mixed = jnp.where(low, dk_acc[1, :, NOPE:], dk_acc[1, :, :NOPE])
    grads[:, NOPE : 2 * NOPE] = pltpu.roll(mixed, ROPE, 1).astype(BF16)
    rope_grad = jnp.where(low, dk_acc[0, :, NOPE:], dk_acc[1, :, NOPE:])
    rope_grad = rope_grad + pltpu.roll(rope_grad, ROPE, 1)
    dl = nt(grads[:, :256], wk_ref[...]) + nt(grads[:, 256:], wv_ref[...])
    if not first:
        dl = dl + before_ref[:, :LATENT]
        rope_grad = rope_grad + before_ref[:, LATENT:]
    dl_ref[:, :LATENT] = dl.astype(dl_ref.dtype)
    dl_ref[:, LATENT:] = rope_grad.astype(dl_ref.dtype)
    dw_ref[...] = tn(lat, grads[...]).astype(BF16)


def pair_call(pair, place, x, lat, key_weight, value_weight, before):
    first = before is None

    def whole(*shape):
        return pl.BlockSpec(shape, lambda i, w: (0,) * len(shape))

    weight_spec = pl.BlockSpec((LATENT, 256), lambda i, w: (0, 2 * w[1] + pair))
    in_specs = [whole(ROWS, PAY), whole(KEYS, PAY), weight_spec, weight_spec]
    args = [x, lat, key_weight, value_weight]
    if not first:
        in_specs.append(whole(KEYS, PAY))
        args.append(before)
    return pl.pallas_call(
        functools.partial(pair_kernel, first),
        grid_spec=pltpu.PrefetchScalarGridSpec(
            num_scalar_prefetch=1,
            grid=(1,),
            in_specs=in_specs,
            out_specs=[whole(ROWS, 256), whole(LATENT, 512), whole(KEYS, PAY)],
            scratch_shapes=[
                pltpu.VMEM((2, KEYS, 256), BF16),
                pltpu.VMEM((KEYS, 256), BF16),
                pltpu.VMEM((2, SPAN, TILE), F32),
                pltpu.VMEM((2, KEYS, 256), F32),
                pltpu.VMEM((KEYS, VDIM), F32),
                pltpu.VMEM((KEYS, 512), BF16),
            ],
        ),
        out_shape=[
            jax.ShapeDtypeStruct((ROWS, 256), BF16),
            jax.ShapeDtypeStruct((LATENT, 512), BF16),
            jax.ShapeDtypeStruct((KEYS, PAY), F32 if first else BF16),
        ],
        compiler_params=pltpu.CompilerParams(vmem_limit_bytes=48 << 20),
        cost_estimate=pl.CostEstimate(
            flops=4_000_000_000, bytes_accessed=8_000_000, transcendentals=800_000
        ),
        name="pair",
    )(place, *args)


def exchanged(x, axes):
    return lax.all_to_all(x, axes, split_axis=0, concat_axis=0, tiled=True)


def sent_to_all(x, axes):
    copies = jnp.broadcast_to(x, (lax.axis_size(axes), *x.shape))
    return exchanged(copies, axes)


def per_device(queries, latents, doc_ids, key_weight, value_weight, out_grad):
    group = lax.axis_index("z")
    place = jnp.stack([group, lax.axis_index("y")]).astype(jnp.int32)
    pay = jnp.concatenate(
        [latents, doc_ids.astype(BF16)[:, None], jnp.zeros((TOK, PAY - 577), BF16)], axis=1
    )
    ahead = [(i, i + 1) for i in range(GROUPS - 1)]
    behind = [(i + 1, i) for i in range(GROUPS - 1)]
    q_parts = queries.reshape(TOK, 4, 2, 384)
    g_parts = out_grad.reshape(TOK, 4, 2, 256)
    earlier = lax.ppermute(pay, "z", ahead)
    xs = []
    for pair in range(2):
        x = jnp.concatenate([q_parts[:, :, pair], g_parts[:, :, pair]], axis=-1)
        xs.append(exchanged(jnp.transpose(x, (1, 0, 2)), "y").reshape(ROWS, PAY))
    lat = sent_to_all(jnp.stack([earlier, pay]), "y")
    lat = jnp.transpose(lat, (1, 0, 2, 3)).reshape(KEYS, PAY)

    out0, dw0, dl = pair_call(0, place, xs[0], lat, key_weight, value_weight, None)
    out0 = exchanged(out0.reshape(4, TOK, 256), "y")
    dw0 = exchanged(dw0.reshape(32, 16, 512), ("z", "y"))
    out1, dw1, dl = pair_call(1, place, xs[1], lat, key_weight, value_weight, dl)
    dl = dl.reshape(2, 4, 8, 16, PAY).transpose(1, 2, 0, 3, 4).reshape(32, 32, PAY)
    dl = exchanged(dl, ("y", "x", "core")).astype(F32).sum(axis=0)
    dw1 = exchanged(dw1.reshape(32, 16, 512), ("z", "y"))
    out1 = exchanged(out1.reshape(4, TOK, 256), "y")
    own = dl[16:] + lax.ppermute(dl[:16].astype(BF16), "z", behind).astype(F32)
    latent_grad = sent_to_all(own.astype(BF16), ("x", "core")).astype(F32)
    latent_grad = latent_grad.reshape(TOK, PAY)[:, : LATENT + ROPE]
    attended = jnp.stack([out0, out1], axis=1).transpose(2, 0, 1, 3).reshape(TOK, 2048)
    dw = jnp.stack([dw0, dw1], axis=1).reshape(GROUPS, 4, 2, 16, 512).astype(F32).sum(axis=0)
    dw = dw.transpose(2, 0, 1, 3)
    key_grad = dw[..., :256].reshape(16, 2048)
    value_grad = dw[..., 256:].reshape(16, 2048)
    return attended, latent_grad, key_grad, value_grad


def solution(mesh):
    split = Mesh(mesh.devices.reshape(GROUPS, 4, 4, 2), ("z", "y", "x", "core"))
    seq, head = ("z", "y"), ("x", "core")
    in_specs = (P(seq, head), P(seq, None), P(seq), P(None, head), P(None, head), P(seq, head))
    out_specs = (P(seq, head), P(seq, None), P(seq, head), P(seq, head))
    return jax.shard_map(
        per_device, mesh=split, in_specs=in_specs, out_specs=out_specs, check_vma=False
    )
```

time: 199 us -> 169 us (0.85)
  blocking collectives: 0 us -> 42.2 us
  matrix products: 33.7 us -> 0 us
  starting transfers between devices: 60.9 us -> 41.5 us
  Pallas kernels: 0 us -> 17.5 us
  waiting for transfers between devices: 61.1 us -> 44.9 us
  between operations: 14.4 us -> 0.89 us
  local copies, waits for them, and re-layouts: 22 us -> 17.5 us
    reduce_scatter x2 -> x0, waiting for transfers between devices: 48.6 us -> none  [summed_rows(): total = lax.psum_scatter(total, axis, scatter_dimension=0, tiled=True)]
    ppermute x16 -> x2, starting transfers between devices: 50 us -> 4.84 us  [the longest x1 3.55 us: per_device(): earlier = lax.ppermute(pay, 'z', ahead)]
    all_to_all x1 -> x7, waiting for transfers between devices: 0.01 us -> 42.4 us  [exchanged(): return lax.all_to_all(x, axes, split_axis=0, concat_axis=0, tiled=True)]
    all_to_all x0 -> x2, blocking collectives: none -> 42.2 us  [exchanged(): return lax.all_to_all(x, axes, split_axis=0, concat_axis=0, tiled=True)]
    dot_general x8 -> x0, matrix products: 33.7 us -> none  [the longest x1 8 us: per_device(): jnp.einsum('tl,tc->lc', stacked_main, key_grads, preferred_element_type=j...]
    all_to_all x1 -> x7, starting transfers between devices: 10.9 us -> 36.7 us  [exchanged(): return lax.all_to_all(x, axes, split_axis=0, concat_axis=0, tiled=True)]
    pallas_call x0 -> x2, Pallas kernels: none -> 17.5 us  [pair_call(): pl.pallas_call(functools.partial(pair_kernel, first), grid_spec=pltpu.Pre...]
    ppermute x16 -> x2, waiting for transfers between devices: 12.5 us -> 2.52 us  [the longest x1 2.52 us: per_device(): earlier = lax.ppermute(pay, 'z', ahead)]
  transfers between devices with their start and end apart: 19 -> 9, of which waited for: 5 -> 6; matrix products, arithmetic and copies ran while one was open for 13% -> 7% of each run, Pallas kernels for 0% -> 10%
where the time goes in v1:
time: 169 us; the launch traced here: 168 us
  waiting for transfers between devices  44.9 us (27%)
  blocking collectives  42.2 us (25%)
  starting transfers between devices  41.5 us (25%)
  local copies, waits for them, and re-layouts  17.5 us (10%)
  Pallas kernels  17.5 us (10%)
  other arithmetic  3.49 us (2%)
    all_to_all x7, waiting for transfers between devices, exchanged(): return lax.all_to_all(x, axes, split_axis=0, concat_axis=0, tiled=True)  42.4 us
    all_to_all x2, blocking collectives, exchanged(): return lax.all_to_all(x, axes, split_axis=0, concat_axis=0, tiled=True)  42.2 us
    all_to_all x7, starting transfers between devices, exchanged(): return lax.all_to_all(x, axes, split_axis=0, concat_axis=0, tiled=True)  36.7 us
    pallas_call x2, Pallas kernels, pair_call(): pl.pallas_call(functools.partial(pair_kernel, first), grid_spec=pltpu.Pre...  17.5 us
    ppermute x1, starting transfers between devices, per_device(): earlier = lax.ppermute(pay, 'z', ahead)  3.55 us
    unnamed x21, local copies, waits for them, and re-layouts  3.45 us
  transfers between devices with their start and end apart: 9, of which 6 were waited for; matrix products, arithmetic and copies ran while one was open for 7% of the time, Pallas kernels for 10%

profile of v1, /device:TPU:1, one launch (start us, length us, event | category | flops | bytes accessed | tf_op | source)
XLA Modules:
  0.0 168.0 jit_solution(7086356287274324219)
XLA Ops:
  0.6 1.4 reshape.60
  5.9 5.0 %all-to-all-start = ((bf16[4,128,640]{2,1,0:T(8,128)(2,1)}), bf16[4,128,640]{2,1,0:T(8,128)(2,1)S(1)}, u32[]{:S(2)}, u32[]{:S(2)}) async-start(bf16[4,128,640]{2,1,0:T(8,128)(2,1)} %maximum_bitcast_fusion), calls=%async_computation | async-start | bytes 1310720 | tf_op jit(solution)/shard_map/all_to_all | solution.py:164
  11.2 3.6 %collective-permute-start = (bf16[128,640]{0,1:T(8,128)(2,1)S(1)}, bf16[128,640]{0,1:T(8,128)(2,1)S(1)}, u32[]{:S(2)}, u32[]{:S(2)}) collective-permute-start(bf16[128,640]{0,1:T(8,128)(2,1)S(1)} %get-tuple-element.34), channel_id=1, source_target_pairs={{0,32},{32,64},{64,96},{96,128},{128,160},{160,192},{192,224},{1,3... | collective-permute-start | bytes 491528 | tf_op jit(solution)/shard_map/ppermute | solution.py:182
  14.7 2.5 %collective-permute-done = bf16[128,640]{0,1:T(8,128)(2,1)S(1)} collective-permute-done((bf16[128,640]{0,1:T(8,128)(2,1)S(1)}, bf16[128,640]{0,1:T(8,128)(2,1)S(1)}, u32[]{:S(2)}, u32[]{:S(2)}) %collective-permute-start) | collective-permute-done | bytes 163872 | tf_op jit(solution)/shard_map/ppermute | solution.py:182
  17.5 2.4 %all-to-all-done = bf16[4,128,640]{2,1,0:T(8,128)(2,1)S(1)} async-done(((bf16[4,128,640]{2,1,0:T(8,128)(2,1)}), bf16[4,128,640]{2,1,0:T(8,128)(2,1)S(1)}, u32[]{:S(2)}, u32[]{:S(2)}) %all-to-all-start) | async-done | bytes 655392 | tf_op jit(solution)/shard_map/all_to_all | solution.py:164
  21.0 3.5 %all-to-all-start.1 = ((bf16[4,2,128,640]{3,2,1,0:T(8,128)(2,1)}), bf16[4,2,128,640]{3,2,1,0:T(8,128)(2,1)S(1)}, u32[]{:S(2)}, u32[]{:S(2)}) async-start(bf16[4,2,128,640]{3,2,1,0:T(8,128)(2,1)} %broadcast_in_dim.14), calls=%async_computation.1 | async-start | bytes 2621440 | tf_op jit(solution)/shard_map/all_to_all | solution.py:164
  25.6 13.9 %all-to-all-done.1 = bf16[4,2,128,640]{3,2,1,0:T(8,128)(2,1)S(1)} async-done(((bf16[4,2,128,640]{3,2,1,0:T(8,128)(2,1)}), bf16[4,2,128,640]{3,2,1,0:T(8,128)(2,1)S(1)}, u32[]{:S(2)}, u32[]{:S(2)}) %all-to-all-start.1) | async-done | bytes 1310752 | tf_op jit(solution)/shard_map/all_to_all | solution.py:164
  39.6 3.5 %all-to-all-start.3 = ((bf16[4,128,640]{2,1,0:T(8,128)(2,1)}), bf16[4,128,640]{2,1,0:T(8,128)(2,1)S(1)}, u32[]{:S(2)}, u32[]{:S(2)}) async-start(bf16[4,128,640]{2,1,0:T(8,128)(2,1)} %maximum_bitcast_fusion.1), calls=%async_computation.3 | async-start | bytes 1310720 | tf_op jit(solution)/shard_map/all_to_all | solution.py:164
  43.1 1.6 copy.36
  45.1 8.5 %pair.2 = (bf16[512,256]{1,0:T(8,128)(2,1)}, bf16[512,512]{1,0:T(8,128)(2,1)S(1)}, f32[1024,640]{1,0:T(8,128)}) custom-call(s32[2]{0:T(128)S(1)} %pad_add_fusion.where_ref, bf16[512,640]{1,0:T(8,128)(2,1)S(1)} %bitcast.46, bf16[1024,640]{1,0:T(8,128)(2,1)S(1)} %bitcast.43, bf16[512,2048]{1,0:T(8,128)(2,1)S(1)} %copy-done.1, bf16[512,2048]{1,0:T(8,128)(2,1)} %wv_ref.3), custom_call_target="tpu_custom_call" | custom-call | flops 4000000000 | bytes 8000000 | tf_op jit(solution)/shard_map/pair/pallas_call | solution.py:134
  53.6 4.2 %all-to-all-start.2 = ((bf16[4,128,256]{2,1,0:T(8,128)(2,1)}), bf16[4,128,256]{2,1,0:T(8,128)(2,1)}, u32[]{:S(2)}, u32[]{:S(2)}) async-start(bf16[4,128,256]{2,1,0:T(8,128)(2,1)} %bitcast.11), calls=%async_computation.2 | async-start | bytes 524288 | tf_op jit(solution)/shard_map/all_to_all | solution.py:164
  57.9 1.6 copy-done.2
  59.5 9.0 %pair.3 = (bf16[512,256]{1,0:T(8,128)(2,1)S(1)}, bf16[512,512]{1,0:T(8,128)(2,1)}, bf16[1024,640]{1,0:T(8,128)(2,1)S(1)}) custom-call(s32[2]{0:T(128)S(1)} %pad_add_fusion.where_ref, bf16[512,640]{1,0:T(8,128)(2,1)S(1)} %bitcast.47, bf16[1024,640]{1,0:T(8,128)(2,1)S(1)} %bitcast.44, bf16[512,2048]{1,0:T(8,128)(2,1)S(1)} %copy-done.2, ...), custom_call_target="tpu_custom_call" | custom-call | flops 4000000000 | bytes 8000000 | tf_op jit(solution)/shard_map/pair/pallas_call | solution.py:134
  68.5 9.6 %all_to_all.45 = bf16[4,128,256]{2,1,0:T(8,128)(2,1)} all-to-all(bf16[4,128,256]{2,1,0:T(8,128)(2,1)S(1)} %bitcast.49), channel_id=1, replica_groups=mesh['z'=8,'y'=4,'x'=4,'core'=2] {'y'}, dimensions={0} | all-to-all | bytes 524288 | tf_op jit(solution)/shard_map/all_to_all | solution.py:164
  78.1 11.3 %all-to-all-start.7 = ((bf16[32,16,512]{2,1,0:T(8,128)(2,1)}), bf16[32,16,512]{2,1,0:T(8,128)(2,1)S(1)}, u32[]{:S(2)}, u32[]{:S(2)}) async-start(bf16[32,16,512]{2,1,0:T(8,128)(2,1)} %bitcast.48), calls=%async_computation.7 | async-start | bytes 1048576 | tf_op jit(solution)/shard_map/all_to_all | solution.py:164
  90.5 11.6 %all-to-all-done.7 = bf16[32,16,512]{2,1,0:T(8,128)(2,1)S(1)} async-done(((bf16[32,16,512]{2,1,0:T(8,128)(2,1)}), bf16[32,16,512]{2,1,0:T(8,128)(2,1)S(1)}, u32[]{:S(2)}, u32[]{:S(2)}) %all-to-all-start.7) | async-done | bytes 524320 | tf_op jit(solution)/shard_map/all_to_all | solution.py:164
  102.2 32.6 %all_to_all.46 = bf16[32,32,640]{2,1,0:T(8,128)(2,1)S(1)} all-to-all(bf16[32,32,640]{2,1,0:T(8,128)(2,1)} %bitcast.51), channel_id=1, replica_groups=mesh['z'=8,'y'=4,'x'=4,'core'=2] {'y','x','core'}, dimensions={0} | all-to-all | bytes 2621440 | tf_op jit(solution)/shard_map/all_to_all | solution.py:164
  134.8 3.9 %all-to-all-start.8 = ((bf16[32,16,512]{2,1,0:T(8,128)(2,1)}), bf16[32,16,512]{2,1,0:T(8,128)(2,1)S(1)}, u32[]{:S(2)}, u32[]{:S(2)}) async-start(bf16[32,16,512]{2,1,0:T(8,128)(2,1)} %bitcast.26), calls=%async_computation.8 | async-start | bytes 1048576 | tf_op jit(solution)/shard_map/all_to_all | solution.py:164
  139.7 1.3 copy.39
  141.1 2.2 %reshape.66 = bf16[128,2048]{1,0:T(8,128)(2,1)} reshape(bf16[128,4,2,256]{3,2,1,0:T(2,128)(2,1)} %copy.39) | data formatting | bytes 1048576 | tf_op jit(solution)/shard_map/reshape | solution.py:201
  143.5 1.3 collective-permute-start.1
  144.8 10.6 %all-to-all-done.8 = bf16[32,16,512]{2,1,0:T(8,128)(2,1)S(1)} async-done(((bf16[32,16,512]{2,1,0:T(8,128)(2,1)}), bf16[32,16,512]{2,1,0:T(8,128)(2,1)S(1)}, u32[]{:S(2)}, u32[]{:S(2)}) %all-to-all-start.8) | async-done | bytes 524320 | tf_op jit(solution)/shard_map/all_to_all | solution.py:164
  156.3 5.2 %all-to-all-start.6 = ((bf16[8,16,640]{2,1,0:T(8,128)(2,1)}), bf16[8,16,640]{2,1,0:T(8,128)(2,1)S(1)}, u32[]{:S(2)}, u32[]{:S(2)}) async-start(bf16[8,16,640]{2,1,0:T(8,128)(2,1)} %broadcast_in_dim.15), calls=%async_computation.6 | async-start | bytes 327680 | tf_op jit(solution)/shard_map/all_to_all | solution.py:164
  163.3 3.8 %all-to-all-done.6 = bf16[8,16,640]{2,1,0:T(8,128)(2,1)S(1)} async-done(((bf16[8,16,640]{2,1,0:T(8,128)(2,1)}), bf16[8,16,640]{2,1,0:T(8,128)(2,1)S(1)}, u32[]{:S(2)}, u32[]{:S(2)}) %all-to-all-start.6) | async-done | bytes 163872 | tf_op jit(solution)/shard_map/all_to_all | solution.py:164
  (49 shorter events, 12.9 us)
Async XLA Ops:
  2.1 1.1 copy-start.5
  4.9 6.0 %copy-start.7 = (s32[128]{0:T(128)S(1)}, s32[128]{0:T(128)}, u32[]{:S(2)}) copy-start(s32[128]{0:T(128)} %param.8) | copy-start | bytes 1540
  5.0 6.1 %copy-start.6 = (bf16[128,576]{0,1:T(8,128)(2,1)S(1)}, bf16[128,576]{0,1:T(8,128)(2,1)}, u32[]{:S(2)}) copy-start(bf16[128,576]{0,1:T(8,128)(2,1)} %param.7) | copy-start | bytes 442372
  5.9 13.9 %all-to-all-start = ((bf16[4,128,640]{2,1,0:T(8,128)(2,1)}), bf16[4,128,640]{2,1,0:T(8,128)(2,1)S(1)}, u32[]{:S(2)}, u32[]{:S(2)}) async-start(bf16[4,128,640]{2,1,0:T(8,128)(2,1)} %maximum_bitcast_fusion), calls=%async_computation | async-start | bytes 1310720 | tf_op jit(solution)/shard_map/all_to_all | solution.py:164
  11.2 6.1 %collective-permute-start = (bf16[128,640]{0,1:T(8,128)(2,1)S(1)}, bf16[128,640]{0,1:T(8,128)(2,1)S(1)}, u32[]{:S(2)}, u32[]{:S(2)}) collective-permute-start(bf16[128,640]{0,1:T(8,128)(2,1)S(1)} %get-tuple-element.34), channel_id=1, source_target_pairs={{0,32},{32,64},{64,96},{96,128},{128,160},{160,192},{192,224},{1,3... | collective-permute-start | bytes 491528 | tf_op jit(solution)/shard_map/ppermute | solution.py:182
  21.0 18.5 %all-to-all-start.1 = ((bf16[4,2,128,640]{3,2,1,0:T(8,128)(2,1)}), bf16[4,2,128,640]{3,2,1,0:T(8,128)(2,1)S(1)}, u32[]{:S(2)}, u32[]{:S(2)}) async-start(bf16[4,2,128,640]{3,2,1,0:T(8,128)(2,1)} %broadcast_in_dim.14), calls=%async_computation.1 | async-start | bytes 2621440 | tf_op jit(solution)/shard_map/all_to_all | solution.py:164
  39.6 3.6 %copy-start.3 = (bf16[4,2,128,640]{3,2,1,0:T(8,128)(2,1)}, bf16[4,2,128,640]{3,2,1,0:T(8,128)(2,1)S(1)}, u32[]{:S(2)}) copy-start(bf16[4,2,128,640]{3,2,1,0:T(8,128)(2,1)S(1)} %all-to-all-done.1) | copy-start | bytes 3932164
  39.6 14.0 %all-to-all-start.3 = ((bf16[4,128,640]{2,1,0:T(8,128)(2,1)}), bf16[4,128,640]{2,1,0:T(8,128)(2,1)S(1)}, u32[]{:S(2)}, u32[]{:S(2)}) async-start(bf16[4,128,640]{2,1,0:T(8,128)(2,1)} %maximum_bitcast_fusion.1), calls=%async_computation.3 | async-start | bytes 1310720 | tf_op jit(solution)/shard_map/all_to_all | solution.py:164
  43.1 2.0 %copy-start.1 = (bf16[512,2048]{1,0:T(8,128)(2,1)S(1)}, bf16[512,2048]{1,0:T(8,128)(2,1)}, u32[]{:S(2)}) copy-start(bf16[512,2048]{1,0:T(8,128)(2,1)} %wk_ref.3) | copy-start | bytes 6291460
  53.6 4.3 %copy-start = (bf16[512,512]{1,0:T(8,128)(2,1)}, bf16[512,512]{1,0:T(8,128)(2,1)S(1)}, u32[]{:S(2)}) copy-start(bf16[512,512]{1,0:T(8,128)(2,1)S(1)} %get-tuple-element.14) | copy-start | bytes 1572868
  53.6 14.9 %all-to-all-start.2 = ((bf16[4,128,256]{2,1,0:T(8,128)(2,1)}), bf16[4,128,256]{2,1,0:T(8,128)(2,1)}, u32[]{:S(2)}, u32[]{:S(2)}) async-start(bf16[4,128,256]{2,1,0:T(8,128)(2,1)} %bitcast.11), calls=%async_computation.2 | async-start | bytes 524288 | tf_op jit(solution)/shard_map/all_to_all | solution.py:164
  57.9 1.6 copy-start.2
  78.1 24.1 %all-to-all-start.7 = ((bf16[32,16,512]{2,1,0:T(8,128)(2,1)}), bf16[32,16,512]{2,1,0:T(8,128)(2,1)S(1)}, u32[]{:S(2)}, u32[]{:S(2)}) async-start(bf16[32,16,512]{2,1,0:T(8,128)(2,1)} %bitcast.48), calls=%async_computation.7 | async-start | bytes 1048576 | tf_op jit(solution)/shard_map/all_to_all | solution.py:164
  102.2 36.5 %copy-start.4 = (bf16[4,128,256]{2,1,0:T(8,128)(2,1)S(1)}, bf16[4,128,256]{2,1,0:T(8,128)(2,1)}, u32[]{:S(2)}) copy-start(bf16[4,128,256]{2,1,0:T(8,128)(2,1)} %all_to_all.45) | copy-start | bytes 786436
  134.8 20.6 %all-to-all-start.8 = ((bf16[32,16,512]{2,1,0:T(8,128)(2,1)}), bf16[32,16,512]{2,1,0:T(8,128)(2,1)S(1)}, u32[]{:S(2)}, u32[]{:S(2)}) async-start(bf16[32,16,512]{2,1,0:T(8,128)(2,1)} %bitcast.26), calls=%async_computation.8 | async-start | bytes 1048576 | tf_op jit(solution)/shard_map/all_to_all | solution.py:164
  143.5 12.1 %collective-permute-start.1 = (bf16[16,640]{1,0:T(8,128)(2,1)S(1)}, bf16[16,640]{1,0:T(8,128)(2,1)S(1)}, u32[]{:S(2)}, u32[]{:S(2)}) collective-permute-start(bf16[16,640]{1,0:T(8,128)(2,1)S(1)} %slice.56), channel_id=1, source_target_pairs={{32,0},{64,32},{96,64},{128,96},{160,128},{192,160},{224,192},{33,... | collective-permute-start | bytes 61448 | tf_op jit(solution)/shard_map/ppermute | solution.py:198
  156.3 10.8 %all-to-all-start.6 = ((bf16[8,16,640]{2,1,0:T(8,128)(2,1)}), bf16[8,16,640]{2,1,0:T(8,128)(2,1)S(1)}, u32[]{:S(2)}, u32[]{:S(2)}) async-start(bf16[8,16,640]{2,1,0:T(8,128)(2,1)} %broadcast_in_dim.15), calls=%async_computation.6 | async-start | bytes 327680 | tf_op jit(solution)/shard_map/all_to_all | solution.py:164

commit v2 on v1

v2 whole, which is shorter than its diff:
```python
import functools
import math

import jax
import jax.numpy as jnp
from jax import lax
from jax.experimental import pallas as pl
from jax.experimental.pallas import tpu as pltpu
from jax.sharding import Mesh
from jax.sharding import PartitionSpec as P

NOPE = 128
ROPE = 64
VDIM = 128
LATENT = 512
TOK = 128
ROWS = 4 * TOK
KEYS = 2 * ROWS
TILE = 256
SPAN = ROWS + TILE
PAY = 640
SCALE = 1.0 / math.sqrt(NOPE + ROPE)
LOG2E = math.log2(math.e)
HIDDEN = -1e30
GROUPS = 8
F32 = jnp.float32
BF16 = jnp.bfloat16


def nt(a, b):
    return lax.dot_general(a, b, (((1,), (1,)), ((), ())), preferred_element_type=F32)


def nn(a, b):
    return lax.dot_general(a, b, (((1,), (0,)), ((), ())), preferred_element_type=F32)


def tn(a, b):
    return lax.dot_general(a, b, (((0,), (0,)), ((), ())), preferred_element_type=F32)


def pack_kernel(where_ref, q_ref, g_ref, *piece_refs):
    y = where_ref[1]
    for k in range(4):
        to = (y + k) & 3
        for pair in range(2):
            piece = piece_refs[4 * pair + k]
            piece[:, :384] = q_ref[:, pl.ds(pl.multiple_of(to * 768 + pair * 384, 128), 384)]
            piece[:, 384:] = g_ref[:, pl.ds(pl.multiple_of(to * 512 + pair * 256, 128), 256)]


def pack_call(place, queries, out_grad):
    vmem = pl.BlockSpec(memory_space=pltpu.VMEM)
    return pl.pallas_call(
        pack_kernel,
        in_specs=[pl.BlockSpec(memory_space=pltpu.SMEM), vmem, vmem],
        out_specs=[vmem] * 8,
        out_shape=[jax.ShapeDtypeStruct((TOK, PAY), BF16)] * 8,
        cost_estimate=pl.CostEstimate(flops=0, bytes_accessed=2_600_000, transcendentals=0),
        name="pack",
    )(place, queries, out_grad)


def pair_kernel(first, where_ref, *refs):
    pieces, refs = refs[:4], refs[4:]
    mine_ref, other_ref, wk_ref, wv_ref, refs = *refs[:4], refs[4:]
    if first:
        before_ref, refs = None, refs
        (dl_ref,), outs = refs[:1], refs[1:]
    else:
        before_ref, refs = refs[0], refs[1:]
        keep_ref, send_ref, outs = refs[0], refs[1], refs[2:]
    out_refs, dw_ref = outs[:4], outs[4]
    x_ref, l_ref, kcat, vals, bias, dk_acc, dv_acc, grads, attended, dl_acc = outs[5:]
    group, y, core = where_ref[0], where_ref[1], where_ref[2]
    half = TOK // 2
    for k in range(4):
        block = (y - k) & 3
        x_ref[pl.ds(pl.multiple_of(block * TOK, TOK), TOK), :] = pieces[k][...]
        for back in range(2):
            row = (1 - back) * ROWS + block * TOK
            own = pl.multiple_of(row + core * half, half)
            l_ref[pl.ds(own, half), :] = mine_ref[4 * back + k]
            swapped = pl.multiple_of(row + (1 - core) * half, half)
            l_ref[pl.ds(swapped, half), :] = other_ref[4 * back + k]
    lat = l_ref[:, :LATENT]
    tail = l_ref[:, LATENT:].astype(F32)
    lane = lax.broadcasted_iota(jnp.int32, (KEYS, 128), 1)
    low = lane < ROPE

    key_id = tail[:, ROPE : ROPE + 1]
    key_row = lax.broadcasted_iota(jnp.int32, (KEYS, 1), 0)
    key_id = jnp.where((key_row < ROWS) & (group == 0), -1.0, key_id)
    query_id = jnp.transpose(tail[ROWS:])[ROPE : ROPE + 1, :]
    for i in range(2):
        start = i * TILE
        at = lax.broadcasted_iota(jnp.int32, (SPAN, TILE), 0)
        by = lax.broadcasted_iota(jnp.int32, (SPAN, TILE), 1)
        seen = (key_id[start : start + SPAN] == query_id[:, start : start + TILE]) & (
            at <= by + ROWS
        )
        bias[i] = jnp.where(seen, 0.0, HIDDEN)

    keys_up = nn(lat, wk_ref[...])
    vals_up = nn(lat, wv_ref[...])
    vals[...] = vals_up.astype(BF16)
    rope_low = jnp.where(low, tail, 0.0)
    rope_high = pltpu.roll(rope_low, ROPE, 1)
    turned = pltpu.roll(keys_up[:, NOPE:], ROPE, 1)
    kcat[0, :, :NOPE] = keys_up[:, :NOPE].astype(BF16)
    kcat[0, :, NOPE:] = rope_low.astype(BF16)
    kcat[1, :, :NOPE] = jnp.where(low, 0.0, turned).astype(BF16)
    kcat[1, :, NOPE:] = jnp.where(low, turned, rope_high).astype(BF16)

    for h in range(2):
        v_turned = jnp.transpose(vals_up[:, h * VDIM : (h + 1) * VDIM]).astype(BF16)
        for i in range(2):
            start = i * TILE
            span = slice(start, start + SPAN)
            rows = slice(start, start + TILE)
            qc = x_ref[rows, h * NOPE : h * NOPE + 256]
            og = x_ref[rows, 384 + h * VDIM : 384 + (h + 1) * VDIM]
            s = nt(kcat[h, span, :], qc) * (SCALE * LOG2E) + bias[i]
            top = jnp.max(s, axis=0, keepdims=True)
            e = jnp.exp2(s - top)
            p = e * (1.0 / jnp.sum(e, axis=0, keepdims=True))
            pb = p.astype(BF16)
            out_t = nn(v_turned[:, span], pb).astype(BF16).astype(F32)
            attended[rows, h * VDIM : (h + 1) * VDIM] = jnp.transpose(out_t).astype(BF16)
            og_t = jnp.transpose(og.astype(F32))
            delta = jnp.sum(og_t * out_t, axis=0, keepdims=True)
            dp = nn(vals[span, h * VDIM : (h + 1) * VDIM], og_t.astype(BF16))
            ds = (p * (dp - delta) * SCALE).astype(BF16)
            dk = nn(ds, qc)
            dv = nn(pb, og)
            if i == 0:
                dk_acc[h, :SPAN, :] = dk
                dv_acc[:SPAN, :] = dv
            else:
                dk_acc[h, TILE : ROWS + TILE, :] += dk[:ROWS]
                dv_acc[TILE : ROWS + TILE, :] += dv[:ROWS]
                dk_acc[h, SPAN:, :] = dk[ROWS:]
                dv_acc[SPAN:, :] = dv[ROWS:]
        grads[:, 256 + h * VDIM : 256 + (h + 1) * VDIM] = dv_acc[...].astype(BF16)
    for k in range(4):
        to = pl.multiple_of(((y + k) & 3) * TOK, TOK)
        out_refs[k][...] = attended[pl.ds(to, TOK), :]
    grads[:, :NOPE] = dk_acc[0, :, :NOPE].astype(BF16)
    mixed = jnp.where(low, dk_acc[1, :, NOPE:], dk_acc[1, :, :NOPE])
    grads[:, NOPE : 2 * NOPE] = pltpu.roll(mixed, ROPE, 1).astype(BF16)
    rope_grad = jnp.where(low, dk_acc[0, :, NOPE:], dk_acc[1, :, NOPE:])
    rope_grad = rope_grad + pltpu.roll(rope_grad, ROPE, 1)
    dl = nt(grads[:, :256], wk_ref[...]) + nt(grads[:, 256:], wv_ref[...])
    if first:
        dl_ref[:, :LATENT] = dl
        dl_ref[:, LATENT:] = rope_grad
    else:
        dl_acc[:, :LATENT] = (dl + before_ref[:, :LATENT]).astype(BF16)
        dl_acc[:, LATENT:] = (rope_grad + before_ref[:, LATENT:]).astype(BF16)
        for k in range(4):
            for back in range(2):
                row = (1 - back) * ROWS + ((y + k) & 3) * TOK
                own = pl.multiple_of(row + core * half, half)
                keep_ref[k, back * half : (back + 1) * half, :] = dl_acc[pl.ds(own, half), :]
                swapped = pl.multiple_of(row + (1 - core) * half, half)
                send_ref[k, back * half : (back + 1) * half, :] = dl_acc[pl.ds(swapped, half), :]
    dw_ref[...] = tn(lat, grads[...]).astype(BF16)


def pair_call(pair, place, pieces, mine, other, key_weight, value_weight, before):
    first = before is None

    def whole(*shape):
        return pl.BlockSpec(shape, lambda i, w: (0,) * len(shape))

    weight_spec = pl.BlockSpec((LATENT, 256), lambda i, w: (0, 2 * w[1] + pair))
    in_specs = [whole(TOK, PAY)] * 4 + [whole(8, TOK // 2, PAY)] * 2 + [weight_spec] * 2
    args = [*pieces, mine, other, key_weight, value_weight]
    if first:
        dl_shapes = [jax.ShapeDtypeStruct((KEYS, PAY), F32)]
    else:
        in_specs.append(whole(KEYS, PAY))
        args.append(before)
        dl_shapes = [jax.ShapeDtypeStruct((4, TOK, PAY), BF16)] * 2
    out_shape = dl_shapes + [jax.ShapeDtypeStruct((TOK, 256), BF16)] * 4
    out_shape.append(jax.ShapeDtypeStruct((LATENT, 512), BF16))
    return pl.pallas_call(
        functools.partial(pair_kernel, first),
        grid_spec=pltpu.PrefetchScalarGridSpec(
            num_scalar_prefetch=1,
            grid=(1,),
            in_specs=in_specs,
            out_specs=[whole(*leaf.shape) for leaf in out_shape],
            scratch_shapes=[
                pltpu.VMEM((ROWS, PAY), BF16),
                pltpu.VMEM((KEYS, PAY), BF16),
                pltpu.VMEM((2, KEYS, 256), BF16),
                pltpu.VMEM((KEYS, 256), BF16),
                pltpu.VMEM((2, SPAN, TILE), F32),
                pltpu.VMEM((2, KEYS, 256), F32),
                pltpu.VMEM((KEYS, VDIM), F32),
                pltpu.VMEM((KEYS, 512), BF16),
                pltpu.VMEM((ROWS, 256), BF16),
                pltpu.VMEM((KEYS, PAY), BF16),
            ],
        ),
        out_shape=out_shape,
        compiler_params=pltpu.CompilerParams(vmem_limit_bytes=48 << 20),
        cost_estimate=pl.CostEstimate(
            flops=4_000_000_000, bytes_accessed=8_000_000, transcendentals=800_000
        ),
        name="pair",
    )(place, *args)


def latent_kernel(where_ref, *refs):
    terms, out_ref, held = refs[:8], refs[8], refs[9]
    x = where_ref[3]
    for k in range(4):
        held[(x - k) & 3] = terms[k][...].astype(F32)
        held[4 + ((x - k) & 3)] = terms[4 + k][...].astype(F32)
    total = held[0]
    for k in range(1, 8):
        total = total + held[k]
    out_ref[...] = total


def latent_call(place, terms):
    vmem = pl.BlockSpec(memory_space=pltpu.VMEM)
    return pl.pallas_call(
        latent_kernel,
        in_specs=[pl.BlockSpec(memory_space=pltpu.SMEM)] + [vmem] * 8,
        out_specs=vmem,
        out_shape=jax.ShapeDtypeStruct((TOK // 2, PAY), F32),
        scratch_shapes=[pltpu.VMEM((8, TOK // 2, PAY), F32)],
        name="latent",
    )(place, *terms)


def attended_kernel(where_ref, *refs):
    pieces, out_ref = refs[:8], refs[8]
    y = where_ref[1]
    for pair in range(2):
        for k in range(4):
            column = pl.multiple_of(((y - k) & 3) * 512 + pair * 256, 128)
            out_ref[:, pl.ds(column, 256)] = pieces[4 * pair + k][...]


def attended_call(place, pieces):
    vmem = pl.BlockSpec(memory_space=pltpu.VMEM)
    return pl.pallas_call(
        attended_kernel,
        in_specs=[pl.BlockSpec(memory_space=pltpu.SMEM)] + [vmem] * 8,
        out_specs=vmem,
        out_shape=jax.ShapeDtypeStruct((TOK, 2048), BF16),
        name="attended",
    )(place, *pieces)


def weight_kernel(first_ref, second_ref, key_ref, value_ref):
    for pair, ref in enumerate((first_ref, second_ref)):
        for y in range(4):
            total = ref[y].astype(F32)
            for z in range(1, GROUPS):
                total = total + ref[4 * z + y].astype(F32)
            column = y * 512 + pair * 256
            key_ref[:, column : column + 256] = total[:, :256]
            value_ref[:, column : column + 256] = total[:, 256:]


def weight_call(first, second):
    vmem = pl.BlockSpec(memory_space=pltpu.VMEM)
    return pl.pallas_call(
        weight_kernel,
        in_specs=[vmem] * 2,
        out_specs=[vmem] * 2,
        out_shape=[jax.ShapeDtypeStruct((16, 2048), F32)] * 2,
        name="weight",
    )(first, second)


def exchanged(x, axes):
    return lax.all_to_all(x, axes, split_axis=0, concat_axis=0, tiled=True)


def moved(value, ahead, along, size, step):
    if not ahead:
        return lax.ppermute(value, along, [(i, (i + step) % size) for i in range(size)])
    pairs = []
    for group in range(GROUPS):
        if 0 <= group + ahead < GROUPS:
            for i in range(size):
                pairs.append((group * size + i, (group + ahead) * size + (i + step) % size))
    return lax.ppermute(value, ("z", along), pairs)


def swapped(value):
    return lax.ppermute(value, "core", [(0, 1), (1, 0)])


def per_device(queries, latents, doc_ids, key_weight, value_weight, out_grad):
    core = lax.axis_index("core")
    place = [lax.axis_index("z"), lax.axis_index("y"), core, lax.axis_index("x")]
    place = jnp.stack(place).astype(jnp.int32)
    half = TOK // 2
    rows = lax.dynamic_slice_in_dim(latents, core * half, half)
    ids = lax.dynamic_slice_in_dim(doc_ids, core * half, half)
    pay = jnp.concatenate(
        [rows, ids.astype(BF16)[:, None], jnp.zeros((half, PAY - 577), BF16)], axis=1
    )
    mine = [pay] + [moved(pay, 0, "y", 4, k) for k in range(1, 4)]
    mine = jnp.stack(mine + [moved(pay, 1, "y", 4, k) for k in range(4)])
    other = swapped(mine)
    pieces = pack_call(place, queries, out_grad)
    pieces = [p if i % 4 == 0 else moved(p, 0, "y", 4, i % 4) for i, p in enumerate(pieces)]

    dl, *outs, dw0 = pair_call(
        0, place, pieces[:4], mine, other, key_weight, value_weight, None
    )
    dw0 = exchanged(dw0.reshape(32, 16, 512), ("z", "y"))
    keep, send, *outs1, dw1 = pair_call(
        1, place, pieces[4:], mine, other, key_weight, value_weight, dl
    )
    dw1 = exchanged(dw1.reshape(32, 16, 512), ("z", "y"))
    outs = [p if i % 4 == 0 else moved(p, 0, "y", 4, i % 4) for i, p in enumerate(outs + outs1)]
    attended = attended_call(place, outs)

    came = swapped(send)
    both = [(keep[k].astype(F32) + came[k].astype(F32)) for k in range(4)]
    total = both[0]
    for k in range(1, 4):
        total = total + moved(both[k].astype(BF16), 0, "y", 4, k).astype(F32)
    total = total.astype(BF16)
    own, later = total[:half], total[half:]
    terms = [own] + [moved(own, 0, "x", 4, k) for k in range(1, 4)]
    terms += [moved(later, -1, "x", 4, k) for k in range(4)]
    part = latent_call(place, terms)
    part_other = swapped(part)
    ordered = jnp.where(core == 0, jnp.stack([part, part_other]), jnp.stack([part_other, part]))
    latent_grad = ordered.reshape(TOK, PAY)[:, : LATENT + ROPE]
    key_grad, value_grad = weight_call(dw0, dw1)
    return attended, latent_grad, key_grad, value_grad


def solution(mesh):
    split = Mesh(mesh.devices.reshape(GROUPS, 4, 4, 2), ("z", "y", "x", "core"))
    seq, head = ("z", "y"), ("x", "core")
    in_specs = (P(seq, head), P(seq, None), P(seq), P(None, head), P(None, head), P(seq, head))
    out_specs = (P(seq, head), P(seq, None), P(seq, head), P(seq, head))
    return jax.shard_map(
        per_device, mesh=split, in_specs=in_specs, out_specs=out_specs, check_vma=False
    )
```

time: 169 us -> 159 us (0.941)
  the two profiles are of different devices: /device:TPU:1 before, /device:TPU:224 now
where the time goes in v2:
time: 159 us; the launch traced here: 158 us
  starting transfers between devices  74.1 us (47%)
  waiting for transfers between devices  42.1 us (26%)
  Pallas kernels  26.6 us (17%)
  local copies, waits for them, and re-layouts  12.7 us (8%)
  other arithmetic  1.78 us (1%)
    ppermute x21, waiting for transfers between devices, moved(): lax.ppermute(value, along, [(i, (i + step) % size) for i in range(size)])  34.4 us
    ppermute x21, starting transfers between devices, moved(): lax.ppermute(value, along, [(i, (i + step) % size) for i in range(size)])  28 us
    all_to_all x2, starting transfers between devices, exchanged(): return lax.all_to_all(x, axes, split_axis=0, concat_axis=0, tiled=True)  25 us
    ppermute x8, starting transfers between devices, moved(): return lax.ppermute(value, ('z', along), pairs)  21 us
    pallas_call x2, Pallas kernels, pair_call(): pl.pallas_call(functools.partial(pair_kernel, first), grid_spec=pltpu.Pre...  18.2 us
    unnamed x78, local copies, waits for them, and re-layouts  12.4 us
    ppermute x8, waiting for transfers between devices, moved(): return lax.ppermute(value, ('z', along), pairs)  7.69 us
  transfers between devices with their start and end apart: 34, of which 12 were waited for; matrix products, arithmetic and copies ran while one was open for 1% of the time, Pallas kernels for 17%

profile of v2, /device:TPU:224, one launch (start us, length us, event | category | flops | bytes accessed | tf_op | source)
XLA Modules:
  0.0 158.4 jit_solution(1999465008298117432)
XLA Ops:
  9.3 2.0 %collective-permute-start.4 = (bf16[64,640]{1,0:T(8,128)(2,1)S(1)}, bf16[64,640]{1,0:T(8,128)(2,1)S(1)}, u32[]{:S(2)}, u32[]{:S(2)}) collective-permute-start(bf16[64,640]{1,0:T(8,128)(2,1)S(1)} %get-tuple-element.51), channel_id=1, source_target_pairs={{0,16},{8,24},{16,0},{24,8},{1,17},{9,25},{17,1},{25,9},{2,18},{10... | collective-permute-start | bytes 245768 | tf_op jit(solution)/shard_map/ppermute | solution.py:288
  11.2 5.2 %collective-permute-done.4 = bf16[64,640]{1,0:T(8,128)(2,1)S(1)} collective-permute-done((bf16[64,640]{1,0:T(8,128)(2,1)S(1)}, bf16[64,640]{1,0:T(8,128)(2,1)S(1)}, u32[]{:S(2)}, u32[]{:S(2)}) %collective-permute-start.4) | collective-permute-done | bytes 81952 | tf_op jit(solution)/shard_map/ppermute | solution.py:288
  17.9 7.7 %collective-permute-done.9 = bf16[64,640]{1,0:T(8,128)(2,1)S(1)} collective-permute-done((bf16[64,640]{1,0:T(8,128)(2,1)S(1)}, bf16[64,640]{1,0:T(8,128)(2,1)S(1)}, u32[]{:S(2)}, u32[]{:S(2)}) %collective-permute-start.9) | collective-permute-done | bytes 81952 | tf_op jit(solution)/shard_map/ppermute | solution.py:294
  26.3 2.5 %pack.1 = (bf16[128,640]{1,0:T(8,128)(2,1)}, bf16[128,640]{1,0:T(8,128)(2,1)}, bf16[128,640]{1,0:T(8,128)(2,1)}, bf16[128,640]{1,0:T(8,128)(2,1)}, bf16[128,640]...) custom-call(s32[4]{0:T(128)} %pad_add_fusion.where_ref, ...), custom_call_target="tpu_custom_call" | custom-call | bytes 2600000 | tf_op jit(solution)/shard_map/pack/pallas_call | solution.py:54
  28.8 4.0 %collective-permute-start.1 = (bf16[128,640]{1,0:T(8,128)(2,1)}, bf16[128,640]{1,0:T(8,128)(2,1)S(1)}, u32[]{:S(2)}, u32[]{:S(2)}) collective-permute-start(bf16[128,640]{1,0:T(8,128)(2,1)} %get-tuple-element.29), channel_id=1, source_target_pairs={{0,16},{8,24},{16,0},{24,8},{1,17},{9,25},{17,1},{25,9},{2,18},{10... | collective-permute-start | bytes 491528 | tf_op jit(solution)/shard_map/ppermute | solution.py:288
  37.7 3.9 %collective-permute-done.1.refs_2_ = bf16[128,640]{1,0:T(8,128)(2,1)S(1)} collective-permute-done((bf16[128,640]{1,0:T(8,128)(2,1)}, bf16[128,640]{1,0:T(8,128)(2,1)S(1)}, u32[]{:S(2)}, u32[]{:S(2)}) %collective-permute-start.1) | collective-permute-done | bytes 163872 | tf_op jit(solution)/shard_map/ppermute | solution.py:288
  44.9 8.8 %pair.2 = (f32[1024,640]{1,0:T(8,128)}, bf16[128,256]{1,0:T(8,128)(2,1)S(1)}, bf16[128,256]{1,0:T(8,128)(2,1)S(1)}, bf16[128,256]{1,0:T(8,128)(2,1)S(1)}, bf16[1...) custom-call(s32[4]{0:T(128)S(1)} %copy-done.3, bf16[128,640]{1,0:T(8,128)(2,1)S(1)} %copy-done.8, ...), custom_call_target="tpu_custom_call" | custom-call | flops 4000000000 | bytes 8000000 | tf_op jit(solution)/shard_map/pair/pallas_call | solution.py:187
  55.5 15.1 %all-to-all-start = ((bf16[32,16,512]{2,1,0:T(8,128)(2,1)}), bf16[32,16,512]{2,1,0:T(8,128)(2,1)}, u32[]{:S(2)}, u32[]{:S(2)}) async-start(bf16[32,16,512]{2,1,0:T(8,128)(2,1)} %bitcast.20), calls=%async_computation | async-start | bytes 1048576 | tf_op jit(solution)/shard_map/all_to_all | solution.py:283
  72.3 9.4 %pair.3 = (bf16[4,128,640]{2,1,0:T(8,128)(2,1)S(1)}, bf16[4,128,640]{2,1,0:T(8,128)(2,1)S(1)}, bf16[128,256]{1,0:T(8,128)(2,1)S(1)}, bf16[128,256]{1,0:T(8,128)(...) custom-call(s32[4]{0:T(128)S(1)} %copy-done.4, ...), custom_call_target="tpu_custom_call" | custom-call | flops 4000000000 | bytes 8000000 | tf_op jit(solution)/shard_map/pair/pallas_call | solution.py:187
  84.2 9.9 %all-to-all-start.1 = ((bf16[32,16,512]{2,1,0:T(8,128)(2,1)}), bf16[32,16,512]{2,1,0:T(8,128)(2,1)S(1)}, u32[]{:S(2)}, u32[]{:S(2)}) async-start(bf16[32,16,512]{2,1,0:T(8,128)(2,1)} %bitcast.21), calls=%async_computation.1 | async-start | bytes 1048576 | tf_op jit(solution)/shard_map/all_to_all | solution.py:283
  99.3 6.9 %collective-permute-done.21 = bf16[128,640]{1,0:T(8,128)(2,1)S(1)} collective-permute-done((bf16[128,640]{1,0:T(8,128)(2,1)S(1)}, bf16[128,640]{1,0:T(8,128)(2,1)S(1)}, u32[]{:S(2)}, u32[]{:S(2)}) %collective-permute-start.21) | collective-permute-done | bytes 163872 | tf_op jit(solution)/shard_map/ppermute | solution.py:288
  106.2 4.6 %collective-permute-done.22 = bf16[128,640]{1,0:T(8,128)(2,1)S(1)} collective-permute-done((bf16[128,640]{1,0:T(8,128)(2,1)S(1)}, bf16[128,640]{1,0:T(8,128)(2,1)S(1)}, u32[]{:S(2)}, u32[]{:S(2)}) %collective-permute-start.22) | collective-permute-done | bytes 163872 | tf_op jit(solution)/shard_map/ppermute | solution.py:288
  110.9 5.6 %collective-permute-start.30 = (bf16[64,640]{1,0:T(8,128)(2,1)S(1)}, bf16[64,640]{1,0:T(8,128)(2,1)S(1)}, u32[]{:S(2)}, u32[]{:S(2)}) collective-permute-start(bf16[64,640]{1,0:T(8,128)(2,1)S(1)} %get-tuple-element.55), channel_id=1, source_target_pairs={{32,6},{34,0},{36,2},{38,4},{64,38},{66,32},{68,34},{70,36},{96,70... | collective-permute-start | bytes 245768 | tf_op jit(solution)/shard_map/ppermute | solution.py:294
  116.5 3.8 %collective-permute-start.29 = (bf16[64,640]{1,0:T(8,128)(2,1)S(1)}, bf16[64,640]{1,0:T(8,128)(2,1)S(1)}, u32[]{:S(2)}, u32[]{:S(2)}) collective-permute-start(bf16[64,640]{1,0:T(8,128)(2,1)S(1)} %get-tuple-element.55), channel_id=1, source_target_pairs={{32,4},{34,6},{36,0},{38,2},{64,36},{66,38},{68,32},{70,34},{96,68... | collective-permute-start | bytes 245768 | tf_op jit(solution)/shard_map/ppermute | solution.py:294
  120.3 3.2 %collective-permute-start.28 = (bf16[64,640]{1,0:T(8,128)(2,1)S(1)}, bf16[64,640]{1,0:T(8,128)(2,1)S(1)}, u32[]{:S(2)}, u32[]{:S(2)}) collective-permute-start(bf16[64,640]{1,0:T(8,128)(2,1)S(1)} %get-tuple-element.55), channel_id=1, source_target_pairs={{32,2},{34,4},{36,6},{38,0},{64,34},{66,36},{68,38},{70,32},{96,66... | collective-permute-start | bytes 245768 | tf_op jit(solution)/shard_map/ppermute | solution.py:294
  123.6 3.2 %collective-permute-start.27 = (bf16[64,640]{1,0:T(8,128)(2,1)S(1)}, bf16[64,640]{1,0:T(8,128)(2,1)S(1)}, u32[]{:S(2)}, u32[]{:S(2)}) collective-permute-start(bf16[64,640]{1,0:T(8,128)(2,1)S(1)} %get-tuple-element.55), channel_id=1, source_target_pairs={{32,0},{34,2},{36,4},{38,6},{64,32},{66,34},{68,36},{70,38},{96,64... | collective-permute-start | bytes 245768 | tf_op jit(solution)/shard_map/ppermute | solution.py:294
  126.8 2.4 %collective-permute-start.26 = (bf16[64,640]{1,0:T(8,128)(2,1)S(1)}, bf16[64,640]{1,0:T(8,128)(2,1)S(1)}, u32[]{:S(2)}, u32[]{:S(2)}) collective-permute-start(bf16[64,640]{1,0:T(8,128)(2,1)S(1)} %get-tuple-element.56.refs_0_), channel_id=1, source_target_pairs={{0,6},{2,0},{4,2},{6,4},{1,7},{3,1},{5,3},{7,5},{8,14},{10,8},{12,... | collective-permute-start | bytes 245768 | tf_op jit(solution)/shard_map/ppermute | solution.py:288
  132.1 3.1 %collective-permute-done.25.refs_2_ = bf16[64,640]{1,0:T(8,128)(2,1)S(1)} collective-permute-done((bf16[64,640]{1,0:T(8,128)(2,1)S(1)}, bf16[64,640]{1,0:T(8,128)(2,1)S(1)}, u32[]{:S(2)}, u32[]{:S(2)}) %collective-permute-start.25) | collective-permute-done | bytes 81952 | tf_op jit(solution)/shard_map/ppermute | solution.py:288
  137.1 2.0 %latent.1 = f32[64,640]{1,0:T(8,128)} custom-call(s32[4]{0:T(128)} %pad_add_fusion.where_ref, bf16[64,640]{1,0:T(8,128)(2,1)} %copy-done.21, bf16[64,640]{1,0:T(8,128)(2,1)} %copy-done.28, bf16[64,640]{1,0:T(8,128)(2,1)} %copy-done.27, bf16[64,640]{1,0:T(8,128)(2,1)} %copy-done.26, bf16[64,640]{1,0:T(8,128)(2,1)} %copy-done.25, bf16[64,640]{1,0:T(8,128)(2,1)} %copy-done.24, ...), custom_call_target="tpu_custom_call" | custom-call | tf_op jit(solution)/shard_map/latent/pallas_call | solution.py:230
  139.4 2.0 %collective-permute-start.12 = (bf16[128,256]{1,0:T(8,128)(2,1)S(1)}, bf16[128,256]{1,0:T(8,128)(2,1)S(1)}, u32[]{:S(2)}, u32[]{:S(2)}) collective-permute-start(bf16[128,256]{1,0:T(8,128)(2,1)S(1)} %copy-done.10), channel_id=1, source_target_pairs={{0,16},{8,24},{16,0},{24,8},{1,17},{9,25},{17,1},{25,9},{2,18},{10... | collective-permute-start | bytes 196616 | tf_op jit(solution)/shard_map/ppermute | solution.py:288
  143.4 2.9 %collective-permute-done.11.refs_1_ = bf16[128,256]{1,0:T(8,128)(2,1)S(1)} collective-permute-done((bf16[128,256]{1,0:T(8,128)(2,1)S(1)}, bf16[128,256]{1,0:T(8,128)(2,1)S(1)}, u32[]{:S(2)}, u32[]{:S(2)}) %collective-permute-start.11) | collective-permute-done | bytes 65568 | tf_op jit(solution)/shard_map/ppermute | solution.py:288
  146.3 2.5 %collective-permute-start.19 = (bf16[128,256]{1,0:T(8,128)(2,1)S(1)}, bf16[128,256]{1,0:T(8,128)(2,1)S(1)}, u32[]{:S(2)}, u32[]{:S(2)}) collective-permute-start(bf16[128,256]{1,0:T(8,128)(2,1)S(1)} %copy-done.14), channel_id=1, source_target_pairs={{0,24},{8,0},{16,8},{24,16},{1,25},{9,1},{17,9},{25,17},{2,26},{10... | collective-permute-start | bytes 196616 | tf_op jit(solution)/shard_map/ppermute | solution.py:288
  148.8 3.2 %collective-permute-done.18.refs_6_ = bf16[128,256]{1,0:T(8,128)(2,1)S(1)} collective-permute-done((bf16[128,256]{1,0:T(8,128)(2,1)S(1)}, bf16[128,256]{1,0:T(8,128)(2,1)S(1)}, u32[]{:S(2)}, u32[]{:S(2)}) %collective-permute-start.18) | collective-permute-done | bytes 65568 | tf_op jit(solution)/shard_map/ppermute | solution.py:288
  155.5 2.0 %weight.1 = (f32[16,2048]{1,0:T(8,128)}, f32[16,2048]{1,0:T(8,128)}) custom-call(bf16[32,16,512]{2,1,0:T(8,128)(2,1)} %all-to-all-done.first_ref, bf16[32,16,512]{2,1,0:T(8,128)(2,1)} %copy-done.19), custom_call_target="tpu_custom_call" | custom-call | tf_op jit(solution)/shard_map/weight/pallas_call | solution.py:273
  (140 shorter events, 41.5 us)
Async XLA Ops:
  2.0 7.3 %collective-permute-start.3 = (bf16[64,640]{1,0:T(8,128)(2,1)S(1)}, bf16[64,640]{1,0:T(8,128)(2,1)S(1)}, u32[]{:S(2)}, u32[]{:S(2)}) collective-permute-start(bf16[64,640]{1,0:T(8,128)(2,1)S(1)} %get-tuple-element.51), channel_id=1, source_target_pairs={{0,8},{8,16},{16,24},{24,0},{1,9},{9,17},{17,25},{25,1},{2,10},{10... | collective-permute-start | bytes 245768 | tf_op jit(solution)/shard_map/ppermute | solution.py:288
  3.6 14.2 %collective-permute-start.8 = (bf16[64,640]{1,0:T(8,128)(2,1)S(1)}, bf16[64,640]{1,0:T(8,128)(2,1)S(1)}, u32[]{:S(2)}, u32[]{:S(2)}) collective-permute-start(bf16[64,640]{1,0:T(8,128)(2,1)S(1)} %get-tuple-element.51), channel_id=1, source_target_pairs={{0,48},{8,56},{16,32},{24,40},{32,80},{40,88},{48,64},{56,72},{64,... | collective-permute-start | bytes 245768 | tf_op jit(solution)/shard_map/ppermute | solution.py:294
  4.9 12.9 %collective-permute-start.7 = (bf16[64,640]{1,0:T(8,128)(2,1)S(1)}, bf16[64,640]{1,0:T(8,128)(2,1)S(1)}, u32[]{:S(2)}, u32[]{:S(2)}) collective-permute-start(bf16[64,640]{1,0:T(8,128)(2,1)S(1)} %get-tuple-element.51), channel_id=1, source_target_pairs={{0,40},{8,48},{16,56},{24,32},{32,72},{40,80},{48,88},{56,64},{64,... | collective-permute-start | bytes 245768 | tf_op jit(solution)/shard_map/ppermute | solution.py:294
  6.2 11.6 %collective-permute-start.6 = (bf16[64,640]{1,0:T(8,128)(2,1)S(1)}, bf16[64,640]{1,0:T(8,128)(2,1)S(1)}, u32[]{:S(2)}, u32[]{:S(2)}) collective-permute-start(bf16[64,640]{1,0:T(8,128)(2,1)S(1)} %get-tuple-element.51), channel_id=1, source_target_pairs={{0,32},{8,40},{16,48},{24,56},{32,64},{40,72},{48,80},{56,88},{64,... | collective-permute-start | bytes 245768 | tf_op jit(solution)/shard_map/ppermute | solution.py:294
  7.5 10.2 %collective-permute-start.5 = (bf16[64,640]{1,0:T(8,128)(2,1)S(1)}, bf16[64,640]{1,0:T(8,128)(2,1)S(1)}, u32[]{:S(2)}, u32[]{:S(2)}) collective-permute-start(bf16[64,640]{1,0:T(8,128)(2,1)S(1)} %get-tuple-element.51), channel_id=1, source_target_pairs={{0,24},{8,0},{16,8},{24,16},{1,25},{9,1},{17,9},{25,17},{2,26},{10... | collective-permute-start | bytes 245768 | tf_op jit(solution)/shard_map/ppermute | solution.py:288
  16.4 9.1 %collective-permute-start.9 = (bf16[64,640]{1,0:T(8,128)(2,1)S(1)}, bf16[64,640]{1,0:T(8,128)(2,1)S(1)}, u32[]{:S(2)}, u32[]{:S(2)}) collective-permute-start(bf16[64,640]{1,0:T(8,128)(2,1)S(1)} %get-tuple-element.51), channel_id=1, source_target_pairs={{0,56},{8,32},{16,40},{24,48},{32,88},{40,64},{48,72},{56,80},{64,... | collective-permute-start | bytes 245768 | tf_op jit(solution)/shard_map/ppermute | solution.py:294
  25.6 16.1 %collective-permute-start.10 = (bf16[8,64,640]{2,1,0:T(8,128)(2,1)S(1)}, bf16[8,64,640]{2,1,0:T(8,128)(2,1)S(1)}, u32[]{:S(2)}, u32[]{:S(2)}) collective-permute-start(bf16[8,64,640]{2,1,0:T(8,128)(2,1)S(1)} %bitcast_dynamic-update-slice_fusion.refs_4_), channel_id=1, source_target_pairs={{0,1},{1,0},{2,3},{3,2},{4,5},{5,4},{6,7},{7,6},{8,9},{9,8},{10,11... | collective-permute-start | bytes 1966088 | tf_op jit(solution)/shard_map/ppermute | solution.py:298
  28.8 8.0 %collective-permute-start = (bf16[128,640]{1,0:T(8,128)(2,1)}, bf16[128,640]{1,0:T(8,128)(2,1)S(1)}, u32[]{:S(2)}, u32[]{:S(2)}) collective-permute-start(bf16[128,640]{1,0:T(8,128)(2,1)} %get-tuple-element.28), channel_id=1, source_target_pairs={{0,8},{8,16},{16,24},{24,0},{1,9},{9,17},{17,25},{25,1},{2,10},{10... | collective-permute-start | bytes 491528 | tf_op jit(solution)/shard_map/ppermute | solution.py:288
  28.8 12.8 %collective-permute-start.1 = (bf16[128,640]{1,0:T(8,128)(2,1)}, bf16[128,640]{1,0:T(8,128)(2,1)S(1)}, u32[]{:S(2)}, u32[]{:S(2)}) collective-permute-start(bf16[128,640]{1,0:T(8,128)(2,1)} %get-tuple-element.29), channel_id=1, source_target_pairs={{0,16},{8,24},{16,0},{24,8},{1,17},{9,25},{17,1},{25,9},{2,18},{10... | collective-permute-start | bytes 491528 | tf_op jit(solution)/shard_map/ppermute | solution.py:288
  32.8 8.8 %collective-permute-start.2 = (bf16[128,640]{1,0:T(8,128)(2,1)}, bf16[128,640]{1,0:T(8,128)(2,1)S(1)}, u32[]{:S(2)}, u32[]{:S(2)}) collective-permute-start(bf16[128,640]{1,0:T(8,128)(2,1)} %get-tuple-element.30), channel_id=1, source_target_pairs={{0,24},{8,0},{16,8},{24,16},{1,25},{9,1},{17,9},{25,17},{2,26},{10... | collective-permute-start | bytes 491528 | tf_op jit(solution)/shard_map/ppermute | solution.py:288
  33.0 37.6 %collective-permute-start.14 = (bf16[128,640]{1,0:T(8,128)(2,1)}, bf16[128,640]{1,0:T(8,128)(2,1)S(1)}, u32[]{:S(2)}, u32[]{:S(2)}) collective-permute-start(bf16[128,640]{1,0:T(8,128)(2,1)} %get-tuple-element.36), channel_id=1, source_target_pairs={{0,8},{8,16},{16,24},{24,0},{1,9},{9,17},{17,25},{25,1},{2,10},{10... | collective-permute-start | bytes 491528 | tf_op jit(solution)/shard_map/ppermute | solution.py:288
  36.8 33.8 %collective-permute-start.15 = (bf16[128,640]{1,0:T(8,128)(2,1)}, bf16[128,640]{1,0:T(8,128)(2,1)S(1)}, u32[]{:S(2)}, u32[]{:S(2)}) collective-permute-start(bf16[128,640]{1,0:T(8,128)(2,1)} %get-tuple-element.37), channel_id=1, source_target_pairs={{0,16},{8,24},{16,0},{24,8},{1,17},{9,25},{17,1},{25,9},{2,18},{10... | collective-permute-start | bytes 491528 | tf_op jit(solution)/shard_map/ppermute | solution.py:288
  41.6 29.1 %collective-permute-start.16 = (bf16[128,640]{1,0:T(8,128)(2,1)}, bf16[128,640]{1,0:T(8,128)(2,1)S(1)}, u32[]{:S(2)}, u32[]{:S(2)}) collective-permute-start(bf16[128,640]{1,0:T(8,128)(2,1)} %get-tuple-element.38), channel_id=1, source_target_pairs={{0,24},{8,0},{16,8},{24,16},{1,25},{9,1},{17,9},{25,17},{2,26},{10... | collective-permute-start | bytes 491528 | tf_op jit(solution)/shard_map/ppermute | solution.py:288
  55.5 28.6 %all-to-all-start = ((bf16[32,16,512]{2,1,0:T(8,128)(2,1)}), bf16[32,16,512]{2,1,0:T(8,128)(2,1)}, u32[]{:S(2)}, u32[]{:S(2)}) async-start(bf16[32,16,512]{2,1,0:T(8,128)(2,1)} %bitcast.20), calls=%async_computation | async-start | bytes 1048576 | tf_op jit(solution)/shard_map/all_to_all | solution.py:283
  84.1 10.0 %collective-permute-start.20 = (bf16[4,128,640]{2,1,0:T(8,128)(2,1)S(1)}, bf16[4,128,640]{2,1,0:T(8,128)(2,1)S(1)}, u32[]{:S(2)}, u32[]{:S(2)}) collective-permute-start(bf16[4,128,640]{2,1,0:T(8,128)(2,1)S(1)} %get-tuple-element.45), channel_id=1, source_target_pairs={{0,1},{1,0},{2,3},{3,2},{4,5},{5,4},{6,7},{7,6},{8,9},{9,8},{10,11... | collective-permute-start | bytes 1966088 | tf_op jit(solution)/shard_map/ppermute | solution.py:298
  84.2 70.5 %all-to-all-start.1 = ((bf16[32,16,512]{2,1,0:T(8,128)(2,1)}), bf16[32,16,512]{2,1,0:T(8,128)(2,1)S(1)}, u32[]{:S(2)}, u32[]{:S(2)}) async-start(bf16[32,16,512]{2,1,0:T(8,128)(2,1)} %bitcast.21), calls=%async_computation.1 | async-start | bytes 1048576 | tf_op jit(solution)/shard_map/all_to_all | solution.py:283
  94.2 12.0 %collective-permute-start.21 = (bf16[128,640]{1,0:T(8,128)(2,1)S(1)}, bf16[128,640]{1,0:T(8,128)(2,1)S(1)}, u32[]{:S(2)}, u32[]{:S(2)}) collective-permute-start(bf16[128,640]{1,0:T(8,128)(2,1)S(1)} %get-tuple-element.52), channel_id=1, source_target_pairs={{0,8},{8,16},{16,24},{24,0},{1,9},{9,17},{17,25},{25,1},{2,10},{10... | collective-permute-start | bytes 491528 | tf_op jit(solution)/shard_map/ppermute | solution.py:288
  95.8 10.4 %collective-permute-start.23 = (bf16[128,640]{1,0:T(8,128)(2,1)S(1)}, bf16[128,640]{1,0:T(8,128)(2,1)S(1)}, u32[]{:S(2)}, u32[]{:S(2)}) collective-permute-start(bf16[128,640]{1,0:T(8,128)(2,1)S(1)} %get-tuple-element.53), channel_id=1, source_target_pairs={{0,24},{8,0},{16,8},{24,16},{1,25},{9,1},{17,9},{25,17},{2,26},{10... | collective-permute-start | bytes 491528 | tf_op jit(solution)/shard_map/ppermute | solution.py:288
  97.6 13.2 %collective-permute-start.22 = (bf16[128,640]{1,0:T(8,128)(2,1)S(1)}, bf16[128,640]{1,0:T(8,128)(2,1)S(1)}, u32[]{:S(2)}, u32[]{:S(2)}) collective-permute-start(bf16[128,640]{1,0:T(8,128)(2,1)S(1)} %get-tuple-element.54), channel_id=1, source_target_pairs={{0,16},{8,24},{16,0},{24,8},{1,17},{9,25},{17,1},{25,9},{2,18},{10... | collective-permute-start | bytes 491528 | tf_op jit(solution)/shard_map/ppermute | solution.py:288
  110.9 18.3 %collective-permute-start.30 = (bf16[64,640]{1,0:T(8,128)(2,1)S(1)}, bf16[64,640]{1,0:T(8,128)(2,1)S(1)}, u32[]{:S(2)}, u32[]{:S(2)}) collective-permute-start(bf16[64,640]{1,0:T(8,128)(2,1)S(1)} %get-tuple-element.55), channel_id=1, source_target_pairs={{32,6},{34,0},{36,2},{38,4},{64,38},{66,32},{68,34},{70,36},{96,70... | collective-permute-start | bytes 245768 | tf_op jit(solution)/shard_map/ppermute | solution.py:294
  116.5 14.2 %collective-permute-start.29 = (bf16[64,640]{1,0:T(8,128)(2,1)S(1)}, bf16[64,640]{1,0:T(8,128)(2,1)S(1)}, u32[]{:S(2)}, u32[]{:S(2)}) collective-permute-start(bf16[64,640]{1,0:T(8,128)(2,1)S(1)} %get-tuple-element.55), channel_id=1, source_target_pairs={{32,4},{34,6},{36,0},{38,2},{64,36},{66,38},{68,32},{70,34},{96,68... | collective-permute-start | bytes 245768 | tf_op jit(solution)/shard_map/ppermute | solution.py:294
  120.3 10.4 %collective-permute-start.28 = (bf16[64,640]{1,0:T(8,128)(2,1)S(1)}, bf16[64,640]{1,0:T(8,128)(2,1)S(1)}, u32[]{:S(2)}, u32[]{:S(2)}) collective-permute-start(bf16[64,640]{1,0:T(8,128)(2,1)S(1)} %get-tuple-element.55), channel_id=1, source_target_pairs={{32,2},{34,4},{36,6},{38,0},{64,34},{66,36},{68,38},{70,32},{96,66... | collective-permute-start | bytes 245768 | tf_op jit(solution)/shard_map/ppermute | solution.py:294
  139.1 18.4 %collective-permute-start.31 = (f32[64,640]{1,0:T(8,128)}, f32[64,640]{1,0:T(8,128)S(1)}, u32[]{:S(2)}, u32[]{:S(2)}) collective-permute-start(f32[64,640]{1,0:T(8,128)} %latent.1), channel_id=1, source_target_pairs={{0,1},{1,0},{2,3},{3,2},{4,5},{5,4},{6,7},{7,6},{8,9},{9,8},{10,11... | collective-permute-start | bytes 491528 | tf_op jit(solution)/shard_map/ppermute | solution.py:298
  141.4 7.4 %collective-permute-start.13 = (bf16[128,256]{1,0:T(8,128)(2,1)S(1)}, bf16[128,256]{1,0:T(8,128)(2,1)S(1)}, u32[]{:S(2)}, u32[]{:S(2)}) collective-permute-start(bf16[128,256]{1,0:T(8,128)(2,1)S(1)} %get-tuple-element.34), channel_id=1, source_target_pairs={{0,24},{8,0},{16,8},{24,16},{1,25},{9,1},{17,9},{25,17},{2,26},{10... | collective-permute-start | bytes 196616 | tf_op jit(solution)/shard_map/ppermute | solution.py:288
  (45 other events, 512.2 us)

commit v3 on v2

--- a/solution.py
+++ b/solution.py
@@ -25,6 +25,7 @@
 GROUPS = 8
 F32 = jnp.float32
 BF16 = jnp.bfloat16
+SMALL = pltpu.CompilerParams(vmem_limit_bytes=12 << 20)
 
 
 def nt(a, b):
@@ -57,13 +58,15 @@
         out_specs=[vmem] * 8,
         out_shape=[jax.ShapeDtypeStruct((TOK, PAY), BF16)] * 8,
         cost_estimate=pl.CostEstimate(flops=0, bytes_accessed=2_600_000, transcendentals=0),
+        compiler_params=SMALL,
         name="pack",
     )(place, queries, out_grad)
 
 
 def pair_kernel(first, where_ref, *refs):
     pieces, refs = refs[:4], refs[4:]
-    mine_ref, other_ref, wk_ref, wv_ref, refs = *refs[:4], refs[4:]
+    mine_refs, other_refs, refs = refs[:4], refs[4:8], refs[8:]
+    wk_ref, wv_ref, refs = refs[0], refs[1], refs[2:]
     if first:
         before_ref, refs = None, refs
         (dl_ref,), outs = refs[:1], refs[1:]
@@ -80,9 +83,9 @@
         for back in range(2):
             row = (1 - back) * ROWS + block * TOK
             own = pl.multiple_of(row + core * half, half)
-            l_ref[pl.ds(own, half), :] = mine_ref[4 * back + k]
+            l_ref[pl.ds(own, half), :] = mine_refs[k][(1 - back) * half : (2 - back) * half]
             swapped = pl.multiple_of(row + (1 - core) * half, half)
-            l_ref[pl.ds(swapped, half), :] = other_ref[4 * back + k]
+            l_ref[pl.ds(swapped, half), :] = other_refs[k][(1 - back) * half : (2 - back) * half]
     lat = l_ref[:, :LATENT]
     tail = l_ref[:, LATENT:].astype(F32)
     lane = lax.broadcasted_iota(jnp.int32, (KEYS, 128), 1)
@@ -152,11 +155,11 @@
     rope_grad = rope_grad + pltpu.roll(rope_grad, ROPE, 1)
     dl = nt(grads[:, :256], wk_ref[...]) + nt(grads[:, 256:], wv_ref[...])
     if first:
-        dl_ref[:, :LATENT] = dl
-        dl_ref[:, LATENT:] = rope_grad
+        dl_ref[:, :LATENT] = dl.astype(BF16)
+        dl_ref[:, LATENT:] = rope_grad.astype(BF16)
     else:
-        dl_acc[:, :LATENT] = (dl + before_ref[:, :LATENT]).astype(BF16)
-        dl_acc[:, LATENT:] = (rope_grad + before_ref[:, LATENT:]).astype(BF16)
+        dl_acc[:, :LATENT] = (dl + before_ref[:, :LATENT].astype(F32)).astype(BF16)
+        dl_acc[:, LATENT:] = (rope_grad + before_ref[:, LATENT:].astype(F32)).astype(BF16)
         for k in range(4):
             for back in range(2):
                 row = (1 - back) * ROWS + ((y + k) & 3) * TOK
@@ -167,6 +170,10 @@
     dw_ref[...] = tn(lat, grads[...]).astype(BF16)
 
 
+def in_hbm(x):
+    return pltpu.with_memory_space_constraint(x, pltpu.HBM)
+
+
 def pair_call(pair, place, pieces, mine, other, key_weight, value_weight, before):
     first = before is None
 
@@ -174,16 +181,16 @@
         return pl.BlockSpec(shape, lambda i, w: (0,) * len(shape))
 
     weight_spec = pl.BlockSpec((LATENT, 256), lambda i, w: (0, 2 * w[1] + pair))
-    in_specs = [whole(TOK, PAY)] * 4 + [whole(8, TOK // 2, PAY)] * 2 + [weight_spec] * 2
-    args = [*pieces, mine, other, key_weight, value_weight]
+    in_specs = [whole(TOK, PAY)] * 12 + [weight_spec] * 2
+    args = [in_hbm(x) for x in (*pieces, *mine, *other, key_weight, value_weight)]
     if first:
-        dl_shapes = [jax.ShapeDtypeStruct((KEYS, PAY), F32)]
+        dl_shapes = [pltpu.HBM((KEYS, PAY), BF16)]
     else:
         in_specs.append(whole(KEYS, PAY))
         args.append(before)
         dl_shapes = [jax.ShapeDtypeStruct((4, TOK, PAY), BF16)] * 2
-    out_shape = dl_shapes + [jax.ShapeDtypeStruct((TOK, 256), BF16)] * 4
-    out_shape.append(jax.ShapeDtypeStruct((LATENT, 512), BF16))
+    out_shape = dl_shapes + [pltpu.HBM((TOK, 256), BF16)] * 4
+    out_shape.append(pltpu.HBM((LATENT, 512), BF16))
     return pl.pallas_call(
         functools.partial(pair_kernel, first),
         grid_spec=pltpu.PrefetchScalarGridSpec(
@@ -205,7 +212,7 @@
             ],
         ),
         out_shape=out_shape,
-        compiler_params=pltpu.CompilerParams(vmem_limit_bytes=48 << 20),
+        compiler_params=pltpu.CompilerParams(vmem_limit_bytes=40 << 20),
         cost_estimate=pl.CostEstimate(
             flops=4_000_000_000, bytes_accessed=8_000_000, transcendentals=800_000
         ),
@@ -214,27 +221,45 @@
 
 
 def latent_kernel(where_ref, *refs):
-    terms, out_ref, held = refs[:8], refs[8], refs[9]
+    terms, out_ref, held = refs[:4], refs[4], refs[5]
     x = where_ref[3]
     for k in range(4):
         held[(x - k) & 3] = terms[k][...].astype(F32)
-        held[4 + ((x - k) & 3)] = terms[4 + k][...].astype(F32)
-    total = held[0]
-    for k in range(1, 8):
-        total = total + held[k]
-    out_ref[...] = total
+    out_ref[...] = (held[0] + held[1]) + (held[2] + held[3])
 
 
 def latent_call(place, terms):
     vmem = pl.BlockSpec(memory_space=pltpu.VMEM)
     return pl.pallas_call(
         latent_kernel,
-        in_specs=[pl.BlockSpec(memory_space=pltpu.SMEM)] + [vmem] * 8,
+        in_specs=[pl.BlockSpec(memory_space=pltpu.SMEM)] + [vmem] * 4,
         out_specs=vmem,
         out_shape=jax.ShapeDtypeStruct((TOK // 2, PAY), F32),
-        scratch_shapes=[pltpu.VMEM((8, TOK // 2, PAY), F32)],
+        scratch_shapes=[pltpu.VMEM((4, TOK // 2, PAY), F32)],
+        compiler_params=SMALL,
         name="latent",
     )(place, *terms)
+
+
+def join_kernel(where_ref, mine_ref, other_ref, out_ref):
+    first = where_ref[2] == 0
+    mine, other = mine_ref[...], other_ref[...]
+    rows = jnp.concatenate(
+        [jnp.where(first, mine, other), jnp.where(first, other, mine)], axis=0
+    )
+    out_ref[...] = jnp.transpose(rows)[: LATENT + ROPE]
+
+
+def join_call(place, mine, other):
+    vmem = pl.BlockSpec(memory_space=pltpu.VMEM)
+    return pl.pallas_call(
+        join_kernel,
+        in_specs=[pl.BlockSpec(memory_space=pltpu.SMEM), vmem, vmem],
+        out_specs=vmem,
+        out_shape=jax.ShapeDtypeStruct((LATENT + ROPE, TOK), F32),
+        compiler_params=SMALL,
+        name="join",
+    )(place, mine, other)
 
 
 def attended_kernel(where_ref, *refs):
@@ -253,45 +278,72 @@
         in_specs=[pl.BlockSpec(memory_space=pltpu.SMEM)] + [vmem] * 8,
         out_specs=vmem,
         out_shape=jax.ShapeDtypeStruct((TOK, 2048), BF16),
+        compiler_params=SMALL,
         name="attended",
     )(place, *pieces)
 
 
-def weight_kernel(first_ref, second_ref, key_ref, value_ref):
-    for pair, ref in enumerate((first_ref, second_ref)):
-        for y in range(4):
-            total = ref[y].astype(F32)
-            for z in range(1, GROUPS):
-                total = total + ref[4 * z + y].astype(F32)
-            column = y * 512 + pair * 256
-            key_ref[:, column : column + 256] = total[:, :256]
-            value_ref[:, column : column + 256] = total[:, 256:]
-
-
-def weight_call(first, second):
+def half_kernel(where_ref, sent_ref, *piece_refs):
+    y = where_ref[1]
+    for k in range(4):
+        row = pl.ds(pl.multiple_of(((y + k) & 3) * 16, 16), 16)
+        total = sent_ref[0, row, :].astype(F32)
+        for z in range(1, GROUPS):
+            total = total + sent_ref[z, row, :].astype(F32)
+        piece_refs[k][...] = total.astype(BF16)
+
+
+def half_call(place, sent):
+    vmem = pl.BlockSpec(memory_space=pltpu.VMEM)
+    return pl.pallas_call(
+        half_kernel,
+        in_specs=[pl.BlockSpec(memory_space=pltpu.SMEM), vmem],
+        out_specs=[vmem] * 4,
+        out_shape=[jax.ShapeDtypeStruct((16, 512), BF16)] * 4,
+        compiler_params=SMALL,
+        name="half",
+    )(place, sent)
+
+
+def weight_kernel(where_ref, *refs):
+    pieces, second_ref, key_ref, value_ref = refs[:4], refs[4], refs[5], refs[6]
+    here = where_ref[1]
+    for k in range(4):
+        column = pl.multiple_of(((here - k) & 3) * 512, 512)
+        total = pieces[k][...].astype(F32)
+        key_ref[:, pl.ds(column, 256)] = total[:, :256]
+        value_ref[:, pl.ds(column, 256)] = total[:, 256:]
+    for y in range(4):
+        total = second_ref[y].astype(F32)
+        for z in range(1, GROUPS):
+            total = total + second_ref[4 * z + y].astype(F32)
+        column = y * 512 + 256
+        key_ref[:, column : column + 256] = total[:, :256]
+        value_ref[:, column : column + 256] = total[:, 256:]
+
+
+def weight_call(place, pieces, second):
     vmem = pl.BlockSpec(memory_space=pltpu.VMEM)
     return pl.pallas_call(
         weight_kernel,
-        in_specs=[vmem] * 2,
+        in_specs=[pl.BlockSpec(memory_space=pltpu.SMEM)] + [vmem] * 5,
         out_specs=[vmem] * 2,
         out_shape=[jax.ShapeDtypeStruct((16, 2048), F32)] * 2,
+        compiler_params=SMALL,
         name="weight",
-    )(first, second)
+    )(place, *pieces, second)
 
 
 def exchanged(x, axes):
     return lax.all_to_all(x, axes, split_axis=0, concat_axis=0, tiled=True)
 
 
-def moved(value, ahead, along, size, step):
-    if not ahead:
-        return lax.ppermute(value, along, [(i, (i + step) % size) for i in range(size)])
-    pairs = []
-    for group in range(GROUPS):
-        if 0 <= group + ahead < GROUPS:
-            for i in range(size):
-                pairs.append((group * size + i, (group + ahead) * size + (i + step) % size))
-    return lax.ppermute(value, ("z", along), pairs)
+def moved(value, along, size, step):
+    return lax.ppermute(value, along, [(i, (i + step) % size) for i in range(size)])
+
+
+def fanned(pieces, along):
+    return [p if k == 0 else moved(p, along, 4, k) for k, p in enumerate(pieces)]
 
 
 def swapped(value):
@@ -308,37 +360,35 @@
     pay = jnp.concatenate(
         [rows, ids.astype(BF16)[:, None], jnp.zeros((half, PAY - 577), BF16)], axis=1
     )
-    mine = [pay] + [moved(pay, 0, "y", 4, k) for k in range(1, 4)]
-    mine = jnp.stack(mine + [moved(pay, 1, "y", 4, k) for k in range(4)])
-    other = swapped(mine)
+    ahead = [(i, i + 1) for i in range(GROUPS - 1)]
+    behind = [(i + 1, i) for i in range(GROUPS - 1)]
+    earlier = lax.ppermute(pay, "z", ahead)
     pieces = pack_call(place, queries, out_grad)
-    pieces = [p if i % 4 == 0 else moved(p, 0, "y", 4, i % 4) for i, p in enumerate(pieces)]
-
-    dl, *outs, dw0 = pair_call(
-        0, place, pieces[:4], mine, other, key_weight, value_weight, None
-    )
-    dw0 = exchanged(dw0.reshape(32, 16, 512), ("z", "y"))
+    both = jnp.concatenate([earlier, pay], axis=0)
+    mine = fanned([both] * 4, "y")
+    other = [swapped(piece) for piece in mine]
+    x0, x1 = fanned(pieces[:4], "y"), fanned(pieces[4:], "y")
+
+    dl, *outs0, dw0 = pair_call(0, place, x0, mine, other, key_weight, value_weight, None)
+    dw0 = half_call(place, exchanged(dw0.reshape(8, 64, 512), "z"))
     keep, send, *outs1, dw1 = pair_call(
-        1, place, pieces[4:], mine, other, key_weight, value_weight, dl
+        1, place, x1, mine, other, key_weight, value_weight, dl
     )
     dw1 = exchanged(dw1.reshape(32, 16, 512), ("z", "y"))
-    outs = [p if i % 4 == 0 else moved(p, 0, "y", 4, i % 4) for i, p in enumerate(outs + outs1)]
-    attended = attended_call(place, outs)
 
     came = swapped(send)
-    both = [(keep[k].astype(F32) + came[k].astype(F32)) for k in range(4)]
-    total = both[0]
-    for k in range(1, 4):
-        total = total + moved(both[k].astype(BF16), 0, "y", 4, k).astype(F32)
-    total = total.astype(BF16)
-    own, later = total[:half], total[half:]
-    terms = [own] + [moved(own, 0, "x", 4, k) for k in range(1, 4)]
-    terms += [moved(later, -1, "x", 4, k) for k in range(4)]
-    part = latent_call(place, terms)
-    part_other = swapped(part)
-    ordered = jnp.where(core == 0, jnp.stack([part, part_other]), jnp.stack([part_other, part]))
-    latent_grad = ordered.reshape(TOK, PAY)[:, : LATENT + ROPE]
-    key_grad, value_grad = weight_call(dw0, dw1)
+    both = [keep[k].astype(F32) + came[k].astype(F32) for k in range(4)]
+    parts = fanned([both[0]] + [part.astype(BF16) for part in both[1:]], "y")
+    total = parts[0]
+    for part in parts[1:]:
+        total = total + part.astype(F32)
+    later = lax.ppermute(total[half:].astype(BF16), "z", behind)
+    later, dw0, outs0, outs1 = lax.optimization_barrier((later, dw0, outs0, outs1))
+    own = (total[:half] + later.astype(F32)).astype(BF16)
+    part = latent_call(place, fanned([own] * 4, "x"))
+    latent_grad = jnp.transpose(join_call(place, part, swapped(part)))
+    attended = attended_call(place, fanned(outs0, "y") + fanned(outs1, "y"))
+    key_grad, value_grad = weight_call(place, fanned(dw0, "y"), dw1)
     return attended, latent_grad, key_grad, value_grad
 
 

time: 159 us -> 125 us (0.79)
  the two profiles are of different devices: /device:TPU:224 before, /device:TPU:1 now
where the time goes in v3:
time: 125 us; the launch traced here: 122 us
  starting transfers between devices  63.6 us (51%)
  waiting for transfers between devices  25.7 us (21%)
  Pallas kernels  24.6 us (20%)
  local copies, waits for them, and re-layouts  5.99 us (5%)
  other arithmetic  1.27 us (1%)
    ppermute x24, starting transfers between devices, moved(): lax.ppermute(value, along, [(i, (i + step) % size) for i in range(size)])  27.6 us
    ppermute x24, waiting for transfers between devices, moved(): lax.ppermute(value, along, [(i, (i + step) % size) for i in range(size)])  22.4 us
    pallas_call x2, Pallas kernels, pair_call(): pl.pallas_call(functools.partial(pair_kernel, first), grid_spec=pltpu.Pre...  18.6 us
    ppermute x6, starting transfers between devices, swapped(): return lax.ppermute(value, 'core', [(0, 1), (1, 0)])  15.7 us
    all_to_all x2, starting transfers between devices, exchanged(): return lax.all_to_all(x, axes, split_axis=0, concat_axis=0, tiled=True)  14.6 us
    unnamed x57, local copies, waits for them, and re-layouts  5.75 us
    ppermute x1, starting transfers between devices, per_device(): earlier = lax.ppermute(pay, 'z', ahead)  4.38 us
    ppermute x1, waiting for transfers between devices, per_device(): later = lax.ppermute(total[half:].astype(BF16), 'z', behind)  3.26 us
  transfers between devices with their start and end apart: 34, of which 14 were waited for; matrix products, arithmetic and copies ran while one was open for 0% of the time, Pallas kernels for 19%

profile of v3, /device:TPU:1, one launch (start us, length us, event | category | flops | bytes accessed | tf_op | source)
XLA Modules:
  0.0 122.2 jit_solution(5398224348520926363)
XLA Ops:
  1.9 4.4 %collective-permute-start.3 = (bf16[64,640]{1,0:T(8,128)(2,1)S(1)}, bf16[64,640]{1,0:T(8,128)(2,1)S(1)}, u32[]{:S(2)}, u32[]{:S(2)}) collective-permute-start(bf16[64,640]{1,0:T(8,128)(2,1)S(1)} %pad_maximum_fusion), channel_id=1, source_target_pairs={{0,32},{32,64},{64,96},{96,128},{128,160},{160,192},{192,224},{1,3... | collective-permute-start | bytes 245768 | tf_op jit(solution)/shard_map/ppermute | solution.py:365
  11.2 2.6 %collective-permute-start.12 = (bf16[128,640]{1,0:T(8,128)(2,1)S(1)}, bf16[128,640]{1,0:T(8,128)(2,1)S(1)}, u32[]{:S(2)}, u32[]{:S(2)}) collective-permute-start(bf16[128,640]{1,0:T(8,128)(2,1)S(1)} %get-tuple-element.50), channel_id=1, source_target_pairs={{0,16},{8,24},{16,0},{24,8},{1,17},{9,25},{17,1},{25,9},{2,18},{10... | collective-permute-start | bytes 491528 | tf_op jit(solution)/shard_map/ppermute | solution.py:342
  16.0 1.9 %collective-permute-start.13 = (bf16[128,640]{1,0:T(8,128)(2,1)S(1)}, bf16[128,640]{1,0:T(8,128)(2,1)S(1)}, u32[]{:S(2)}, u32[]{:S(2)}) collective-permute-start(bf16[128,640]{1,0:T(8,128)(2,1)S(1)} %get-tuple-element.51), channel_id=1, source_target_pairs={{0,24},{8,0},{16,8},{24,16},{1,25},{9,1},{17,9},{25,17},{2,26},{10... | collective-permute-start | bytes 491528 | tf_op jit(solution)/shard_map/ppermute | solution.py:342
  18.0 2.7 %collective-permute-done.12.refs_2_ = bf16[128,640]{1,0:T(8,128)(2,1)S(1)} collective-permute-done((bf16[128,640]{1,0:T(8,128)(2,1)S(1)}, bf16[128,640]{1,0:T(8,128)(2,1)S(1)}, u32[]{:S(2)}, u32[]{:S(2)}) %collective-permute-start.12) | collective-permute-done | bytes 163872 | tf_op jit(solution)/shard_map/ppermute | solution.py:342
  20.6 3.4 %collective-permute-start.7 = (bf16[128,640]{1,0:T(8,128)(2,1)S(1)}, bf16[128,640]{1,0:T(8,128)(2,1)S(1)}, u32[]{:S(2)}, u32[]{:S(2)}) collective-permute-start(bf16[128,640]{1,0:T(8,128)(2,1)S(1)} %maximum_maximum_fusion.refs_4_), channel_id=1, source_target_pairs={{0,1},{1,0},{2,3},{3,2},{4,5},{5,4},{6,7},{7,6},{8,9},{9,8},{10,11... | collective-permute-start | bytes 491528 | tf_op jit(solution)/shard_map/ppermute | solution.py:350
  24.6 2.9 %collective-permute-start.9 = (bf16[128,640]{1,0:T(8,128)(2,1)S(1)}, bf16[128,640]{1,0:T(8,128)(2,1)S(1)}, u32[]{:S(2)}, u32[]{:S(2)}) collective-permute-start(bf16[128,640]{1,0:T(8,128)(2,1)S(1)} %collective-permute-done.5.refs_6_), channel_id=1, source_target_pairs={{0,1},{1,0},{2,3},{3,2},{4,5},{5,4},{6,7},{7,6},{8,9},{9,8},{10,11... | collective-permute-start | bytes 491528 | tf_op jit(solution)/shard_map/ppermute | solution.py:350
  29.5 1.5 %collective-permute-start.1 = (bf16[128,640]{1,0:T(8,128)(2,1)S(1)}, bf16[128,640]{1,0:T(8,128)(2,1)S(1)}, u32[]{:S(2)}, u32[]{:S(2)}) collective-permute-start(bf16[128,640]{1,0:T(8,128)(2,1)S(1)} %get-tuple-element.46), channel_id=1, source_target_pairs={{0,16},{8,24},{16,0},{24,8},{1,17},{9,25},{17,1},{25,9},{2,18},{10... | collective-permute-start | bytes 491528 | tf_op jit(solution)/shard_map/ppermute | solution.py:342
  32.8 9.2 %pair.2 = (bf16[1024,640]{1,0:T(8,128)(2,1)}, bf16[128,256]{1,0:T(8,128)(2,1)}, bf16[128,256]{1,0:T(8,128)(2,1)}, bf16[128,256]{1,0:T(8,128)(2,1)}, bf16[128,256]{1,0:T(8,128)(2,1)}, /*index=5*/bf16[512,512]{1,0:T(8,128)(2,1)}) custom-call(s32[4]{0:T(128)S(1)} %pad_add_fusion.where_ref, bf16[128,640]{1,0:T(8,128)(2,1)} %copy-done.6, ...), custom_call_target="tpu_custom_call" | custom-call | flops 4000000000 | bytes 8000000 | tf_op jit(solution)/shard_map/pair/pallas_call | solution.py:194
  42.0 7.3 %all-to-all-start = ((bf16[8,64,512]{2,1,0:T(8,128)(2,1)}), bf16[8,64,512]{2,1,0:T(8,128)(2,1)S(1)}, u32[]{:S(2)}, u32[]{:S(2)}) async-start(bf16[8,64,512]{2,1,0:T(8,128)(2,1)} %bitcast.22), calls=%async_computation | async-start | bytes 1048576 | tf_op jit(solution)/shard_map/all_to_all | solution.py:338
  51.4 9.4 %pair.3 = (bf16[4,128,640]{2,1,0:T(8,128)(2,1)S(1)}, bf16[4,128,640]{2,1,0:T(8,128)(2,1)S(1)}, bf16[128,256]{1,0:T(8,128)(2,1)}, bf16[128,256]{1,0:T(8,128)(2,1)...) custom-call(s32[4]{0:T(128)S(1)} %pad_add_fusion.where_ref, ...), custom_call_target="tpu_custom_call" | custom-call | flops 4000000000 | bytes 8000000 | tf_op jit(solution)/shard_map/pair/pallas_call | solution.py:194
  60.8 3.0 %collective-permute-start.14 = (bf16[4,128,640]{2,1,0:T(8,128)(2,1)S(1)}, bf16[4,128,640]{2,1,0:T(8,128)(2,1)S(1)}, u32[]{:S(2)}, u32[]{:S(2)}) collective-permute-start(bf16[4,128,640]{2,1,0:T(8,128)(2,1)S(1)} %get-tuple-element.54), channel_id=1, source_target_pairs={{0,1},{1,0},{2,3},{3,2},{4,5},{5,4},{6,7},{7,6},{8,9},{9,8},{10,11... | collective-permute-start | bytes 1966088 | tf_op jit(solution)/shard_map/ppermute | solution.py:350
  63.7 7.3 %all-to-all-start.1 = ((bf16[32,16,512]{2,1,0:T(8,128)(2,1)}), bf16[32,16,512]{2,1,0:T(8,128)(2,1)S(1)}, u32[]{:S(2)}, u32[]{:S(2)}) async-start(bf16[32,16,512]{2,1,0:T(8,128)(2,1)} %bitcast.21), calls=%async_computation.1 | async-start | bytes 1048576 | tf_op jit(solution)/shard_map/all_to_all | solution.py:338
  72.6 1.4 %collective-permute-start.17 = (bf16[128,640]{1,0:T(8,128)(2,1)S(1)}, bf16[128,640]{1,0:T(8,128)(2,1)S(1)}, u32[]{:S(2)}, u32[]{:S(2)}) collective-permute-start(bf16[128,640]{1,0:T(8,128)(2,1)S(1)} %get-tuple-element.85), channel_id=1, source_target_pairs={{0,24},{8,0},{16,8},{24,16},{1,25},{9,1},{17,9},{25,17},{2,26},{10... | collective-permute-start | bytes 491528 | tf_op jit(solution)/shard_map/ppermute | solution.py:342
  74.1 1.5 %collective-permute-start.16 = (bf16[128,640]{1,0:T(8,128)(2,1)S(1)}, bf16[128,640]{1,0:T(8,128)(2,1)S(1)}, u32[]{:S(2)}, u32[]{:S(2)}) collective-permute-start(bf16[128,640]{1,0:T(8,128)(2,1)S(1)} %get-tuple-element.86), channel_id=1, source_target_pairs={{0,16},{8,24},{16,0},{24,8},{1,17},{9,25},{17,1},{25,9},{2,18},{10... | collective-permute-start | bytes 491528 | tf_op jit(solution)/shard_map/ppermute | solution.py:342
  75.6 4.1 %collective-permute-done.15 = bf16[128,640]{1,0:T(8,128)(2,1)S(1)} collective-permute-done((bf16[128,640]{1,0:T(8,128)(2,1)S(1)}, bf16[128,640]{1,0:T(8,128)(2,1)S(1)}, u32[]{:S(2)}, u32[]{:S(2)}) %collective-permute-start.15) | collective-permute-done | bytes 163872 | tf_op jit(solution)/shard_map/ppermute | solution.py:342
  79.6 1.6 %collective-permute-done.17 = bf16[128,640]{1,0:T(8,128)(2,1)S(1)} collective-permute-done((bf16[128,640]{1,0:T(8,128)(2,1)S(1)}, bf16[128,640]{1,0:T(8,128)(2,1)S(1)}, u32[]{:S(2)}, u32[]{:S(2)}) %collective-permute-start.17) | collective-permute-done | bytes 163872 | tf_op jit(solution)/shard_map/ppermute | solution.py:342
  81.3 5.4 %collective-permute-done.16 = bf16[128,640]{1,0:T(8,128)(2,1)S(1)} collective-permute-done((bf16[128,640]{1,0:T(8,128)(2,1)S(1)}, bf16[128,640]{1,0:T(8,128)(2,1)S(1)}, u32[]{:S(2)}, u32[]{:S(2)}) %collective-permute-start.16) | collective-permute-done | bytes 163872 | tf_op jit(solution)/shard_map/ppermute | solution.py:342
  88.8 3.3 %collective-permute-done.18 = bf16[64,640]{1,0:T(8,128)(2,1)S(1)} collective-permute-done((bf16[64,640]{1,0:T(8,128)(2,1)S(1)}, bf16[64,640]{1,0:T(8,128)(2,1)S(1)}, u32[]{:S(2)}, u32[]{:S(2)}) %collective-permute-start.18) | collective-permute-done | bytes 81952 | tf_op jit(solution)/shard_map/ppermute | solution.py:385
  92.1 2.6 %collective-permute-start.27 = (bf16[64,640]{1,0:T(8,128)(2,1)S(1)}, bf16[64,640]{1,0:T(8,128)(2,1)S(1)}, u32[]{:S(2)}, u32[]{:S(2)}) collective-permute-start(bf16[64,640]{1,0:T(8,128)(2,1)S(1)} %fusion.5.refs_0_), channel_id=1, source_target_pairs={{0,6},{2,0},{4,2},{6,4},{1,7},{3,1},{5,3},{7,5},{8,14},{10,8},{12,... | collective-permute-start | bytes 245768 | tf_op jit(solution)/shard_map/ppermute | solution.py:342
  96.1 3.4 %collective-permute-done.26.refs_2_ = bf16[64,640]{1,0:T(8,128)(2,1)S(1)} collective-permute-done((bf16[64,640]{1,0:T(8,128)(2,1)S(1)}, bf16[64,640]{1,0:T(8,128)(2,1)S(1)}, u32[]{:S(2)}, u32[]{:S(2)}) %collective-permute-start.26) | collective-permute-done | bytes 81952 | tf_op jit(solution)/shard_map/ppermute | solution.py:342
  101.0 4.8 %collective-permute-start.28 = (f32[64,640]{1,0:T(8,128)S(1)}, f32[64,640]{1,0:T(8,128)S(1)}, u32[]{:S(2)}, u32[]{:S(2)}) collective-permute-start(f32[64,640]{1,0:T(8,128)S(1)} %latent.1.mine_ref), channel_id=1, source_target_pairs={{0,1},{1,0},{2,3},{3,2},{4,5},{5,4},{6,7},{7,6},{8,9},{9,8},{10,11... | collective-permute-start | bytes 491528 | tf_op jit(solution)/shard_map/ppermute | solution.py:350
  106.3 1.7 %collective-permute-start.20 = (bf16[128,256]{1,0:T(8,128)(2,1)S(1)}, bf16[128,256]{1,0:T(8,128)(2,1)S(1)}, u32[]{:S(2)}, u32[]{:S(2)}) collective-permute-start(bf16[128,256]{1,0:T(8,128)(2,1)S(1)} %copy-done.24), channel_id=1, source_target_pairs={{0,16},{8,24},{16,0},{24,8},{1,17},{9,25},{17,1},{25,9},{2,18},{10... | collective-permute-start | bytes 196616 | tf_op jit(solution)/shard_map/ppermute | solution.py:342
  111.4 1.8 %collective-permute-start.24 = (bf16[128,256]{1,0:T(8,128)(2,1)S(1)}, bf16[128,256]{1,0:T(8,128)(2,1)S(1)}, u32[]{:S(2)}, u32[]{:S(2)}) collective-permute-start(bf16[128,256]{1,0:T(8,128)(2,1)S(1)} %copy-done.23), channel_id=1, source_target_pairs={{0,24},{8,0},{16,8},{24,16},{1,25},{9,1},{17,9},{25,17},{2,26},{10... | collective-permute-start | bytes 196616 | tf_op jit(solution)/shard_map/ppermute | solution.py:342
  113.2 3.4 %collective-permute-start.30 = (bf16[16,512]{1,0:T(8,128)(2,1)S(1)}, bf16[16,512]{1,0:T(8,128)(2,1)S(1)}, u32[]{:S(2)}, u32[]{:S(2)}) collective-permute-start(bf16[16,512]{1,0:T(8,128)(2,1)S(1)} %get-tuple-element.79), channel_id=1, source_target_pairs={{0,16},{8,24},{16,0},{24,8},{1,17},{9,25},{17,1},{25,9},{2,18},{10... | collective-permute-start | bytes 49160 | tf_op jit(solution)/shard_map/ppermute | solution.py:342
  (120 shorter events, 30.5 us)
Async XLA Ops:
  1.9 11.9 %collective-permute-start.3 = (bf16[64,640]{1,0:T(8,128)(2,1)S(1)}, bf16[64,640]{1,0:T(8,128)(2,1)S(1)}, u32[]{:S(2)}, u32[]{:S(2)}) collective-permute-start(bf16[64,640]{1,0:T(8,128)(2,1)S(1)} %pad_maximum_fusion), channel_id=1, source_target_pairs={{0,32},{32,64},{64,96},{96,128},{128,160},{160,192},{192,224},{1,3... | collective-permute-start | bytes 245768 | tf_op jit(solution)/shard_map/ppermute | solution.py:365
  9.9 6.1 %collective-permute-start.11 = (bf16[128,640]{1,0:T(8,128)(2,1)S(1)}, bf16[128,640]{1,0:T(8,128)(2,1)S(1)}, u32[]{:S(2)}, u32[]{:S(2)}) collective-permute-start(bf16[128,640]{1,0:T(8,128)(2,1)S(1)} %get-tuple-element.49), channel_id=1, source_target_pairs={{0,8},{8,16},{16,24},{24,0},{1,9},{9,17},{17,25},{25,1},{2,10},{10... | collective-permute-start | bytes 491528 | tf_op jit(solution)/shard_map/ppermute | solution.py:342
  11.2 9.4 %collective-permute-start.12 = (bf16[128,640]{1,0:T(8,128)(2,1)S(1)}, bf16[128,640]{1,0:T(8,128)(2,1)S(1)}, u32[]{:S(2)}, u32[]{:S(2)}) collective-permute-start(bf16[128,640]{1,0:T(8,128)(2,1)S(1)} %get-tuple-element.50), channel_id=1, source_target_pairs={{0,16},{8,24},{16,0},{24,8},{1,17},{9,25},{17,1},{25,9},{2,18},{10... | collective-permute-start | bytes 491528 | tf_op jit(solution)/shard_map/ppermute | solution.py:342
  13.9 10.1 %collective-permute-start.6 = (bf16[128,640]{1,0:T(8,128)(2,1)S(1)}, bf16[128,640]{1,0:T(8,128)(2,1)S(1)}, u32[]{:S(2)}, u32[]{:S(2)}) collective-permute-start(bf16[128,640]{1,0:T(8,128)(2,1)S(1)} %maximum_maximum_fusion.refs_4_), channel_id=1, source_target_pairs={{0,24},{8,0},{16,8},{24,16},{1,25},{9,1},{17,9},{25,17},{2,26},{10... | collective-permute-start | bytes 491528 | tf_op jit(solution)/shard_map/ppermute | solution.py:342
  15.1 9.5 %collective-permute-start.5 = (bf16[128,640]{1,0:T(8,128)(2,1)S(1)}, bf16[128,640]{1,0:T(8,128)(2,1)S(1)}, u32[]{:S(2)}, u32[]{:S(2)}) collective-permute-start(bf16[128,640]{1,0:T(8,128)(2,1)S(1)} %maximum_maximum_fusion.refs_4_), channel_id=1, source_target_pairs={{0,16},{8,24},{16,0},{24,8},{1,17},{9,25},{17,1},{25,9},{2,18},{10... | collective-permute-start | bytes 491528 | tf_op jit(solution)/shard_map/ppermute | solution.py:342
  15.2 12.8 %collective-permute-start.4 = (bf16[128,640]{1,0:T(8,128)(2,1)S(1)}, bf16[128,640]{1,0:T(8,128)(2,1)S(1)}, u32[]{:S(2)}, u32[]{:S(2)}) collective-permute-start(bf16[128,640]{1,0:T(8,128)(2,1)S(1)} %maximum_maximum_fusion.refs_4_), channel_id=1, source_target_pairs={{0,8},{8,16},{16,24},{24,0},{1,9},{9,17},{17,25},{25,1},{2,10},{10... | collective-permute-start | bytes 491528 | tf_op jit(solution)/shard_map/ppermute | solution.py:342
  16.0 13.0 %collective-permute-start.13 = (bf16[128,640]{1,0:T(8,128)(2,1)S(1)}, bf16[128,640]{1,0:T(8,128)(2,1)S(1)}, u32[]{:S(2)}, u32[]{:S(2)}) collective-permute-start(bf16[128,640]{1,0:T(8,128)(2,1)S(1)} %get-tuple-element.51), channel_id=1, source_target_pairs={{0,24},{8,0},{16,8},{24,16},{1,25},{9,1},{17,9},{25,17},{2,26},{10... | collective-permute-start | bytes 491528 | tf_op jit(solution)/shard_map/ppermute | solution.py:342
  20.6 8.9 %collective-permute-start.7 = (bf16[128,640]{1,0:T(8,128)(2,1)S(1)}, bf16[128,640]{1,0:T(8,128)(2,1)S(1)}, u32[]{:S(2)}, u32[]{:S(2)}) collective-permute-start(bf16[128,640]{1,0:T(8,128)(2,1)S(1)} %maximum_maximum_fusion.refs_4_), channel_id=1, source_target_pairs={{0,1},{1,0},{2,3},{3,2},{4,5},{5,4},{6,7},{7,6},{8,9},{9,8},{10,11... | collective-permute-start | bytes 491528 | tf_op jit(solution)/shard_map/ppermute | solution.py:350
  24.1 7.0 %collective-permute-start.10 = (bf16[128,640]{1,0:T(8,128)(2,1)S(1)}, bf16[128,640]{1,0:T(8,128)(2,1)S(1)}, u32[]{:S(2)}, u32[]{:S(2)}) collective-permute-start(bf16[128,640]{1,0:T(8,128)(2,1)S(1)} %collective-permute-done.6.refs_7_), channel_id=1, source_target_pairs={{0,1},{1,0},{2,3},{3,2},{4,5},{5,4},{6,7},{7,6},{8,9},{9,8},{10,11... | collective-permute-start | bytes 491528 | tf_op jit(solution)/shard_map/ppermute | solution.py:350
  24.6 7.4 %collective-permute-start.9 = (bf16[128,640]{1,0:T(8,128)(2,1)S(1)}, bf16[128,640]{1,0:T(8,128)(2,1)S(1)}, u32[]{:S(2)}, u32[]{:S(2)}) collective-permute-start(bf16[128,640]{1,0:T(8,128)(2,1)S(1)} %collective-permute-done.5.refs_6_), channel_id=1, source_target_pairs={{0,1},{1,0},{2,3},{3,2},{4,5},{5,4},{6,7},{7,6},{8,9},{9,8},{10,11... | collective-permute-start | bytes 491528 | tf_op jit(solution)/shard_map/ppermute | solution.py:350
  29.1 20.2 %collective-permute-start = (bf16[128,640]{1,0:T(8,128)(2,1)S(1)}, bf16[128,640]{1,0:T(8,128)(2,1)S(1)}, u32[]{:S(2)}, u32[]{:S(2)}) collective-permute-start(bf16[128,640]{1,0:T(8,128)(2,1)S(1)} %get-tuple-element.45), channel_id=1, source_target_pairs={{0,8},{8,16},{16,24},{24,0},{1,9},{9,17},{17,25},{25,1},{2,10},{10... | collective-permute-start | bytes 491528 | tf_op jit(solution)/shard_map/ppermute | solution.py:342
  29.5 19.8 %collective-permute-start.1 = (bf16[128,640]{1,0:T(8,128)(2,1)S(1)}, bf16[128,640]{1,0:T(8,128)(2,1)S(1)}, u32[]{:S(2)}, u32[]{:S(2)}) collective-permute-start(bf16[128,640]{1,0:T(8,128)(2,1)S(1)} %get-tuple-element.46), channel_id=1, source_target_pairs={{0,16},{8,24},{16,0},{24,8},{1,17},{9,25},{17,1},{25,9},{2,18},{10... | collective-permute-start | bytes 491528 | tf_op jit(solution)/shard_map/ppermute | solution.py:342
  31.1 18.3 %collective-permute-start.2 = (bf16[128,640]{1,0:T(8,128)(2,1)S(1)}, bf16[128,640]{1,0:T(8,128)(2,1)S(1)}, u32[]{:S(2)}, u32[]{:S(2)}) collective-permute-start(bf16[128,640]{1,0:T(8,128)(2,1)S(1)} %get-tuple-element.47), channel_id=1, source_target_pairs={{0,24},{8,0},{16,8},{24,16},{1,25},{9,1},{17,9},{25,17},{2,26},{10... | collective-permute-start | bytes 491528 | tf_op jit(solution)/shard_map/ppermute | solution.py:342
  42.0 21.7 %all-to-all-start = ((bf16[8,64,512]{2,1,0:T(8,128)(2,1)}), bf16[8,64,512]{2,1,0:T(8,128)(2,1)S(1)}, u32[]{:S(2)}, u32[]{:S(2)}) async-start(bf16[8,64,512]{2,1,0:T(8,128)(2,1)} %bitcast.22), calls=%async_computation | async-start | bytes 1048576 | tf_op jit(solution)/shard_map/all_to_all | solution.py:338
  60.8 10.4 %collective-permute-start.14 = (bf16[4,128,640]{2,1,0:T(8,128)(2,1)S(1)}, bf16[4,128,640]{2,1,0:T(8,128)(2,1)S(1)}, u32[]{:S(2)}, u32[]{:S(2)}) collective-permute-start(bf16[4,128,640]{2,1,0:T(8,128)(2,1)S(1)} %get-tuple-element.54), channel_id=1, source_target_pairs={{0,1},{1,0},{2,3},{3,2},{4,5},{5,4},{6,7},{7,6},{8,9},{9,8},{10,11... | collective-permute-start | bytes 1966088 | tf_op jit(solution)/shard_map/ppermute | solution.py:350
  63.7 55.7 %all-to-all-start.1 = ((bf16[32,16,512]{2,1,0:T(8,128)(2,1)}), bf16[32,16,512]{2,1,0:T(8,128)(2,1)S(1)}, u32[]{:S(2)}, u32[]{:S(2)}) async-start(bf16[32,16,512]{2,1,0:T(8,128)(2,1)} %bitcast.21), calls=%async_computation.1 | async-start | bytes 1048576 | tf_op jit(solution)/shard_map/all_to_all | solution.py:338
  71.3 8.3 %collective-permute-start.15 = (bf16[128,640]{1,0:T(8,128)(2,1)S(1)}, bf16[128,640]{1,0:T(8,128)(2,1)S(1)}, u32[]{:S(2)}, u32[]{:S(2)}) collective-permute-start(bf16[128,640]{1,0:T(8,128)(2,1)S(1)} %get-tuple-element.84), channel_id=1, source_target_pairs={{0,8},{8,16},{16,24},{24,0},{1,9},{9,17},{17,25},{25,1},{2,10},{10... | collective-permute-start | bytes 491528 | tf_op jit(solution)/shard_map/ppermute | solution.py:342
  72.6 8.7 %collective-permute-start.17 = (bf16[128,640]{1,0:T(8,128)(2,1)S(1)}, bf16[128,640]{1,0:T(8,128)(2,1)S(1)}, u32[]{:S(2)}, u32[]{:S(2)}) collective-permute-start(bf16[128,640]{1,0:T(8,128)(2,1)S(1)} %get-tuple-element.85), channel_id=1, source_target_pairs={{0,24},{8,0},{16,8},{24,16},{1,25},{9,1},{17,9},{25,17},{2,26},{10... | collective-permute-start | bytes 491528 | tf_op jit(solution)/shard_map/ppermute | solution.py:342
  74.1 12.7 %collective-permute-start.16 = (bf16[128,640]{1,0:T(8,128)(2,1)S(1)}, bf16[128,640]{1,0:T(8,128)(2,1)S(1)}, u32[]{:S(2)}, u32[]{:S(2)}) collective-permute-start(bf16[128,640]{1,0:T(8,128)(2,1)S(1)} %get-tuple-element.86), channel_id=1, source_target_pairs={{0,16},{8,24},{16,0},{24,8},{1,17},{9,25},{17,1},{25,9},{2,18},{10... | collective-permute-start | bytes 491528 | tf_op jit(solution)/shard_map/ppermute | solution.py:342
  86.9 5.2 %collective-permute-start.18 = (bf16[64,640]{1,0:T(8,128)(2,1)S(1)}, bf16[64,640]{1,0:T(8,128)(2,1)S(1)}, u32[]{:S(2)}, u32[]{:S(2)}) collective-permute-start(bf16[64,640]{1,0:T(8,128)(2,1)S(1)} %slice.59), channel_id=1, source_target_pairs={{32,0},{64,32},{96,64},{128,96},{160,128},{192,160},{224,192},{33,... | collective-permute-start | bytes 245768 | tf_op jit(solution)/shard_map/ppermute | solution.py:385
  101.0 19.8 %collective-permute-start.28 = (f32[64,640]{1,0:T(8,128)S(1)}, f32[64,640]{1,0:T(8,128)S(1)}, u32[]{:S(2)}, u32[]{:S(2)}) collective-permute-start(f32[64,640]{1,0:T(8,128)S(1)} %latent.1.mine_ref), channel_id=1, source_target_pairs={{0,1},{1,0},{2,3},{3,2},{4,5},{5,4},{6,7},{7,6},{8,9},{9,8},{10,11... | collective-permute-start | bytes 491528 | tf_op jit(solution)/shard_map/ppermute | solution.py:350
  110.8 5.8 %collective-permute-start.23 = (bf16[128,256]{1,0:T(8,128)(2,1)S(1)}, bf16[128,256]{1,0:T(8,128)(2,1)S(1)}, u32[]{:S(2)}, u32[]{:S(2)}) collective-permute-start(bf16[128,256]{1,0:T(8,128)(2,1)S(1)} %copy-done.25), channel_id=1, source_target_pairs={{0,16},{8,24},{16,0},{24,8},{1,17},{9,25},{17,1},{25,9},{2,18},{10... | collective-permute-start | bytes 196616 | tf_op jit(solution)/shard_map/ppermute | solution.py:342
  111.4 5.2 %collective-permute-start.24 = (bf16[128,256]{1,0:T(8,128)(2,1)S(1)}, bf16[128,256]{1,0:T(8,128)(2,1)S(1)}, u32[]{:S(2)}, u32[]{:S(2)}) collective-permute-start(bf16[128,256]{1,0:T(8,128)(2,1)S(1)} %copy-done.23), channel_id=1, source_target_pairs={{0,24},{8,0},{16,8},{24,16},{1,25},{9,1},{17,9},{25,17},{2,26},{10... | collective-permute-start | bytes 196616 | tf_op jit(solution)/shard_map/ppermute | solution.py:342
  113.2 5.3 %collective-permute-start.30 = (bf16[16,512]{1,0:T(8,128)(2,1)S(1)}, bf16[16,512]{1,0:T(8,128)(2,1)S(1)}, u32[]{:S(2)}, u32[]{:S(2)}) collective-permute-start(bf16[16,512]{1,0:T(8,128)(2,1)S(1)} %get-tuple-element.79), channel_id=1, source_target_pairs={{0,16},{8,24},{16,0},{24,8},{1,17},{9,25},{17,1},{25,9},{2,18},{10... | collective-permute-start | bytes 49160 | tf_op jit(solution)/shard_map/ppermute | solution.py:342
  (38 other events, 463.8 us)

commit v4 on v3

v4 whole, which is shorter than its diff:
```python
import functools
import math

import jax
import jax.numpy as jnp
from jax import lax
from jax.experimental import pallas as pl
from jax.experimental.pallas import tpu as pltpu
from jax.sharding import Mesh
from jax.sharding import PartitionSpec as P

NOPE = 128
ROPE = 64
VDIM = 128
LATENT = 512
TOK = 128
ROWS = 4 * TOK
KEYS = 2 * ROWS
TILE = 256
SPAN = ROWS + TILE
PAY = 640
SCALE = 1.0 / math.sqrt(NOPE + ROPE)
LOG2E = math.log2(math.e)
HIDDEN = -1e30
GROUPS = 8
F32 = jnp.float32
BF16 = jnp.bfloat16
SMALL = pltpu.CompilerParams(vmem_limit_bytes=12 << 20)


def nt(a, b):
    return lax.dot_general(a, b, (((1,), (1,)), ((), ())), preferred_element_type=F32)


def nn(a, b):
    return lax.dot_general(a, b, (((1,), (0,)), ((), ())), preferred_element_type=F32)


def tn(a, b):
    return lax.dot_general(a, b, (((0,), (0,)), ((), ())), preferred_element_type=F32)


def in_hbm(x):
    return pltpu.with_memory_space_constraint(x, pltpu.HBM)


def pack_kernel(q_ref, g_ref, earlier_ref, own_ref, out_ref):
    for pair in range(2):
        rows = slice(pair * TOK, (pair + 1) * TOK)
        out_ref[0, rows, :384] = q_ref[:, pair * 384 : (pair + 1) * 384]
        out_ref[0, rows, 384:] = g_ref[:, pair * 256 : (pair + 1) * 256]
    out_ref[0, 2 * TOK : 2 * TOK + TOK // 2, :] = earlier_ref[...]
    out_ref[0, 2 * TOK + TOK // 2 :, :] = own_ref[...]


def pack_call(queries, out_grad, earlier, own):
    half = pl.BlockSpec((TOK // 2, PAY), lambda y: (0, 0))
    return pl.pallas_call(
        pack_kernel,
        grid=(4,),
        in_specs=[
            pl.BlockSpec((TOK, 768), lambda y: (0, y)),
            pl.BlockSpec((TOK, 512), lambda y: (0, y)),
            half,
            half,
        ],
        out_specs=pl.BlockSpec((1, 3 * TOK, PAY), lambda y: (y, 0, 0)),
        out_shape=pltpu.HBM((4, 3 * TOK, PAY), BF16),
        cost_estimate=pl.CostEstimate(flops=0, bytes_accessed=3_300_000, transcendentals=0),
        compiler_params=SMALL,
        name="pack",
    )(in_hbm(queries), in_hbm(out_grad), earlier, own)


def pair_kernel(where_ref, x_ref, mine_ref, other_ref, wk_ref, wv_ref, *refs):
    keep_ref, send_ref, out_refs, dw_ref = refs[0], refs[1], refs[2:6], refs[6]
    l_ref, kcat, vals, bias, dk_acc, dv_acc, grads, attended, dl_acc = refs[7:]
    group, y, core = where_ref[0], where_ref[1], where_ref[2]
    pair = pl.program_id(0)
    half = TOK // 2
    lane = lax.broadcasted_iota(jnp.int32, (KEYS, 128), 1)
    low = lane < ROPE

    @pl.when(pair == 0)
    def _():
        for block in range(4):
            for own in range(2):
                row = own * ROWS + block * TOK
                piece = slice(own * half, (own + 1) * half)
                at = pl.multiple_of(row + core * half, half)
                l_ref[pl.ds(at, half), :] = mine_ref[block, piece]
                at = pl.multiple_of(row + (1 - core) * half, half)
                l_ref[pl.ds(at, half), :] = other_ref[block, piece]
        ids = l_ref[:, LATENT:].astype(F32)
        key_id = ids[:, ROPE : ROPE + 1]
        key_row = lax.broadcasted_iota(jnp.int32, (KEYS, 1), 0)
        key_id = jnp.where((key_row < ROWS) & (group == 0), -1.0, key_id)
        query_id = jnp.transpose(ids[ROWS:])[ROPE : ROPE + 1, :]
        for i in range(2):
            start = i * TILE
            at = lax.broadcasted_iota(jnp.int32, (SPAN, TILE), 0)
            by = lax.broadcasted_iota(jnp.int32, (SPAN, TILE), 1)
            seen = (key_id[start : start + SPAN] == query_id[:, start : start + TILE]) & (
                at <= by + ROWS
            )
            bias[i] = jnp.where(seen, 0.0, HIDDEN)

    lat = l_ref[:, :LATENT]
    tail = l_ref[:, LATENT:].astype(F32)
    keys_up = nn(lat, wk_ref[...])
    vals_up = nn(lat, wv_ref[...])
    vals[...] = vals_up.astype(BF16)
    rope_low = jnp.where(low, tail, 0.0)
    rope_high = pltpu.roll(rope_low, ROPE, 1)
    turned = pltpu.roll(keys_up[:, NOPE:], ROPE, 1)
    kcat[0, :, :NOPE] = keys_up[:, :NOPE].astype(BF16)
    kcat[0, :, NOPE:] = rope_low.astype(BF16)
    kcat[1, :, :NOPE] = jnp.where(low, 0.0, turned).astype(BF16)
    kcat[1, :, NOPE:] = jnp.where(low, turned, rope_high).astype(BF16)

    for h in range(2):
        v_turned = jnp.transpose(vals_up[:, h * VDIM : (h + 1) * VDIM]).astype(BF16)
        for i in range(2):
            start = i * TILE
            span = slice(start, start + SPAN)
            rows = slice(start, start + TILE)
            qc = x_ref[2 * i : 2 * i + 2, :, h * NOPE : h * NOPE + 256].reshape(TILE, 256)
            og = x_ref[2 * i : 2 * i + 2, :, 384 + h * VDIM : 384 + (h + 1) * VDIM]
            og = og.reshape(TILE, VDIM)
            s = nt(kcat[h, span, :], qc) * (SCALE * LOG2E) + bias[i]
            top = jnp.max(s, axis=0, keepdims=True)
            e = jnp.exp2(s - top)
            p = e * (1.0 / jnp.sum(e, axis=0, keepdims=True))
            pb = p.astype(BF16)
            out_t = nn(v_turned[:, span], pb).astype(BF16).astype(F32)
            attended[rows, h * VDIM : (h + 1) * VDIM] = jnp.transpose(out_t).astype(BF16)
            og_t = jnp.transpose(og.astype(F32))
            delta = jnp.sum(og_t * out_t, axis=0, keepdims=True)
            dp = nn(vals[span, h * VDIM : (h + 1) * VDIM], og_t.astype(BF16))
            ds = (p * (dp - delta) * SCALE).astype(BF16)
            dk = nn(ds, qc)
            dv = nn(pb, og)
            if i == 0:
                dk_acc[h, :SPAN, :] = dk
                dv_acc[:SPAN, :] = dv
            else:
                dk_acc[h, TILE : ROWS + TILE, :] += dk[:ROWS]
                dv_acc[TILE : ROWS + TILE, :] += dv[:ROWS]
                dk_acc[h, SPAN:, :] = dk[ROWS:]
                dv_acc[SPAN:, :] = dv[ROWS:]
        grads[:, 256 + h * VDIM : 256 + (h + 1) * VDIM] = dv_acc[...].astype(BF16)
    column = pl.ds(pl.multiple_of(pair * 256, 256), 256)
    for k in range(4):
        to = pl.multiple_of(((y + k) & 3) * TOK, TOK)
        out_refs[k][:, column] = attended[pl.ds(to, TOK), :]
    grads[:, :NOPE] = dk_acc[0, :, :NOPE].astype(BF16)
    mixed = jnp.where(low, dk_acc[1, :, NOPE:], dk_acc[1, :, :NOPE])
    grads[:, NOPE : 2 * NOPE] = pltpu.roll(mixed, ROPE, 1).astype(BF16)
    rope_grad = jnp.where(low, dk_acc[0, :, NOPE:], dk_acc[1, :, NOPE:])
    rope_grad = rope_grad + pltpu.roll(rope_grad, ROPE, 1)
    dl = nt(grads[:, :256], wk_ref[...]) + nt(grads[:, 256:], wv_ref[...])
    dw_ref[...] = tn(lat, grads[...]).astype(BF16)

    @pl.when(pair == 0)
    def _():
        dl_acc[:, :LATENT] = dl
        dl_acc[:, LATENT:] = rope_grad

    @pl.when(pair == 1)
    def _():
        dl_acc[:, :LATENT] += dl
        dl_acc[:, LATENT:] += rope_grad
        for k in range(4):
            for back in range(2):
                row = (1 - back) * ROWS + ((y + k) & 3) * TOK
                piece = slice(back * half, (back + 1) * half)
                at = pl.multiple_of(row + core * half, half)
                keep_ref[k, piece, :] = dl_acc[pl.ds(at, half), :].astype(BF16)
                at = pl.multiple_of(row + (1 - core) * half, half)
                send_ref[k, piece, :] = dl_acc[pl.ds(at, half), :].astype(BF16)


def pair_call(place, x, other, key_weight, value_weight):
    def whole(*shape):
        return pl.BlockSpec(shape, lambda i, w: (0,) * len(shape))

    weight_spec = pl.BlockSpec((LATENT, 256), lambda i, w: (0, 2 * w[1] + i))
    x_spec = pl.BlockSpec((4, TOK, PAY), lambda i, w: (0, i, 0))
    lat_spec = pl.BlockSpec((4, TOK, PAY), lambda i, w: (0, 2, 0))
    dw_spec = pl.BlockSpec((LATENT, 512), lambda i, w: (0, i))
    return pl.pallas_call(
        pair_kernel,
        grid_spec=pltpu.PrefetchScalarGridSpec(
            num_scalar_prefetch=1,
            grid=(2,),
            in_specs=[x_spec, lat_spec, whole(4, TOK, PAY), weight_spec, weight_spec],
            out_specs=[whole(4, TOK, PAY)] * 2 + [whole(TOK, 512)] * 4 + [dw_spec],
            scratch_shapes=[
                pltpu.VMEM((KEYS, PAY), BF16),
                pltpu.VMEM((2, KEYS, 256), BF16),
                pltpu.VMEM((KEYS, 256), BF16),
                pltpu.VMEM((2, SPAN, TILE), F32),
                pltpu.VMEM((2, KEYS, 256), F32),
                pltpu.VMEM((KEYS, VDIM), F32),
                pltpu.VMEM((KEYS, 512), BF16),
                pltpu.VMEM((ROWS, 256), BF16),
                pltpu.VMEM((KEYS, PAY), F32),
            ],
        ),
        out_shape=[pltpu.HBM((4, TOK, PAY), BF16)] * 2
        + [pltpu.HBM((TOK, 512), BF16)] * 4
        + [pltpu.HBM((LATENT, 1024), BF16)],
        compiler_params=pltpu.CompilerParams(vmem_limit_bytes=40 << 20),
        cost_estimate=pl.CostEstimate(
            flops=8_000_000_000, bytes_accessed=10_000_000, transcendentals=1_600_000
        ),
        name="pair",
    )(place, in_hbm(x), in_hbm(x), in_hbm(other), in_hbm(key_weight), in_hbm(value_weight))


def latent_kernel(where_ref, *refs):
    terms, out_ref, held = refs[:4], refs[4], refs[5]
    x = where_ref[3]
    for k in range(4):
        held[(x - k) & 3] = terms[k][...].astype(F32)
    out_ref[...] = (held[0] + held[1]) + (held[2] + held[3])


def latent_call(place, terms):
    vmem = pl.BlockSpec(memory_space=pltpu.VMEM)
    return pl.pallas_call(
        latent_kernel,
        in_specs=[pl.BlockSpec(memory_space=pltpu.SMEM)] + [vmem] * 4,
        out_specs=vmem,
        out_shape=jax.ShapeDtypeStruct((TOK // 2, PAY), F32),
        scratch_shapes=[pltpu.VMEM((4, TOK // 2, PAY), F32)],
        compiler_params=SMALL,
        name="latent",
    )(place, *terms)


def join_kernel(where_ref, mine_ref, other_ref, out_ref):
    first = where_ref[2] == 0
    mine, other = mine_ref[...], other_ref[...]
    rows = jnp.concatenate(
        [jnp.where(first, mine, other), jnp.where(first, other, mine)], axis=0
    )
    out_ref[...] = jnp.transpose(rows)[: LATENT + ROPE]


def join_call(place, mine, other):
    vmem = pl.BlockSpec(memory_space=pltpu.VMEM)
    return pl.pallas_call(
        join_kernel,
        in_specs=[pl.BlockSpec(memory_space=pltpu.SMEM), vmem, vmem],
        out_specs=vmem,
        out_shape=jax.ShapeDtypeStruct((LATENT + ROPE, TOK), F32),
        compiler_params=SMALL,
        name="join",
    )(place, mine, other)


def attended_kernel(where_ref, *refs):
    pieces, out_ref = refs[:4], refs[4]
    y = where_ref[1]
    for k in range(4):
        column = pl.multiple_of(((y - k) & 3) * 512, 512)
        out_ref[:, pl.ds(column, 512)] = pieces[k][...]


def attended_call(place, pieces):
    vmem = pl.BlockSpec(memory_space=pltpu.VMEM)
    return pl.pallas_call(
        attended_kernel,
        in_specs=[pl.BlockSpec(memory_space=pltpu.SMEM)] + [vmem] * 4,
        out_specs=vmem,
        out_shape=jax.ShapeDtypeStruct((TOK, 2048), BF16),
        compiler_params=SMALL,
        name="attended",
    )(place, *pieces)


def half_kernel(where_ref, sent_ref, *piece_refs):
    y = where_ref[1]
    for k in range(4):
        row = pl.ds(pl.multiple_of(((y + k) & 3) * 16, 16), 16)
        total = sent_ref[0, row, :].astype(F32)
        for z in range(1, GROUPS):
            total = total + sent_ref[z, row, :].astype(F32)
        piece_refs[k][...] = total.astype(BF16)


def half_call(place, sent):
    vmem = pl.BlockSpec(memory_space=pltpu.VMEM)
    return pl.pallas_call(
        half_kernel,
        in_specs=[pl.BlockSpec(memory_space=pltpu.SMEM), vmem],
        out_specs=[vmem] * 4,
        out_shape=[jax.ShapeDtypeStruct((16, 1024), BF16)] * 4,
        compiler_params=SMALL,
        name="half",
    )(place, sent)


def weight_kernel(where_ref, *refs):
    pieces, key_ref, value_ref = refs[:4], refs[4], refs[5]
    y = where_ref[1]
    for k in range(4):
        column = ((y - k) & 3) * 512
        for pair in range(2):
            here = pl.ds(pl.multiple_of(column + pair * 256, 256), 256)
            key_ref[:, here] = pieces[k][:, pair * 512 : pair * 512 + 256].astype(F32)
            value_ref[:, here] = pieces[k][:, pair * 512 + 256 : pair * 512 + 512].astype(F32)


def weight_call(place, pieces):
    vmem = pl.BlockSpec(memory_space=pltpu.VMEM)
    return pl.pallas_call(
        weight_kernel,
        in_specs=[pl.BlockSpec(memory_space=pltpu.SMEM)] + [vmem] * 4,
        out_specs=[vmem] * 2,
        out_shape=[jax.ShapeDtypeStruct((16, 2048), F32)] * 2,
        compiler_params=SMALL,
        name="weight",
    )(place, *pieces)


def exchanged(x, axes):
    return lax.all_to_all(x, axes, split_axis=0, concat_axis=0, tiled=True)


def moved(value, along, size, step):
    return lax.ppermute(value, along, [(i, (i + step) % size) for i in range(size)])


def fanned(pieces, along):
    return [p if k == 0 else moved(p, along, 4, k) for k, p in enumerate(pieces)]


def swapped(value):
    return lax.ppermute(value, "core", [(0, 1), (1, 0)])


def per_device(queries, latents, doc_ids, key_weight, value_weight, out_grad):
    core = lax.axis_index("core")
    place = [lax.axis_index("z"), lax.axis_index("y"), core, lax.axis_index("x")]
    place = jnp.stack(place).astype(jnp.int32)
    half = TOK // 2
    rows = lax.dynamic_slice_in_dim(latents, core * half, half)
    ids = lax.dynamic_slice_in_dim(doc_ids, core * half, half)
    pay = jnp.concatenate(
        [rows, ids.astype(BF16)[:, None], jnp.zeros((half, PAY - 577), BF16)], axis=1
    )
    ahead = [(i, i + 1) for i in range(GROUPS - 1)]
    behind = [(i + 1, i) for i in range(GROUPS - 1)]
    earlier = lax.ppermute(pay, "z", ahead)
    x = exchanged(pack_call(queries, out_grad, earlier, pay), "y")
    other = swapped(x[:, 2 * TOK :])
    keep, send, *outs, dw = pair_call(place, x, other, key_weight, value_weight)

    came = swapped(send)
    dw = half_call(place, exchanged(dw.reshape(8, 64, 1024), "z"))
    both = [keep[k].astype(F32) + came[k].astype(F32) for k in range(4)]
    parts = fanned([both[0]] + [part.astype(BF16) for part in both[1:]], "y")
    total = parts[0]
    for part in parts[1:]:
        total = total + part.astype(F32)
    later, outs = lax.optimization_barrier((total[half:].astype(BF16), outs))
    later = lax.ppermute(later, "z", behind)
    own = (total[:half] + later.astype(F32)).astype(BF16)
    part = latent_call(place, fanned([own] * 4, "x"))
    latent_grad = jnp.transpose(join_call(place, part, swapped(part)))
    attended = attended_call(place, fanned(outs, "y"))
    key_grad, value_grad = weight_call(place, fanned(dw, "y"))
    return attended, latent_grad, key_grad, value_grad


def solution(mesh):
    split = Mesh(mesh.devices.reshape(GROUPS, 4, 4, 2), ("z", "y", "x", "core"))
    seq, head = ("z", "y"), ("x", "core")
    in_specs = (P(seq, head), P(seq, None), P(seq), P(None, head), P(None, head), P(seq, head))
    out_specs = (P(seq, head), P(seq, None), P(seq, head), P(seq, head))
    return jax.shard_map(
        per_device, mesh=split, in_specs=in_specs, out_specs=out_specs, check_vma=False
    )
```

time: 125 us -> 121 us (0.968); the launches traced: 122 us -> 121 us
  starting transfers between devices: 63.6 us -> 33.6 us
  blocking collectives: 0 us -> 27.3 us
  waiting for transfers between devices: 25.7 us -> 30.9 us
  local copies, waits for them, and re-layouts: 5.99 us -> 1.42 us
    all_to_all x0 -> x1, blocking collectives: none -> 27.3 us  [exchanged(): return lax.all_to_all(x, axes, split_axis=0, concat_axis=0, tiled=True)]
    ppermute x24 -> x12, starting transfers between devices: 27.6 us -> 12.1 us  [moved(): lax.ppermute(value, along, [(i, (i + step) % size) for i in range(size)])]
    ppermute x1, waiting for transfers between devices: 3.26 us -> 15.5 us  [per_device(): later = lax.ppermute(later, 'z', behind)]
    ppermute x24 -> x12, waiting for transfers between devices: 22.4 us -> 12.3 us  [moved(): lax.ppermute(value, along, [(i, (i + step) % size) for i in range(size)])]
    ppermute x6 -> x3, starting transfers between devices: 15.7 us -> 6.13 us  [swapped(): return lax.ppermute(value, 'core', [(0, 1), (1, 0)])]
    all_to_all x2 -> x1, starting transfers between devices: 14.6 us -> 9.7 us  [exchanged(): return lax.all_to_all(x, axes, split_axis=0, concat_axis=0, tiled=True)]
    unnamed x57 -> x17, local copies, waits for them, and re-layouts: 5.75 us -> 1.05 us
    ppermute x6 -> x3, waiting for transfers between devices: 0.02 us -> 1.65 us  [swapped(): return lax.ppermute(value, 'core', [(0, 1), (1, 0)])]
  transfers between devices with their start and end apart: 34 -> 18, of which waited for: 14 -> 10; matrix products, arithmetic and copies ran while one was open for 0% -> 0% of each run, Pallas kernels for 19% -> 3%
where the time goes in v4:
time: 121 us
  starting transfers between devices  33.6 us (28%)
  waiting for transfers between devices  30.9 us (26%)
  blocking collectives  27.3 us (23%)
  Pallas kernels  25.7 us (21%)
  local copies, waits for them, and re-layouts  1.42 us (1%)
    all_to_all x1, blocking collectives, exchanged(): return lax.all_to_all(x, axes, split_axis=0, concat_axis=0, tiled=True)  27.3 us
    pallas_call x1, Pallas kernels, pair_call(): pl.pallas_call(pair_kernel, grid_spec=pltpu.PrefetchScalarGridSpec(num_sc...  16.6 us
    ppermute x1, waiting for transfers between devices, per_device(): later = lax.ppermute(later, 'z', behind)  15.5 us
    ppermute x12, waiting for transfers between devices, moved(): lax.ppermute(value, along, [(i, (i + step) % size) for i in range(size)])  12.3 us
    ppermute x12, starting transfers between devices, moved(): lax.ppermute(value, along, [(i, (i + step) % size) for i in range(size)])  12.1 us
    all_to_all x1, starting transfers between devices, exchanged(): return lax.all_to_all(x, axes, split_axis=0, concat_axis=0, tiled=True)  9.7 us
    ppermute x3, starting transfers between devices, swapped(): return lax.ppermute(value, 'core', [(0, 1), (1, 0)])  6.13 us
    ppermute x1, starting transfers between devices, per_device(): earlier = lax.ppermute(pay, 'z', ahead)  4.36 us
  transfers between devices with their start and end apart: 18, of which 10 were waited for; matrix products, arithmetic and copies ran while one was open for 0% of the time, Pallas kernels for 3%

profile of v4, /device:TPU:1, one launch (start us, length us, event | category | flops | bytes accessed | tf_op | source)
XLA Modules:
  0.0 121.0 jit_solution(3125050929634135317)
XLA Ops:
  2.0 4.4 %collective-permute-start = (bf16[64,640]{1,0:T(8,128)(2,1)S(1)}, bf16[64,640]{1,0:T(8,128)(2,1)S(1)}, u32[]{:S(2)}, u32[]{:S(2)}) collective-permute-start(bf16[64,640]{1,0:T(8,128)(2,1)S(1)} %maximum_maximum_fusion.own_ref), channel_id=1, source_target_pairs={{0,32},{32,64},{64,96},{96,128},{128,160},{160,192},{192,224},{1,3... | collective-permute-start | bytes 245768 | tf_op jit(solution)/shard_map/ppermute | solution.py:356
  6.4 1.5 %collective-permute-done.earlier_ref = bf16[64,640]{1,0:T(8,128)(2,1)S(1)} collective-permute-done((bf16[64,640]{1,0:T(8,128)(2,1)S(1)}, bf16[64,640]{1,0:T(8,128)(2,1)S(1)}, u32[]{:S(2)}, u32[]{:S(2)}) %collective-permute-start) | collective-permute-done | bytes 81952 | tf_op jit(solution)/shard_map/ppermute | solution.py:356
  7.8 3.7 %pack.1 = bf16[4,384,640]{2,1,0:T(8,128)(2,1)} custom-call(bf16[128,3072]{1,0:T(8,128)(2,1)} %q_ref.1, bf16[128,2048]{1,0:T(8,128)(2,1)} %g_ref.1, bf16[64,640]{1,0:T(8,128)(2,1)S(1)} %collective-permute-done.earlier_ref, bf16[64,640]{1,0:T(8,128)(2,1)S(1)} %maximum_maximum_fusion.own_ref), custom_call_target="tpu_custom_call" | custom-call | bytes 3300000 | tf_op jit(solution)/shard_map/pack/pallas_call | solution.py:58
  11.5 27.3 %all_to_all.10.x_ref.mine_ref = bf16[4,384,640]{2,1,0:T(8,128)(2,1)S(1)} all-to-all(bf16[4,384,640]{2,1,0:T(8,128)(2,1)} %pack.1), channel_id=1, replica_groups=mesh['z'=8,'y'=4,'x'=4,'core'=2] {'y'}, dimensions={0} | all-to-all | bytes 3932160 | tf_op jit(solution)/shard_map/all_to_all | solution.py:329
  38.9 2.8 %collective-permute-start.1 = (bf16[4,128,640]{2,1,0:T(8,128)(2,1)S(1)}, bf16[4,128,640]{2,1,0:T(8,128)(2,1)S(1)}, u32[]{:S(2)}, u32[]{:S(2)}) collective-permute-start(bf16[4,128,640]{2,1,0:T(8,128)(2,1)S(1)} %slice.45), channel_id=1, source_target_pairs={{0,1},{1,0},{2,3},{3,2},{4,5},{5,4},{6,7},{7,6},{8,9},{9,8},{10,11... | collective-permute-start | bytes 1966088 | tf_op jit(solution)/shard_map/ppermute | solution.py:341
  41.8 1.6 %collective-permute-done.1.other_ref = bf16[4,128,640]{2,1,0:T(8,128)(2,1)S(1)} collective-permute-done((bf16[4,128,640]{2,1,0:T(8,128)(2,1)S(1)}, bf16[4,128,640]{2,1,0:T(8,128)(2,1)S(1)}, u32[]{:S(2)}, u32[]{:S(2)}) %collective-permute-start.1) | collective-permute-done | bytes 655392 | tf_op jit(solution)/shard_map/ppermute | solution.py:341
  43.5 0.9 copy-done.4
  44.3 16.6 %pair.1 = (bf16[4,128,640]{2,1,0:T(8,128)(2,1)}, bf16[4,128,640]{2,1,0:T(8,128)(2,1)}, bf16[128,512]{1,0:T(8,128)(2,1)}, bf16[128,512]{1,0:T(8,128)(2,1)}, bf16[...) custom-call(s32[4]{0:T(128)S(1)} %pad_add_fusion.where_ref, ...), custom_call_target="tpu_custom_call" | custom-call | flops 8000000000 | bytes 10000000 | tf_op jit(solution)/shard_map/pair/pallas_call | solution.py:191
  61.4 9.7 %all-to-all-start.1 = ((bf16[8,64,1024]{2,1,0:T(8,128)(2,1)}), bf16[8,64,1024]{2,1,0:T(8,128)(2,1)S(1)}, u32[]{:S(2)}, u32[]{:S(2)}) async-start(bf16[8,64,1024]{2,1,0:T(8,128)(2,1)} %bitcast.20), calls=%async_computation.1 | async-start | bytes 2097152 | tf_op jit(solution)/shard_map/all_to_all | solution.py:329
  71.6 2.4 %collective-permute-start.5 = (bf16[128,640]{1,0:T(8,128)(2,1)S(1)}, bf16[128,640]{1,0:T(8,128)(2,1)S(1)}, u32[]{:S(2)}, u32[]{:S(2)}) collective-permute-start(bf16[128,640]{1,0:T(8,128)(2,1)S(1)} %get-tuple-element.41), channel_id=1, source_target_pairs={{0,24},{8,0},{16,8},{24,16},{1,25},{9,1},{17,9},{25,17},{2,26},{10... | collective-permute-start | bytes 491528 | tf_op jit(solution)/shard_map/ppermute | solution.py:333
  74.0 3.9 %collective-permute-done.3 = bf16[128,640]{1,0:T(8,128)(2,1)S(1)} collective-permute-done((bf16[128,640]{1,0:T(8,128)(2,1)S(1)}, bf16[128,640]{1,0:T(8,128)(2,1)S(1)}, u32[]{:S(2)}, u32[]{:S(2)}) %collective-permute-start.3) | collective-permute-done | bytes 163872 | tf_op jit(solution)/shard_map/ppermute | solution.py:333
  77.9 2.4 %collective-permute-done.4 = bf16[128,640]{1,0:T(8,128)(2,1)S(1)} collective-permute-done((bf16[128,640]{1,0:T(8,128)(2,1)S(1)}, bf16[128,640]{1,0:T(8,128)(2,1)S(1)}, u32[]{:S(2)}, u32[]{:S(2)}) %collective-permute-start.4) | collective-permute-done | bytes 163872 | tf_op jit(solution)/shard_map/ppermute | solution.py:333
  80.4 1.3 %collective-permute-start.9 = (bf16[64,640]{1,0:T(8,128)(2,1)S(1)}, bf16[64,640]{1,0:T(8,128)(2,1)S(1)}, u32[]{:S(2)}, u32[]{:S(2)}) collective-permute-start(bf16[64,640]{1,0:T(8,128)(2,1)S(1)} %slice.64), channel_id=1, source_target_pairs={{32,0},{64,32},{96,64},{128,96},{160,128},{192,160},{224,192},{33,... | collective-permute-start | bytes 245768 | tf_op jit(solution)/shard_map/ppermute | solution.py:369
  81.7 15.5 %collective-permute-done.9 = bf16[64,640]{1,0:T(8,128)(2,1)S(1)} collective-permute-done((bf16[64,640]{1,0:T(8,128)(2,1)S(1)}, bf16[64,640]{1,0:T(8,128)(2,1)S(1)}, u32[]{:S(2)}, u32[]{:S(2)}) %collective-permute-start.9) | collective-permute-done | bytes 81952 | tf_op jit(solution)/shard_map/ppermute | solution.py:369
  97.3 2.6 %collective-permute-start.12 = (bf16[64,640]{1,0:T(8,128)(2,1)S(1)}, bf16[64,640]{1,0:T(8,128)(2,1)S(1)}, u32[]{:S(2)}, u32[]{:S(2)}) collective-permute-start(bf16[64,640]{1,0:T(8,128)(2,1)S(1)} %fusion.5.refs_0_), channel_id=1, source_target_pairs={{0,6},{2,0},{4,2},{6,4},{1,7},{3,1},{5,3},{7,5},{8,14},{10,8},{12,... | collective-permute-start | bytes 245768 | tf_op jit(solution)/shard_map/ppermute | solution.py:333
  101.3 3.4 %collective-permute-done.11.refs_2_ = bf16[64,640]{1,0:T(8,128)(2,1)S(1)} collective-permute-done((bf16[64,640]{1,0:T(8,128)(2,1)S(1)}, bf16[64,640]{1,0:T(8,128)(2,1)S(1)}, u32[]{:S(2)}, u32[]{:S(2)}) %collective-permute-start.11) | collective-permute-done | bytes 81952 | tf_op jit(solution)/shard_map/ppermute | solution.py:333
  106.2 2.9 %collective-permute-start.13 = (f32[64,640]{1,0:T(8,128)S(1)}, f32[64,640]{1,0:T(8,128)S(1)}, u32[]{:S(2)}, u32[]{:S(2)}) collective-permute-start(f32[64,640]{1,0:T(8,128)S(1)} %latent.1.mine_ref), channel_id=1, source_target_pairs={{0,1},{1,0},{2,3},{3,2},{4,5},{5,4},{6,7},{7,6},{8,9},{9,8},{10,11... | collective-permute-start | bytes 491528 | tf_op jit(solution)/shard_map/ppermute | solution.py:341
  109.6 2.1 %collective-permute-start.8 = (bf16[128,512]{1,0:T(8,128)(2,1)S(1)}, bf16[128,512]{1,0:T(8,128)(2,1)S(1)}, u32[]{:S(2)}, u32[]{:S(2)}) collective-permute-start(bf16[128,512]{1,0:T(8,128)(2,1)S(1)} %copy-done.5), channel_id=1, source_target_pairs={{0,24},{8,0},{16,8},{24,16},{1,25},{9,1},{17,9},{25,17},{2,26},{10... | collective-permute-start | bytes 393224 | tf_op jit(solution)/shard_map/ppermute | solution.py:333
  112.5 1.7 %collective-permute-start.15 = (bf16[16,1024]{1,0:T(8,128)(2,1)S(1)}, bf16[16,1024]{1,0:T(8,128)(2,1)S(1)}, u32[]{:S(2)}, u32[]{:S(2)}) collective-permute-start(bf16[16,1024]{1,0:T(8,128)(2,1)S(1)} %get-tuple-element.36), channel_id=1, source_target_pairs={{0,16},{8,24},{16,0},{24,8},{1,17},{9,25},{17,1},{25,9},{2,18},{10... | collective-permute-start | bytes 98312 | tf_op jit(solution)/shard_map/ppermute | solution.py:333
  114.3 1.3 %collective-permute-done.7.refs_2_ = bf16[128,512]{1,0:T(8,128)(2,1)S(1)} collective-permute-done((bf16[128,512]{1,0:T(8,128)(2,1)S(1)}, bf16[128,512]{1,0:T(8,128)(2,1)S(1)}, u32[]{:S(2)}, u32[]{:S(2)}) %collective-permute-start.7) | collective-permute-done | bytes 131104 | tf_op jit(solution)/shard_map/ppermute | solution.py:333
  115.6 0.9 collective-permute-start.16
  116.9 1.4 %attended.1 = bf16[128,2048]{1,0:T(8,128)(2,1)} custom-call(s32[4]{0:T(128)S(1)} %pad_add_fusion.where_ref, bf16[128,512]{1,0:T(8,128)(2,1)S(1)} %copy-done.1, bf16[128,512]{1,0:T(8,128)(2,1)S(1)} %collective-permute-done.6.refs_1_, bf16[128,512]{1,0:T(8,128)(2,1)S(1)} %collective-permute-done.7.refs_2_, bf16[128,512]{1,0:T(8,128)(2,1)S(1)} %collective-permute-done.8.refs_3_), custom_call_target="tpu_custom_call" | custom-call | tf_op jit(solution)/shard_map/attended/pallas_call | solution.py:273
  118.3 1.4 %join.1 = f32[576,128]{1,0:T(8,128)} custom-call(s32[4]{0:T(128)S(1)} %pad_add_fusion.where_ref, f32[64,640]{1,0:T(8,128)S(1)} %latent.1.mine_ref, f32[64,640]{1,0:T(8,128)S(1)} %collective-permute-done.13.other_ref), custom_call_target="tpu_custom_call" | custom-call | tf_op jit(solution)/shard_map/join/pallas_call | solution.py:253
  119.7 1.3 %weight.1 = (f32[16,2048]{1,0:T(8,128)}, f32[16,2048]{1,0:T(8,128)}) custom-call(s32[4]{0:T(128)S(1)} %pad_add_fusion.where_ref, bf16[16,1024]{1,0:T(8,128)(2,1)S(1)} %get-tuple-element.34.refs_0_, bf16[16,1024]{1,0:T(8,128)(2,1)S(1)} %collective-permute-done.14.refs_1_, bf16[16,1024]{1,0:T(8,128)(2,1)S(1)} %collective-permute-done.15.refs_2_, ...), custom_call_target="tpu_custom_call" | custom-call | tf_op jit(solution)/shard_map/weight/pallas_call | solution.py:318
  (49 shorter events, 7.3 us)
Async XLA Ops:
  2.0 5.8 %collective-permute-start = (bf16[64,640]{1,0:T(8,128)(2,1)S(1)}, bf16[64,640]{1,0:T(8,128)(2,1)S(1)}, u32[]{:S(2)}, u32[]{:S(2)}) collective-permute-start(bf16[64,640]{1,0:T(8,128)(2,1)S(1)} %maximum_maximum_fusion.own_ref), channel_id=1, source_target_pairs={{0,32},{32,64},{64,96},{96,128},{128,160},{160,192},{192,224},{1,3... | collective-permute-start | bytes 245768 | tf_op jit(solution)/shard_map/ppermute | solution.py:356
  38.9 4.6 %copy-start.2 = (bf16[4,384,640]{2,1,0:T(8,128)(2,1)}, bf16[4,384,640]{2,1,0:T(8,128)(2,1)S(1)}, u32[]{:S(2)}) copy-start(bf16[4,384,640]{2,1,0:T(8,128)(2,1)S(1)} %all_to_all.10.x_ref.mine_ref) | copy-start | bytes 5898244
  38.9 4.5 %collective-permute-start.1 = (bf16[4,128,640]{2,1,0:T(8,128)(2,1)S(1)}, bf16[4,128,640]{2,1,0:T(8,128)(2,1)S(1)}, u32[]{:S(2)}, u32[]{:S(2)}) collective-permute-start(bf16[4,128,640]{2,1,0:T(8,128)(2,1)S(1)} %slice.45), channel_id=1, source_target_pairs={{0,1},{1,0},{2,3},{3,2},{4,5},{5,4},{6,7},{7,6},{8,9},{9,8},{10,11... | collective-permute-start | bytes 1966088 | tf_op jit(solution)/shard_map/ppermute | solution.py:341
  60.9 10.2 %copy-start.3 = (bf16[4,128,640]{2,1,0:T(8,128)(2,1)S(1)}, bf16[4,128,640]{2,1,0:T(8,128)(2,1)}, u32[]{:S(2)}) copy-start(bf16[4,128,640]{2,1,0:T(8,128)(2,1)} %get-tuple-element.22) | copy-start | bytes 1966084
  60.9 10.2 %collective-permute-start.2 = (bf16[4,128,640]{2,1,0:T(8,128)(2,1)}, bf16[4,128,640]{2,1,0:T(8,128)(2,1)S(1)}, u32[]{:S(2)}, u32[]{:S(2)}) collective-permute-start(bf16[4,128,640]{2,1,0:T(8,128)(2,1)} %get-tuple-element.23), channel_id=1, source_target_pairs={{0,1},{1,0},{2,3},{3,2},{4,5},{5,4},{6,7},{7,6},{8,9},{9,8},{10,11... | collective-permute-start | bytes 1966088 | tf_op jit(solution)/shard_map/ppermute | solution.py:341
  61.4 39.6 %copy-start.7 = (bf16[128,512]{1,0:T(8,128)(2,1)S(1)}, bf16[128,512]{1,0:T(8,128)(2,1)}, u32[]{:S(2)}) copy-start(bf16[128,512]{1,0:T(8,128)(2,1)} %get-tuple-element.29) | copy-start | bytes 393220
  61.4 50.3 %all-to-all-start.1 = ((bf16[8,64,1024]{2,1,0:T(8,128)(2,1)}), bf16[8,64,1024]{2,1,0:T(8,128)(2,1)S(1)}, u32[]{:S(2)}, u32[]{:S(2)}) async-start(bf16[8,64,1024]{2,1,0:T(8,128)(2,1)} %bitcast.20), calls=%async_computation.1 | async-start | bytes 2097152 | tf_op jit(solution)/shard_map/all_to_all | solution.py:329
  71.1 37.9 %copy-start.6 = (bf16[128,512]{1,0:T(8,128)(2,1)S(1)}, bf16[128,512]{1,0:T(8,128)(2,1)}, u32[]{:S(2)}) copy-start(bf16[128,512]{1,0:T(8,128)(2,1)} %get-tuple-element.30) | copy-start | bytes 393220
  71.1 38.5 %copy-start.5 = (bf16[128,512]{1,0:T(8,128)(2,1)S(1)}, bf16[128,512]{1,0:T(8,128)(2,1)}, u32[]{:S(2)}) copy-start(bf16[128,512]{1,0:T(8,128)(2,1)} %get-tuple-element.31) | copy-start | bytes 393220
  71.1 45.8 %copy-start.1 = (bf16[128,512]{1,0:T(8,128)(2,1)S(1)}, bf16[128,512]{1,0:T(8,128)(2,1)}, u32[]{:S(2)}) copy-start(bf16[128,512]{1,0:T(8,128)(2,1)} %get-tuple-element.28.refs_0_) | copy-start | bytes 393220
  71.3 6.6 %collective-permute-start.3 = (bf16[128,640]{1,0:T(8,128)(2,1)S(1)}, bf16[128,640]{1,0:T(8,128)(2,1)S(1)}, u32[]{:S(2)}, u32[]{:S(2)}) collective-permute-start(bf16[128,640]{1,0:T(8,128)(2,1)S(1)} %get-tuple-element.40), channel_id=1, source_target_pairs={{0,8},{8,16},{16,24},{24,0},{1,9},{9,17},{17,25},{25,1},{2,10},{10... | collective-permute-start | bytes 491528 | tf_op jit(solution)/shard_map/ppermute | solution.py:333
  71.6 6.3 %collective-permute-start.5 = (bf16[128,640]{1,0:T(8,128)(2,1)S(1)}, bf16[128,640]{1,0:T(8,128)(2,1)S(1)}, u32[]{:S(2)}, u32[]{:S(2)}) collective-permute-start(bf16[128,640]{1,0:T(8,128)(2,1)S(1)} %get-tuple-element.41), channel_id=1, source_target_pairs={{0,24},{8,0},{16,8},{24,16},{1,25},{9,1},{17,9},{25,17},{2,26},{10... | collective-permute-start | bytes 491528 | tf_op jit(solution)/shard_map/ppermute | solution.py:333
  74.0 6.3 %collective-permute-start.4 = (bf16[128,640]{1,0:T(8,128)(2,1)S(1)}, bf16[128,640]{1,0:T(8,128)(2,1)S(1)}, u32[]{:S(2)}, u32[]{:S(2)}) collective-permute-start(bf16[128,640]{1,0:T(8,128)(2,1)S(1)} %get-tuple-element.42), channel_id=1, source_target_pairs={{0,16},{8,24},{16,0},{24,8},{1,17},{9,25},{17,1},{25,9},{2,18},{10... | collective-permute-start | bytes 491528 | tf_op jit(solution)/shard_map/ppermute | solution.py:333
  80.4 16.8 %collective-permute-start.9 = (bf16[64,640]{1,0:T(8,128)(2,1)S(1)}, bf16[64,640]{1,0:T(8,128)(2,1)S(1)}, u32[]{:S(2)}, u32[]{:S(2)}) collective-permute-start(bf16[64,640]{1,0:T(8,128)(2,1)S(1)} %slice.64), channel_id=1, source_target_pairs={{32,0},{64,32},{96,64},{128,96},{160,128},{192,160},{224,192},{33,... | collective-permute-start | bytes 245768 | tf_op jit(solution)/shard_map/ppermute | solution.py:369
  97.3 4.1 %collective-permute-start.12 = (bf16[64,640]{1,0:T(8,128)(2,1)S(1)}, bf16[64,640]{1,0:T(8,128)(2,1)S(1)}, u32[]{:S(2)}, u32[]{:S(2)}) collective-permute-start(bf16[64,640]{1,0:T(8,128)(2,1)S(1)} %fusion.5.refs_0_), channel_id=1, source_target_pairs={{0,6},{2,0},{4,2},{6,4},{1,7},{3,1},{5,3},{7,5},{8,14},{10,8},{12,... | collective-permute-start | bytes 245768 | tf_op jit(solution)/shard_map/ppermute | solution.py:333
  99.9 4.9 %collective-permute-start.11 = (bf16[64,640]{1,0:T(8,128)(2,1)S(1)}, bf16[64,640]{1,0:T(8,128)(2,1)S(1)}, u32[]{:S(2)}, u32[]{:S(2)}) collective-permute-start(bf16[64,640]{1,0:T(8,128)(2,1)S(1)} %fusion.5.refs_0_), channel_id=1, source_target_pairs={{0,4},{2,6},{4,0},{6,2},{1,5},{3,7},{5,1},{7,3},{8,12},{10,14},{12... | collective-permute-start | bytes 245768 | tf_op jit(solution)/shard_map/ppermute | solution.py:333
  100.4 5.1 %collective-permute-start.10 = (bf16[64,640]{1,0:T(8,128)(2,1)S(1)}, bf16[64,640]{1,0:T(8,128)(2,1)S(1)}, u32[]{:S(2)}, u32[]{:S(2)}) collective-permute-start(bf16[64,640]{1,0:T(8,128)(2,1)S(1)} %fusion.5.refs_0_), channel_id=1, source_target_pairs={{0,2},{2,4},{4,6},{6,0},{1,3},{3,5},{5,7},{7,1},{8,10},{10,12},{12... | collective-permute-start | bytes 245768 | tf_op jit(solution)/shard_map/ppermute | solution.py:333
  101.0 11.5 %collective-permute-start.6 = (bf16[128,512]{1,0:T(8,128)(2,1)S(1)}, bf16[128,512]{1,0:T(8,128)(2,1)S(1)}, u32[]{:S(2)}, u32[]{:S(2)}) collective-permute-start(bf16[128,512]{1,0:T(8,128)(2,1)S(1)} %copy-done.7), channel_id=1, source_target_pairs={{0,8},{8,16},{16,24},{24,0},{1,9},{9,17},{17,25},{25,1},{2,10},{10... | collective-permute-start | bytes 393224 | tf_op jit(solution)/shard_map/ppermute | solution.py:333
  106.2 12.1 %collective-permute-start.13 = (f32[64,640]{1,0:T(8,128)S(1)}, f32[64,640]{1,0:T(8,128)S(1)}, u32[]{:S(2)}, u32[]{:S(2)}) collective-permute-start(f32[64,640]{1,0:T(8,128)S(1)} %latent.1.mine_ref), channel_id=1, source_target_pairs={{0,1},{1,0},{2,3},{3,2},{4,5},{5,4},{6,7},{7,6},{8,9},{9,8},{10,11... | collective-permute-start | bytes 491528 | tf_op jit(solution)/shard_map/ppermute | solution.py:341
  109.0 6.6 %collective-permute-start.7 = (bf16[128,512]{1,0:T(8,128)(2,1)S(1)}, bf16[128,512]{1,0:T(8,128)(2,1)S(1)}, u32[]{:S(2)}, u32[]{:S(2)}) collective-permute-start(bf16[128,512]{1,0:T(8,128)(2,1)S(1)} %copy-done.6), channel_id=1, source_target_pairs={{0,16},{8,24},{16,0},{24,8},{1,17},{9,25},{17,1},{25,9},{2,18},{10... | collective-permute-start | bytes 393224 | tf_op jit(solution)/shard_map/ppermute | solution.py:333
  109.6 7.3 %collective-permute-start.8 = (bf16[128,512]{1,0:T(8,128)(2,1)S(1)}, bf16[128,512]{1,0:T(8,128)(2,1)S(1)}, u32[]{:S(2)}, u32[]{:S(2)}) collective-permute-start(bf16[128,512]{1,0:T(8,128)(2,1)S(1)} %copy-done.5), channel_id=1, source_target_pairs={{0,24},{8,0},{16,8},{24,16},{1,25},{9,1},{17,9},{25,17},{2,26},{10... | collective-permute-start | bytes 393224 | tf_op jit(solution)/shard_map/ppermute | solution.py:333
  112.4 7.3 %collective-permute-start.14 = (bf16[16,1024]{1,0:T(8,128)(2,1)S(1)}, bf16[16,1024]{1,0:T(8,128)(2,1)S(1)}, u32[]{:S(2)}, u32[]{:S(2)}) collective-permute-start(bf16[16,1024]{1,0:T(8,128)(2,1)S(1)} %get-tuple-element.35), channel_id=1, source_target_pairs={{0,8},{8,16},{16,24},{24,0},{1,9},{9,17},{17,25},{25,1},{2,10},{10... | collective-permute-start | bytes 98312 | tf_op jit(solution)/shard_map/ppermute | solution.py:333
  112.5 7.2 %collective-permute-start.15 = (bf16[16,1024]{1,0:T(8,128)(2,1)S(1)}, bf16[16,1024]{1,0:T(8,128)(2,1)S(1)}, u32[]{:S(2)}, u32[]{:S(2)}) collective-permute-start(bf16[16,1024]{1,0:T(8,128)(2,1)S(1)} %get-tuple-element.36), channel_id=1, source_target_pairs={{0,16},{8,24},{16,0},{24,8},{1,17},{9,25},{17,1},{25,9},{2,18},{10... | collective-permute-start | bytes 98312 | tf_op jit(solution)/shard_map/ppermute | solution.py:333
  115.6 4.1 %collective-permute-start.16 = (bf16[16,1024]{1,0:T(8,128)(2,1)S(1)}, bf16[16,1024]{1,0:T(8,128)(2,1)S(1)}, u32[]{:S(2)}, u32[]{:S(2)}) collective-permute-start(bf16[16,1024]{1,0:T(8,128)(2,1)S(1)} %get-tuple-element.37), channel_id=1, source_target_pairs={{0,24},{8,0},{16,8},{24,16},{1,25},{9,1},{17,9},{25,17},{2,26},{10... | collective-permute-start | bytes 98312 | tf_op jit(solution)/shard_map/ppermute | solution.py:333
  (2 other events, 1.8 us)

commit v5 on v3

--- a/solution.py
+++ b/solution.py
@@ -40,52 +40,67 @@
     return lax.dot_general(a, b, (((0,), (0,)), ((), ())), preferred_element_type=F32)
 
 
-def pack_kernel(where_ref, q_ref, g_ref, *piece_refs):
+def in_hbm(x):
+    return pltpu.with_memory_space_constraint(x, pltpu.HBM)
+
+
+def pack_kernel(where_ref, q_ref, g_ref, *refs):
+    piece_refs, sems = refs[:8], refs[8]
     y = where_ref[1]
-    for k in range(4):
-        to = (y + k) & 3
-        for pair in range(2):
+    copies = []
+    for pair in range(2):
+        for k in range(4):
+            to = (y + k) & 3
             piece = piece_refs[4 * pair + k]
-            piece[:, :384] = q_ref[:, pl.ds(pl.multiple_of(to * 768 + pair * 384, 128), 384)]
-            piece[:, 384:] = g_ref[:, pl.ds(pl.multiple_of(to * 512 + pair * 256, 128), 256)]
+            from_q = q_ref.at[:, pl.ds(pl.multiple_of(to * 768 + pair * 384, 128), 384)]
+            from_g = g_ref.at[:, pl.ds(pl.multiple_of(to * 512 + pair * 256, 128), 256)]
+            at = 8 * pair + 2 * k
+            copies.append(pltpu.make_async_copy(from_q, piece.at[:, :384], sems.at[at]))
+            copies.append(pltpu.make_async_copy(from_g, piece.at[:, 384:], sems.at[at + 1]))
+    for copy in copies:
+        copy.start()
+    for copy in copies:
+        copy.wait()
 
 
 def pack_call(place, queries, out_grad):
-    vmem = pl.BlockSpec(memory_space=pltpu.VMEM)
+    hbm = pl.BlockSpec(memory_space=pltpu.HBM)
     return pl.pallas_call(
         pack_kernel,
-        in_specs=[pl.BlockSpec(memory_space=pltpu.SMEM), vmem, vmem],
-        out_specs=[vmem] * 8,
-        out_shape=[jax.ShapeDtypeStruct((TOK, PAY), BF16)] * 8,
+        in_specs=[pl.BlockSpec(memory_space=pltpu.SMEM), hbm, hbm],
+        out_specs=[hbm] * 8,
+        out_shape=[pltpu.HBM((TOK, PAY), BF16)] * 8,
+        scratch_shapes=[pltpu.SemaphoreType.DMA((16,))],
         cost_estimate=pl.CostEstimate(flops=0, bytes_accessed=2_600_000, transcendentals=0),
         compiler_params=SMALL,
         name="pack",
-    )(place, queries, out_grad)
+    )(place, in_hbm(queries), in_hbm(out_grad))
 
 
 def pair_kernel(first, where_ref, *refs):
     pieces, refs = refs[:4], refs[4:]
-    mine_refs, other_refs, refs = refs[:4], refs[4:8], refs[8:]
-    wk_ref, wv_ref, refs = refs[0], refs[1], refs[2:]
     if first:
-        before_ref, refs = None, refs
-        (dl_ref,), outs = refs[:1], refs[1:]
+        mine_refs, other_refs, refs = refs[:4], refs[4:8], refs[8:]
+        wk_ref, wv_ref, l_ref, dl_ref, attended, grads = refs[:6]
     else:
-        before_ref, refs = refs[0], refs[1:]
-        keep_ref, send_ref, outs = refs[0], refs[1], refs[2:]
-    out_refs, dw_ref = outs[:4], outs[4]
-    x_ref, l_ref, kcat, vals, bias, dk_acc, dv_acc, grads, attended, dl_acc = outs[5:]
+        l_ref, wk_ref, wv_ref, before_ref, early_ref, refs = *refs[:5], refs[5:]
+        keep_ref, send_ref, out_refs, grads, refs = refs[0], refs[1], refs[2:6], refs[6], refs[7:]
+        attended, dl_acc = refs[-2:]
+    x_ref, kcat, vals, bias, dk_acc, dv_acc = refs[6:12] if first else refs[:6]
     group, y, core = where_ref[0], where_ref[1], where_ref[2]
     half = TOK // 2
     for k in range(4):
         block = (y - k) & 3
         x_ref[pl.ds(pl.multiple_of(block * TOK, TOK), TOK), :] = pieces[k][...]
         for back in range(2):
+            if not first:
+                continue
             row = (1 - back) * ROWS + block * TOK
+            piece = slice((1 - back) * half, (2 - back) * half)
             own = pl.multiple_of(row + core * half, half)
-            l_ref[pl.ds(own, half), :] = mine_refs[k][(1 - back) * half : (2 - back) * half]
+            l_ref[pl.ds(own, half), :] = mine_refs[k][piece]
             swapped = pl.multiple_of(row + (1 - core) * half, half)
-            l_ref[pl.ds(swapped, half), :] = other_refs[k][(1 - back) * half : (2 - back) * half]
+            l_ref[pl.ds(swapped, half), :] = other_refs[k][piece]
     lat = l_ref[:, :LATENT]
     tail = l_ref[:, LATENT:].astype(F32)
     lane = lax.broadcasted_iota(jnp.int32, (KEYS, 128), 1)
@@ -145,9 +160,11 @@
                 dk_acc[h, SPAN:, :] = dk[ROWS:]
                 dv_acc[SPAN:, :] = dv[ROWS:]
         grads[:, 256 + h * VDIM : 256 + (h + 1) * VDIM] = dv_acc[...].astype(BF16)
-    for k in range(4):
-        to = pl.multiple_of(((y + k) & 3) * TOK, TOK)
-        out_refs[k][...] = attended[pl.ds(to, TOK), :]
+    if not first:
+        for k in range(4):
+            to = pl.multiple_of(((y + k) & 3) * TOK, TOK)
+            out_refs[k][:, :256] = early_ref[pl.ds(to, TOK), :]
+            out_refs[k][:, 256:] = attended[pl.ds(to, TOK), :]
     grads[:, :NOPE] = dk_acc[0, :, :NOPE].astype(BF16)
     mixed = jnp.where(low, dk_acc[1, :, NOPE:], dk_acc[1, :, :NOPE])
     grads[:, NOPE : 2 * NOPE] = pltpu.roll(mixed, ROPE, 1).astype(BF16)
@@ -167,30 +184,34 @@
                 keep_ref[k, back * half : (back + 1) * half, :] = dl_acc[pl.ds(own, half), :]
                 swapped = pl.multiple_of(row + (1 - core) * half, half)
                 send_ref[k, back * half : (back + 1) * half, :] = dl_acc[pl.ds(swapped, half), :]
-    dw_ref[...] = tn(lat, grads[...]).astype(BF16)
-
-
-def in_hbm(x):
-    return pltpu.with_memory_space_constraint(x, pltpu.HBM)
-
-
-def pair_call(pair, place, pieces, mine, other, key_weight, value_weight, before):
-    first = before is None
+
+
+def pair_call(pair, place, pieces, lats, key_weight, value_weight, before):
+    first = pair == 0
 
     def whole(*shape):
         return pl.BlockSpec(shape, lambda i, w: (0,) * len(shape))
 
     weight_spec = pl.BlockSpec((LATENT, 256), lambda i, w: (0, 2 * w[1] + pair))
-    in_specs = [whole(TOK, PAY)] * 12 + [weight_spec] * 2
-    args = [in_hbm(x) for x in (*pieces, *mine, *other, key_weight, value_weight)]
+    args = [*pieces, *lats]
+    in_specs = [whole(*arg.shape) for arg in args] + [weight_spec] * 2
+    in_specs += [whole(*arg.shape) for arg in before]
+    scratch = [
+        pltpu.VMEM((ROWS, PAY), BF16),
+        pltpu.VMEM((2, KEYS, 256), BF16),
+        pltpu.VMEM((KEYS, 256), BF16),
+        pltpu.VMEM((2, SPAN, TILE), F32),
+        pltpu.VMEM((2, KEYS, 256), F32),
+        pltpu.VMEM((KEYS, VDIM), F32),
+    ]
+    grads = pltpu.HBM((KEYS, 512), BF16)
     if first:
-        dl_shapes = [pltpu.HBM((KEYS, PAY), BF16)]
+        out_shape = [pltpu.HBM((KEYS, PAY), BF16)] * 2 + [pltpu.HBM((ROWS, 256), BF16), grads]
     else:
-        in_specs.append(whole(KEYS, PAY))
-        args.append(before)
-        dl_shapes = [jax.ShapeDtypeStruct((4, TOK, PAY), BF16)] * 2
-    out_shape = dl_shapes + [pltpu.HBM((TOK, 256), BF16)] * 4
-    out_shape.append(pltpu.HBM((LATENT, 512), BF16))
+        out_shape = [pltpu.HBM((4, TOK, PAY), BF16)] * 2
+        out_shape += [pltpu.HBM((TOK, 512), BF16)] * 4 + [grads]
+        scratch += [pltpu.VMEM((ROWS, 256), BF16), pltpu.VMEM((KEYS, PAY), BF16)]
+    args += [in_hbm(arg) for arg in (key_weight, value_weight, *before)]
     return pl.pallas_call(
         functools.partial(pair_kernel, first),
         grid_spec=pltpu.PrefetchScalarGridSpec(
@@ -198,18 +219,7 @@
             grid=(1,),
             in_specs=in_specs,
             out_specs=[whole(*leaf.shape) for leaf in out_shape],
-            scratch_shapes=[
-                pltpu.VMEM((ROWS, PAY), BF16),
-                pltpu.VMEM((KEYS, PAY), BF16),
-                pltpu.VMEM((2, KEYS, 256), BF16),
-                pltpu.VMEM((KEYS, 256), BF16),
-                pltpu.VMEM((2, SPAN, TILE), F32),
-                pltpu.VMEM((2, KEYS, 256), F32),
-                pltpu.VMEM((KEYS, VDIM), F32),
-                pltpu.VMEM((KEYS, 512), BF16),
-                pltpu.VMEM((ROWS, 256), BF16),
-                pltpu.VMEM((KEYS, PAY), BF16),
-            ],
+            scratch_shapes=scratch,
         ),
         out_shape=out_shape,
         compiler_params=pltpu.CompilerParams(vmem_limit_bytes=40 << 20),
@@ -220,12 +230,35 @@
     )(place, *args)
 
 
+def grad_kernel(l_ref, first_ref, second_ref, out_ref):
+    lat_t = jnp.transpose(l_ref[:, :LATENT])
+    out_ref[:, :512] = nn(lat_t, first_ref[...]).astype(BF16)
+    out_ref[:, 512:] = nn(lat_t, second_ref[...]).astype(BF16)
+
+
+def grad_call(lat, first, second):
+    vmem = pl.BlockSpec(memory_space=pltpu.VMEM)
+    return pl.pallas_call(
+        grad_kernel,
+        in_specs=[vmem] * 3,
+        out_specs=vmem,
+        out_shape=pltpu.HBM((LATENT, 1024), BF16),
+        compiler_params=pltpu.CompilerParams(vmem_limit_bytes=20 << 20),
+        cost_estimate=pl.CostEstimate(
+            flops=1_100_000_000, bytes_accessed=4_400_000, transcendentals=0
+        ),
+        name="grad",
+    )(in_hbm(lat), in_hbm(first), in_hbm(second))
+
+
 def latent_kernel(where_ref, *refs):
-    terms, out_ref, held = refs[:4], refs[4], refs[5]
+    terms, own_ref, later_ref, held = refs[:4], refs[4], refs[5], refs[6]
     x = where_ref[3]
     for k in range(4):
         held[(x - k) & 3] = terms[k][...].astype(F32)
-    out_ref[...] = (held[0] + held[1]) + (held[2] + held[3])
+    total = (held[0] + held[1]) + (held[2] + held[3])
+    own_ref[...] = total[: TOK // 2]
+    later_ref[...] = total[TOK // 2 :].astype(BF16)
 
 
 def latent_call(place, terms):
@@ -233,9 +266,12 @@
     return pl.pallas_call(
         latent_kernel,
         in_specs=[pl.BlockSpec(memory_space=pltpu.SMEM)] + [vmem] * 4,
-        out_specs=vmem,
-        out_shape=jax.ShapeDtypeStruct((TOK // 2, PAY), F32),
-        scratch_shapes=[pltpu.VMEM((4, TOK // 2, PAY), F32)],
+        out_specs=[vmem] * 2,
+        out_shape=[
+            jax.ShapeDtypeStruct((TOK // 2, PAY), F32),
+            jax.ShapeDtypeStruct((TOK // 2, PAY), BF16),
+        ],
+        scratch_shapes=[pltpu.VMEM((4, TOK, PAY), F32)],
         compiler_params=SMALL,
         name="latent",
     )(place, *terms)
@@ -263,19 +299,18 @@
 
 
 def attended_kernel(where_ref, *refs):
-    pieces, out_ref = refs[:8], refs[8]
+    pieces, out_ref = refs[:4], refs[4]
     y = where_ref[1]
-    for pair in range(2):
-        for k in range(4):
-            column = pl.multiple_of(((y - k) & 3) * 512 + pair * 256, 128)
-            out_ref[:, pl.ds(column, 256)] = pieces[4 * pair + k][...]
+    for k in range(4):
+        column = pl.multiple_of(((y - k) & 3) * 512, 512)
+        out_ref[:, pl.ds(column, 512)] = pieces[k][...]
 
 
 def attended_call(place, pieces):
     vmem = pl.BlockSpec(memory_space=pltpu.VMEM)
     return pl.pallas_call(
         attended_kernel,
-        in_specs=[pl.BlockSpec(memory_space=pltpu.SMEM)] + [vmem] * 8,
+        in_specs=[pl.BlockSpec(memory_space=pltpu.SMEM)] + [vmem] * 4,
         out_specs=vmem,
         out_shape=jax.ShapeDtypeStruct((TOK, 2048), BF16),
         compiler_params=SMALL,
@@ -299,39 +334,33 @@
         half_kernel,
         in_specs=[pl.BlockSpec(memory_space=pltpu.SMEM), vmem],
         out_specs=[vmem] * 4,
-        out_shape=[jax.ShapeDtypeStruct((16, 512), BF16)] * 4,
+        out_shape=[jax.ShapeDtypeStruct((16, 1024), BF16)] * 4,
         compiler_params=SMALL,
         name="half",
     )(place, sent)
 
 
 def weight_kernel(where_ref, *refs):
-    pieces, second_ref, key_ref, value_ref = refs[:4], refs[4], refs[5], refs[6]
-    here = where_ref[1]
+    pieces, key_ref, value_ref = refs[:4], refs[4], refs[5]
+    y = where_ref[1]
     for k in range(4):
-        column = pl.multiple_of(((here - k) & 3) * 512, 512)
-        total = pieces[k][...].astype(F32)
-        key_ref[:, pl.ds(column, 256)] = total[:, :256]
-        value_ref[:, pl.ds(column, 256)] = total[:, 256:]
-    for y in range(4):
-        total = second_ref[y].astype(F32)
-        for z in range(1, GROUPS):
-            total = total + second_ref[4 * z + y].astype(F32)
-        column = y * 512 + 256
-        key_ref[:, column : column + 256] = total[:, :256]
-        value_ref[:, column : column + 256] = total[:, 256:]
-
-
-def weight_call(place, pieces, second):
+        column = ((y - k) & 3) * 512
+        for pair in range(2):
+            here = pl.ds(pl.multiple_of(column + pair * 256, 256), 256)
+            key_ref[:, here] = pieces[k][:, pair * 512 : pair * 512 + 256].astype(F32)
+            value_ref[:, here] = pieces[k][:, pair * 512 + 256 : pair * 512 + 512].astype(F32)
+
+
+def weight_call(place, pieces):
     vmem = pl.BlockSpec(memory_space=pltpu.VMEM)
     return pl.pallas_call(
         weight_kernel,
-        in_specs=[pl.BlockSpec(memory_space=pltpu.SMEM)] + [vmem] * 5,
+        in_specs=[pl.BlockSpec(memory_space=pltpu.SMEM)] + [vmem] * 4,
         out_specs=[vmem] * 2,
         out_shape=[jax.ShapeDtypeStruct((16, 2048), F32)] * 2,
         compiler_params=SMALL,
         name="weight",
-    )(place, *pieces, second)
+    )(place, *pieces)
 
 
 def exchanged(x, axes):
@@ -369,26 +398,25 @@
     other = [swapped(piece) for piece in mine]
     x0, x1 = fanned(pieces[:4], "y"), fanned(pieces[4:], "y")
 
-    dl, *outs0, dw0 = pair_call(0, place, x0, mine, other, key_weight, value_weight, None)
-    dw0 = half_call(place, exchanged(dw0.reshape(8, 64, 512), "z"))
-    keep, send, *outs1, dw1 = pair_call(
-        1, place, x1, mine, other, key_weight, value_weight, dl
-    )
-    dw1 = exchanged(dw1.reshape(32, 16, 512), ("z", "y"))
+    lat, dl, early, g0 = pair_call(0, place, x0, mine + other, key_weight, value_weight, [])
+    keep, send, *outs, g1 = pair_call(1, place, x1, [lat], key_weight, value_weight, [dl, early])
 
     came = swapped(send)
     both = [keep[k].astype(F32) + came[k].astype(F32) for k in range(4)]
-    parts = fanned([both[0]] + [part.astype(BF16) for part in both[1:]], "y")
+    both = [both[0]] + [part.astype(BF16) for part in both[1:]]
+    both, g1 = lax.optimization_barrier((both, g1))
+    parts = fanned(both, "y")
+    dw = exchanged(grad_call(lat, g0, g1).reshape(8, 64, 1024), "z")
+    dw = half_call(place, dw)
     total = parts[0]
     for part in parts[1:]:
         total = total + part.astype(F32)
-    later = lax.ppermute(total[half:].astype(BF16), "z", behind)
-    later, dw0, outs0, outs1 = lax.optimization_barrier((later, dw0, outs0, outs1))
-    own = (total[:half] + later.astype(F32)).astype(BF16)
-    part = latent_call(place, fanned([own] * 4, "x"))
+    own, later = latent_call(place, fanned([total.astype(BF16)] * 4, "x"))
+    later, outs = lax.optimization_barrier((later, outs))
+    part = own + lax.ppermute(later, "z", behind).astype(F32)
     latent_grad = jnp.transpose(join_call(place, part, swapped(part)))
-    attended = attended_call(place, fanned(outs0, "y") + fanned(outs1, "y"))
-    key_grad, value_grad = weight_call(place, fanned(dw0, "y"), dw1)
+    attended = attended_call(place, fanned(outs, "y"))
+    key_grad, value_grad = weight_call(place, fanned(dw, "y"))
     return attended, latent_grad, key_grad, value_grad
 
 

time: 125 us -> 154 us (1.23); the launches traced: 122 us -> 154 us
  Pallas kernels: 24.6 us -> 68.9 us
  starting transfers between devices: 63.6 us -> 53.9 us
  local copies, waits for them, and re-layouts: 5.99 us -> 2.64 us
    pallas_call x1, Pallas kernels: 0.69 us -> 41.5 us  [pack_call(): pl.pallas_call(pack_kernel, in_specs=[pl.BlockSpec(memory_space=pltpu.SME...]
    all_to_all x2 -> x1, starting transfers between devices: 14.6 us -> 7.43 us  [exchanged(): return lax.all_to_all(x, axes, split_axis=0, concat_axis=0, tiled=True)]
    pallas_call x0 -> x1, Pallas kernels: none -> 4.21 us  [grad_call(): pl.pallas_call(grad_kernel, in_specs=[vmem] * 3, out_specs=vmem, out_shap...]
    unnamed x57 -> x17, local copies, waits for them, and re-layouts: 5.75 us -> 2.42 us
    ppermute x6, starting transfers between devices: 15.7 us -> 13.2 us  [swapped(): return lax.ppermute(value, 'core', [(0, 1), (1, 0)])]
    ppermute x6, waiting for transfers between devices: 0.02 us -> 1.95 us  [swapped(): return lax.ppermute(value, 'core', [(0, 1), (1, 0)])]
    ppermute x24 -> x21, waiting for transfers between devices: 22.4 us -> 20.9 us  [moved(): lax.ppermute(value, along, [(i, (i + step) % size) for i in range(size)])]
    ppermute x24 -> x21, starting transfers between devices: 27.6 us -> 27.6 us  [moved(): lax.ppermute(value, along, [(i, (i + step) % size) for i in range(size)])]
  transfers between devices with their start and end apart: 34 -> 30, of which waited for: 14 -> 12; matrix products, arithmetic and copies ran while one was open for 0% -> 0% of each run, Pallas kernels for 19% -> 35%
where the time goes in v5:
time: 154 us
  Pallas kernels  68.9 us (45%)
  starting transfers between devices  53.9 us (35%)
  waiting for transfers between devices  25 us (16%)
  local copies, waits for them, and re-layouts  2.64 us (2%)
  other arithmetic  2.48 us (2%)
    pallas_call x1, Pallas kernels, pack_call(): pl.pallas_call(pack_kernel, in_specs=[pl.BlockSpec(memory_space=pltpu.SME...  41.5 us
    ppermute x21, starting transfers between devices, moved(): lax.ppermute(value, along, [(i, (i + step) % size) for i in range(size)])  27.6 us
    ppermute x21, waiting for transfers between devices, moved(): lax.ppermute(value, along, [(i, (i + step) % size) for i in range(size)])  20.9 us
    pallas_call x2, Pallas kernels, pair_call(): pl.pallas_call(functools.partial(pair_kernel, first), grid_spec=pltpu.Pre...  17.7 us
    ppermute x6, starting transfers between devices, swapped(): return lax.ppermute(value, 'core', [(0, 1), (1, 0)])  13.2 us
    all_to_all x1, starting transfers between devices, exchanged(): return lax.all_to_all(x, axes, split_axis=0, concat_axis=0, tiled=True)  7.43 us
    ppermute x1, starting transfers between devices, per_device(): earlier = lax.ppermute(pay, 'z', ahead)  4.38 us
    pallas_call x1, Pallas kernels, grad_call(): pl.pallas_call(grad_kernel, in_specs=[vmem] * 3, out_specs=vmem, out_shap...  4.21 us
  transfers between devices with their start and end apart: 30, of which 12 were waited for; matrix products, arithmetic and copies ran while one was open for 0% of the time, Pallas kernels for 35%

profile of v5, /device:TPU:1, one launch (start us, length us, event | category | flops | bytes accessed | tf_op | source)
XLA Modules:
  0.0 153.7 jit_solution(16426618149853884201)
XLA Ops:
  1.9 4.4 %collective-permute-start.6 = (bf16[64,640]{1,0:T(8,128)(2,1)S(1)}, bf16[64,640]{1,0:T(8,128)(2,1)S(1)}, u32[]{:S(2)}, u32[]{:S(2)}) collective-permute-start(bf16[64,640]{1,0:T(8,128)(2,1)S(1)} %pad_maximum_fusion), channel_id=1, source_target_pairs={{0,32},{32,64},{64,96},{96,128},{128,160},{160,192},{192,224},{1,3... | collective-permute-start | bytes 245768 | tf_op jit(solution)/shard_map/ppermute | solution.py:394
  6.4 41.5 %pack.1 = (bf16[128,640]{1,0:T(8,128)(2,1)}, bf16[128,640]{1,0:T(8,128)(2,1)}, bf16[128,640]{1,0:T(8,128)(2,1)}, bf16[128,640]{1,0:T(8,128)(2,1)}, bf16[128,640]...) custom-call(s32[4]{0:T(128)S(1)} %pad_add_fusion.where_ref, ...), custom_call_target="tpu_custom_call" | custom-call | bytes 2600000 | tf_op jit(solution)/shard_map/pack/pallas_call | solution.py:68
  49.3 2.6 %collective-permute-start.4 = (bf16[128,640]{1,0:T(8,128)(2,1)}, bf16[128,640]{1,0:T(8,128)(2,1)S(1)}, u32[]{:S(2)}, u32[]{:S(2)}) collective-permute-start(bf16[128,640]{1,0:T(8,128)(2,1)} %get-tuple-element.47), channel_id=1, source_target_pairs={{0,16},{8,24},{16,0},{24,8},{1,17},{9,25},{17,1},{25,9},{2,18},{10... | collective-permute-start | bytes 491528 | tf_op jit(solution)/shard_map/ppermute | solution.py:371
  54.3 1.7 %collective-permute-start.5 = (bf16[128,640]{1,0:T(8,128)(2,1)}, bf16[128,640]{1,0:T(8,128)(2,1)S(1)}, u32[]{:S(2)}, u32[]{:S(2)}) collective-permute-start(bf16[128,640]{1,0:T(8,128)(2,1)} %get-tuple-element.48), channel_id=1, source_target_pairs={{0,24},{8,0},{16,8},{24,16},{1,25},{9,1},{17,9},{25,17},{2,26},{10... | collective-permute-start | bytes 491528 | tf_op jit(solution)/shard_map/ppermute | solution.py:371
  56.0 2.9 %collective-permute-done.4.refs_2_ = bf16[128,640]{1,0:T(8,128)(2,1)S(1)} collective-permute-done((bf16[128,640]{1,0:T(8,128)(2,1)}, bf16[128,640]{1,0:T(8,128)(2,1)S(1)}, u32[]{:S(2)}, u32[]{:S(2)}) %collective-permute-start.4) | collective-permute-done | bytes 163872 | tf_op jit(solution)/shard_map/ppermute | solution.py:371
  58.9 3.4 %collective-permute-start.10 = (bf16[128,640]{1,0:T(8,128)(2,1)S(1)}, bf16[128,640]{1,0:T(8,128)(2,1)S(1)}, u32[]{:S(2)}, u32[]{:S(2)}) collective-permute-start(bf16[128,640]{1,0:T(8,128)(2,1)S(1)} %maximum_maximum_fusion.refs_4_), channel_id=1, source_target_pairs={{0,1},{1,0},{2,3},{3,2},{4,5},{5,4},{6,7},{7,6},{8,9},{9,8},{10,11... | collective-permute-start | bytes 491528 | tf_op jit(solution)/shard_map/ppermute | solution.py:379
  62.6 3.1 %collective-permute-start.12 = (bf16[128,640]{1,0:T(8,128)(2,1)S(1)}, bf16[128,640]{1,0:T(8,128)(2,1)S(1)}, u32[]{:S(2)}, u32[]{:S(2)}) collective-permute-start(bf16[128,640]{1,0:T(8,128)(2,1)S(1)} %collective-permute-done.8.refs_6_), channel_id=1, source_target_pairs={{0,1},{1,0},{2,3},{3,2},{4,5},{5,4},{6,7},{7,6},{8,9},{9,8},{10,11... | collective-permute-start | bytes 491528 | tf_op jit(solution)/shard_map/ppermute | solution.py:379
  71.2 8.6 %pair.2 = (bf16[1024,640]{1,0:T(8,128)(2,1)}, bf16[1024,640]{1,0:T(8,128)(2,1)}, bf16[512,256]{1,0:T(8,128)(2,1)}, bf16[1024,512]{1,0:T(8,128)(2,1)}) custom-call(s32[4]{0:T(128)S(1)} %pad_add_fusion.where_ref, bf16[128,640]{1,0:T(8,128)(2,1)S(1)} %copy-done.4, bf16[128,640]{1,0:T(8,128)(2,1)S(1)} %collective-permute-done.3.refs_1_, ...), custom_call_target="tpu_custom_call" | custom-call | flops 4000000000 | bytes 8000000 | tf_op jit(solution)/shard_map/pair/pallas_call | solution.py:215
  81.1 9.1 %pair.3 = (bf16[4,128,640]{2,1,0:T(8,128)(2,1)}, bf16[4,128,640]{2,1,0:T(8,128)(2,1)}, bf16[128,512]{1,0:T(8,128)(2,1)}, bf16[128,512]{1,0:T(8,128)(2,1)}, bf16[...) custom-call(s32[4]{0:T(128)S(1)} %pad_add_fusion.where_ref, ...), custom_call_target="tpu_custom_call" | custom-call | flops 4000000000 | bytes 8000000 | tf_op jit(solution)/shard_map/pair/pallas_call | solution.py:215
  90.3 2.7 %collective-permute-start.14 = (bf16[4,128,640]{2,1,0:T(8,128)(2,1)}, bf16[4,128,640]{2,1,0:T(8,128)(2,1)S(1)}, u32[]{:S(2)}, u32[]{:S(2)}) collective-permute-start(bf16[4,128,640]{2,1,0:T(8,128)(2,1)} %get-tuple-element.53), channel_id=1, source_target_pairs={{0,1},{1,0},{2,3},{3,2},{4,5},{5,4},{6,7},{7,6},{8,9},{9,8},{10,11... | collective-permute-start | bytes 1966088 | tf_op jit(solution)/shard_map/ppermute | solution.py:379
  93.0 1.9 %collective-permute-done.14 = bf16[4,128,640]{2,1,0:T(8,128)(2,1)S(1)} collective-permute-done((bf16[4,128,640]{2,1,0:T(8,128)(2,1)}, bf16[4,128,640]{2,1,0:T(8,128)(2,1)S(1)}, u32[]{:S(2)}, u32[]{:S(2)}) %collective-permute-start.14) | collective-permute-done | bytes 655392 | tf_op jit(solution)/shard_map/ppermute | solution.py:379
  96.3 4.2 %grad.1 = bf16[512,1024]{1,0:T(8,128)(2,1)} custom-call(bf16[1024,640]{1,0:T(8,128)(2,1)} %get-tuple-element.49.refs_4_.l_ref, bf16[1024,512]{1,0:T(8,128)(2,1)} %get-tuple-element.70.first_ref, bf16[1024,512]{1,0:T(8,128)(2,1)} %get-tuple-element.71.second_ref), custom_call_target="tpu_custom_call" | custom-call | flops 1100000000 | bytes 4400000 | tf_op jit(solution)/shard_map/grad/pallas_call | solution.py:241
  100.5 7.4 %all-to-all-start = ((bf16[8,64,1024]{2,1,0:T(8,128)(2,1)}), bf16[8,64,1024]{2,1,0:T(8,128)(2,1)S(1)}, u32[]{:S(2)}, u32[]{:S(2)}) async-start(bf16[8,64,1024]{2,1,0:T(8,128)(2,1)} %bitcast.16), calls=%async_computation | async-start | bytes 2097152 | tf_op jit(solution)/shard_map/all_to_all | solution.py:367
  110.6 7.3 %collective-permute-done.15 = bf16[128,640]{1,0:T(8,128)(2,1)S(1)} collective-permute-done((bf16[128,640]{1,0:T(8,128)(2,1)S(1)}, bf16[128,640]{1,0:T(8,128)(2,1)S(1)}, u32[]{:S(2)}, u32[]{:S(2)}) %collective-permute-start.15) | collective-permute-done | bytes 163872 | tf_op jit(solution)/shard_map/ppermute | solution.py:371
  118.2 2.5 %collective-permute-start.20 = (bf16[128,640]{1,0:T(8,128)(2,1)S(1)}, bf16[128,640]{1,0:T(8,128)(2,1)S(1)}, u32[]{:S(2)}, u32[]{:S(2)}) collective-permute-start(bf16[128,640]{1,0:T(8,128)(2,1)S(1)} %add_convert_fusion.refs_0_), channel_id=1, source_target_pairs={{0,6},{2,0},{4,2},{6,4},{1,7},{3,1},{5,3},{7,5},{8,14},{10,8},{12,... | collective-permute-start | bytes 491528 | tf_op jit(solution)/shard_map/ppermute | solution.py:371
  121.9 2.1 %collective-permute-done.20.refs_3_ = bf16[128,640]{1,0:T(8,128)(2,1)S(1)} collective-permute-done((bf16[128,640]{1,0:T(8,128)(2,1)S(1)}, bf16[128,640]{1,0:T(8,128)(2,1)S(1)}, u32[]{:S(2)}, u32[]{:S(2)}) %collective-permute-start.20) | collective-permute-done | bytes 163872 | tf_op jit(solution)/shard_map/ppermute | solution.py:371
  123.9 2.8 %collective-permute-done.19.refs_2_ = bf16[128,640]{1,0:T(8,128)(2,1)S(1)} collective-permute-done((bf16[128,640]{1,0:T(8,128)(2,1)S(1)}, bf16[128,640]{1,0:T(8,128)(2,1)S(1)}, u32[]{:S(2)}, u32[]{:S(2)}) %collective-permute-start.19) | collective-permute-done | bytes 163872 | tf_op jit(solution)/shard_map/ppermute | solution.py:371
  126.7 4.1 %collective-permute-done.18.refs_1_ = bf16[128,640]{1,0:T(8,128)(2,1)S(1)} collective-permute-done((bf16[128,640]{1,0:T(8,128)(2,1)S(1)}, bf16[128,640]{1,0:T(8,128)(2,1)S(1)}, u32[]{:S(2)}, u32[]{:S(2)}) %collective-permute-start.18) | collective-permute-done | bytes 163872 | tf_op jit(solution)/shard_map/ppermute | solution.py:371
  132.9 2.0 %collective-permute-start.21 = (bf16[128,512]{1,0:T(8,128)(2,1)S(1)}, bf16[128,512]{1,0:T(8,128)(2,1)S(1)}, u32[]{:S(2)}, u32[]{:S(2)}) collective-permute-start(bf16[128,512]{1,0:T(8,128)(2,1)S(1)} %copy-done.7), channel_id=1, source_target_pairs={{0,8},{8,16},{16,24},{24,0},{1,9},{9,17},{17,25},{25,1},{2,10},{10... | collective-permute-start | bytes 393224 | tf_op jit(solution)/shard_map/ppermute | solution.py:371
  134.9 2.1 %collective-permute-done.24 = bf16[64,640]{1,0:T(8,128)(2,1)S(1)} collective-permute-done((bf16[64,640]{1,0:T(8,128)(2,1)S(1)}, bf16[64,640]{1,0:T(8,128)(2,1)S(1)}, u32[]{:S(2)}, u32[]{:S(2)}) %collective-permute-start.24) | collective-permute-done | bytes 81952 | tf_op jit(solution)/shard_map/ppermute | solution.py:416
  137.1 2.5 %collective-permute-start.25 = (f32[64,640]{1,0:T(8,128)S(1)}, f32[64,640]{1,0:T(8,128)S(1)}, u32[]{:S(2)}, u32[]{:S(2)}) collective-permute-start(f32[64,640]{1,0:T(8,128)S(1)} %convert_add_fusion.mine_ref), channel_id=1, source_target_pairs={{0,1},{1,0},{2,3},{3,2},{4,5},{5,4},{6,7},{7,6},{8,9},{9,8},{10,11... | collective-permute-start | bytes 491528 | tf_op jit(solution)/shard_map/ppermute | solution.py:379
  140.4 2.5 %collective-permute-start.23 = (bf16[128,512]{1,0:T(8,128)(2,1)S(1)}, bf16[128,512]{1,0:T(8,128)(2,1)S(1)}, u32[]{:S(2)}, u32[]{:S(2)}) collective-permute-start(bf16[128,512]{1,0:T(8,128)(2,1)S(1)} %copy-done.5), channel_id=1, source_target_pairs={{0,24},{8,0},{16,8},{24,16},{1,25},{9,1},{17,9},{25,17},{2,26},{10... | collective-permute-start | bytes 393224 | tf_op jit(solution)/shard_map/ppermute | solution.py:371
  143.9 1.9 %collective-permute-start.27 = (bf16[16,1024]{1,0:T(8,128)(2,1)S(1)}, bf16[16,1024]{1,0:T(8,128)(2,1)S(1)}, u32[]{:S(2)}, u32[]{:S(2)}) collective-permute-start(bf16[16,1024]{1,0:T(8,128)(2,1)S(1)} %get-tuple-element.74), channel_id=1, source_target_pairs={{0,16},{8,24},{16,0},{24,8},{1,17},{9,25},{17,1},{25,9},{2,18},{10... | collective-permute-start | bytes 98312 | tf_op jit(solution)/shard_map/ppermute | solution.py:371
  146.1 3.1 %collective-permute-start.28 = (bf16[16,1024]{1,0:T(8,128)(2,1)S(1)}, bf16[16,1024]{1,0:T(8,128)(2,1)S(1)}, u32[]{:S(2)}, u32[]{:S(2)}) collective-permute-start(bf16[16,1024]{1,0:T(8,128)(2,1)S(1)} %get-tuple-element.75), channel_id=1, source_target_pairs={{0,24},{8,0},{16,8},{24,16},{1,25},{9,1},{17,9},{25,17},{2,26},{10... | collective-permute-start | bytes 98312 | tf_op jit(solution)/shard_map/ppermute | solution.py:371
  (72 shorter events, 26.2 us)
Async XLA Ops:
  1.9 50.0 %collective-permute-start.6 = (bf16[64,640]{1,0:T(8,128)(2,1)S(1)}, bf16[64,640]{1,0:T(8,128)(2,1)S(1)}, u32[]{:S(2)}, u32[]{:S(2)}) collective-permute-start(bf16[64,640]{1,0:T(8,128)(2,1)S(1)} %pad_maximum_fusion), channel_id=1, source_target_pairs={{0,32},{32,64},{64,96},{96,128},{128,160},{160,192},{192,224},{1,3... | collective-permute-start | bytes 245768 | tf_op jit(solution)/shard_map/ppermute | solution.py:394
  47.9 6.4 %collective-permute-start.3 = (bf16[128,640]{1,0:T(8,128)(2,1)}, bf16[128,640]{1,0:T(8,128)(2,1)S(1)}, u32[]{:S(2)}, u32[]{:S(2)}) collective-permute-start(bf16[128,640]{1,0:T(8,128)(2,1)} %get-tuple-element.46), channel_id=1, source_target_pairs={{0,8},{8,16},{16,24},{24,0},{1,9},{9,17},{17,25},{25,1},{2,10},{10... | collective-permute-start | bytes 491528 | tf_op jit(solution)/shard_map/ppermute | solution.py:371
  49.3 9.6 %collective-permute-start.4 = (bf16[128,640]{1,0:T(8,128)(2,1)}, bf16[128,640]{1,0:T(8,128)(2,1)S(1)}, u32[]{:S(2)}, u32[]{:S(2)}) collective-permute-start(bf16[128,640]{1,0:T(8,128)(2,1)} %get-tuple-element.47), channel_id=1, source_target_pairs={{0,16},{8,24},{16,0},{24,8},{1,17},{9,25},{17,1},{25,9},{2,18},{10... | collective-permute-start | bytes 491528 | tf_op jit(solution)/shard_map/ppermute | solution.py:371
  52.0 10.3 %collective-permute-start.9 = (bf16[128,640]{1,0:T(8,128)(2,1)S(1)}, bf16[128,640]{1,0:T(8,128)(2,1)S(1)}, u32[]{:S(2)}, u32[]{:S(2)}) collective-permute-start(bf16[128,640]{1,0:T(8,128)(2,1)S(1)} %maximum_maximum_fusion.refs_4_), channel_id=1, source_target_pairs={{0,24},{8,0},{16,8},{24,16},{1,25},{9,1},{17,9},{25,17},{2,26},{10... | collective-permute-start | bytes 491528 | tf_op jit(solution)/shard_map/ppermute | solution.py:371
  53.1 9.5 %collective-permute-start.8 = (bf16[128,640]{1,0:T(8,128)(2,1)S(1)}, bf16[128,640]{1,0:T(8,128)(2,1)S(1)}, u32[]{:S(2)}, u32[]{:S(2)}) collective-permute-start(bf16[128,640]{1,0:T(8,128)(2,1)S(1)} %maximum_maximum_fusion.refs_4_), channel_id=1, source_target_pairs={{0,16},{8,24},{16,0},{24,8},{1,17},{9,25},{17,1},{25,9},{2,18},{10... | collective-permute-start | bytes 491528 | tf_op jit(solution)/shard_map/ppermute | solution.py:371
  53.3 12.8 %collective-permute-start.7 = (bf16[128,640]{1,0:T(8,128)(2,1)S(1)}, bf16[128,640]{1,0:T(8,128)(2,1)S(1)}, u32[]{:S(2)}, u32[]{:S(2)}) collective-permute-start(bf16[128,640]{1,0:T(8,128)(2,1)S(1)} %maximum_maximum_fusion.refs_4_), channel_id=1, source_target_pairs={{0,8},{8,16},{16,24},{24,0},{1,9},{9,17},{17,25},{25,1},{2,10},{10... | collective-permute-start | bytes 491528 | tf_op jit(solution)/shard_map/ppermute | solution.py:371
  54.3 13.0 %collective-permute-start.5 = (bf16[128,640]{1,0:T(8,128)(2,1)}, bf16[128,640]{1,0:T(8,128)(2,1)S(1)}, u32[]{:S(2)}, u32[]{:S(2)}) collective-permute-start(bf16[128,640]{1,0:T(8,128)(2,1)} %get-tuple-element.48), channel_id=1, source_target_pairs={{0,24},{8,0},{16,8},{24,16},{1,25},{9,1},{17,9},{25,17},{2,26},{10... | collective-permute-start | bytes 491528 | tf_op jit(solution)/shard_map/ppermute | solution.py:371
  58.9 8.9 %collective-permute-start.10 = (bf16[128,640]{1,0:T(8,128)(2,1)S(1)}, bf16[128,640]{1,0:T(8,128)(2,1)S(1)}, u32[]{:S(2)}, u32[]{:S(2)}) collective-permute-start(bf16[128,640]{1,0:T(8,128)(2,1)S(1)} %maximum_maximum_fusion.refs_4_), channel_id=1, source_target_pairs={{0,1},{1,0},{2,3},{3,2},{4,5},{5,4},{6,7},{7,6},{8,9},{9,8},{10,11... | collective-permute-start | bytes 491528 | tf_op jit(solution)/shard_map/ppermute | solution.py:379
  62.3 7.1 %collective-permute-start.13 = (bf16[128,640]{1,0:T(8,128)(2,1)S(1)}, bf16[128,640]{1,0:T(8,128)(2,1)S(1)}, u32[]{:S(2)}, u32[]{:S(2)}) collective-permute-start(bf16[128,640]{1,0:T(8,128)(2,1)S(1)} %collective-permute-done.9.refs_7_), channel_id=1, source_target_pairs={{0,1},{1,0},{2,3},{3,2},{4,5},{5,4},{6,7},{7,6},{8,9},{9,8},{10,11... | collective-permute-start | bytes 491528 | tf_op jit(solution)/shard_map/ppermute | solution.py:379
  62.6 7.6 %collective-permute-start.12 = (bf16[128,640]{1,0:T(8,128)(2,1)S(1)}, bf16[128,640]{1,0:T(8,128)(2,1)S(1)}, u32[]{:S(2)}, u32[]{:S(2)}) collective-permute-start(bf16[128,640]{1,0:T(8,128)(2,1)S(1)} %collective-permute-done.8.refs_6_), channel_id=1, source_target_pairs={{0,1},{1,0},{2,3},{3,2},{4,5},{5,4},{6,7},{7,6},{8,9},{9,8},{10,11... | collective-permute-start | bytes 491528 | tf_op jit(solution)/shard_map/ppermute | solution.py:379
  67.2 12.6 %collective-permute-start = (bf16[128,640]{1,0:T(8,128)(2,1)}, bf16[128,640]{1,0:T(8,128)(2,1)S(1)}, u32[]{:S(2)}, u32[]{:S(2)}) collective-permute-start(bf16[128,640]{1,0:T(8,128)(2,1)} %get-tuple-element.42), channel_id=1, source_target_pairs={{0,8},{8,16},{16,24},{24,0},{1,9},{9,17},{17,25},{25,1},{2,10},{10... | collective-permute-start | bytes 491528 | tf_op jit(solution)/shard_map/ppermute | solution.py:371
  67.8 12.0 %collective-permute-start.1 = (bf16[128,640]{1,0:T(8,128)(2,1)}, bf16[128,640]{1,0:T(8,128)(2,1)S(1)}, u32[]{:S(2)}, u32[]{:S(2)}) collective-permute-start(bf16[128,640]{1,0:T(8,128)(2,1)} %get-tuple-element.43), channel_id=1, source_target_pairs={{0,16},{8,24},{16,0},{24,8},{1,17},{9,25},{17,1},{25,9},{2,18},{10... | collective-permute-start | bytes 491528 | tf_op jit(solution)/shard_map/ppermute | solution.py:371
  69.5 10.4 %collective-permute-start.2 = (bf16[128,640]{1,0:T(8,128)(2,1)}, bf16[128,640]{1,0:T(8,128)(2,1)S(1)}, u32[]{:S(2)}, u32[]{:S(2)}) collective-permute-start(bf16[128,640]{1,0:T(8,128)(2,1)} %get-tuple-element.44), channel_id=1, source_target_pairs={{0,24},{8,0},{16,8},{24,16},{1,25},{9,1},{17,9},{25,17},{2,26},{10... | collective-permute-start | bytes 491528 | tf_op jit(solution)/shard_map/ppermute | solution.py:371
  100.5 42.4 %all-to-all-start = ((bf16[8,64,1024]{2,1,0:T(8,128)(2,1)}), bf16[8,64,1024]{2,1,0:T(8,128)(2,1)S(1)}, u32[]{:S(2)}, u32[]{:S(2)}) async-start(bf16[8,64,1024]{2,1,0:T(8,128)(2,1)} %bitcast.16), calls=%async_computation | async-start | bytes 2097152 | tf_op jit(solution)/shard_map/all_to_all | solution.py:367
  108.0 10.0 %collective-permute-start.15 = (bf16[128,640]{1,0:T(8,128)(2,1)S(1)}, bf16[128,640]{1,0:T(8,128)(2,1)S(1)}, u32[]{:S(2)}, u32[]{:S(2)}) collective-permute-start(bf16[128,640]{1,0:T(8,128)(2,1)S(1)} %get-tuple-element.56), channel_id=1, source_target_pairs={{0,8},{8,16},{16,24},{24,0},{1,9},{9,17},{17,25},{25,1},{2,10},{10... | collective-permute-start | bytes 491528 | tf_op jit(solution)/shard_map/ppermute | solution.py:371
  108.1 9.9 %collective-permute-start.16 = (bf16[128,640]{1,0:T(8,128)(2,1)S(1)}, bf16[128,640]{1,0:T(8,128)(2,1)S(1)}, u32[]{:S(2)}, u32[]{:S(2)}) collective-permute-start(bf16[128,640]{1,0:T(8,128)(2,1)S(1)} %get-tuple-element.57), channel_id=1, source_target_pairs={{0,16},{8,24},{16,0},{24,8},{1,17},{9,25},{17,1},{25,9},{2,18},{10... | collective-permute-start | bytes 491528 | tf_op jit(solution)/shard_map/ppermute | solution.py:371
  108.9 9.2 %collective-permute-start.17 = (bf16[128,640]{1,0:T(8,128)(2,1)S(1)}, bf16[128,640]{1,0:T(8,128)(2,1)S(1)}, u32[]{:S(2)}, u32[]{:S(2)}) collective-permute-start(bf16[128,640]{1,0:T(8,128)(2,1)S(1)} %get-tuple-element.58), channel_id=1, source_target_pairs={{0,24},{8,0},{16,8},{24,16},{1,25},{9,1},{17,9},{25,17},{2,26},{10... | collective-permute-start | bytes 491528 | tf_op jit(solution)/shard_map/ppermute | solution.py:371
  121.3 9.6 %collective-permute-start.18 = (bf16[128,640]{1,0:T(8,128)(2,1)S(1)}, bf16[128,640]{1,0:T(8,128)(2,1)S(1)}, u32[]{:S(2)}, u32[]{:S(2)}) collective-permute-start(bf16[128,640]{1,0:T(8,128)(2,1)S(1)} %add_convert_fusion.refs_0_), channel_id=1, source_target_pairs={{0,2},{2,4},{4,6},{6,0},{1,3},{3,5},{5,7},{7,1},{8,10},{10,12},{12... | collective-permute-start | bytes 491528 | tf_op jit(solution)/shard_map/ppermute | solution.py:371
  132.9 11.1 %collective-permute-start.21 = (bf16[128,512]{1,0:T(8,128)(2,1)S(1)}, bf16[128,512]{1,0:T(8,128)(2,1)S(1)}, u32[]{:S(2)}, u32[]{:S(2)}) collective-permute-start(bf16[128,512]{1,0:T(8,128)(2,1)S(1)} %copy-done.7), channel_id=1, source_target_pairs={{0,8},{8,16},{16,24},{24,0},{1,9},{9,17},{17,25},{25,1},{2,10},{10... | collective-permute-start | bytes 393224 | tf_op jit(solution)/shard_map/ppermute | solution.py:371
  137.1 13.9 %collective-permute-start.25 = (f32[64,640]{1,0:T(8,128)S(1)}, f32[64,640]{1,0:T(8,128)S(1)}, u32[]{:S(2)}, u32[]{:S(2)}) collective-permute-start(f32[64,640]{1,0:T(8,128)S(1)} %convert_add_fusion.mine_ref), channel_id=1, source_target_pairs={{0,1},{1,0},{2,3},{3,2},{4,5},{5,4},{6,7},{7,6},{8,9},{9,8},{10,11... | collective-permute-start | bytes 491528 | tf_op jit(solution)/shard_map/ppermute | solution.py:379
  139.5 6.6 %collective-permute-start.22 = (bf16[128,512]{1,0:T(8,128)(2,1)S(1)}, bf16[128,512]{1,0:T(8,128)(2,1)S(1)}, u32[]{:S(2)}, u32[]{:S(2)}) collective-permute-start(bf16[128,512]{1,0:T(8,128)(2,1)S(1)} %copy-done.6), channel_id=1, source_target_pairs={{0,16},{8,24},{16,0},{24,8},{1,17},{9,25},{17,1},{25,9},{2,18},{10... | collective-permute-start | bytes 393224 | tf_op jit(solution)/shard_map/ppermute | solution.py:371
  140.4 9.2 %collective-permute-start.23 = (bf16[128,512]{1,0:T(8,128)(2,1)S(1)}, bf16[128,512]{1,0:T(8,128)(2,1)S(1)}, u32[]{:S(2)}, u32[]{:S(2)}) collective-permute-start(bf16[128,512]{1,0:T(8,128)(2,1)S(1)} %copy-done.5), channel_id=1, source_target_pairs={{0,24},{8,0},{16,8},{24,16},{1,25},{9,1},{17,9},{25,17},{2,26},{10... | collective-permute-start | bytes 393224 | tf_op jit(solution)/shard_map/ppermute | solution.py:371
  143.6 8.8 %collective-permute-start.26 = (bf16[16,1024]{1,0:T(8,128)(2,1)S(1)}, bf16[16,1024]{1,0:T(8,128)(2,1)S(1)}, u32[]{:S(2)}, u32[]{:S(2)}) collective-permute-start(bf16[16,1024]{1,0:T(8,128)(2,1)S(1)} %get-tuple-element.73), channel_id=1, source_target_pairs={{0,8},{8,16},{16,24},{24,0},{1,9},{9,17},{17,25},{25,1},{2,10},{10... | collective-permute-start | bytes 98312 | tf_op jit(solution)/shard_map/ppermute | solution.py:371
  143.9 8.4 %collective-permute-start.27 = (bf16[16,1024]{1,0:T(8,128)(2,1)S(1)}, bf16[16,1024]{1,0:T(8,128)(2,1)S(1)}, u32[]{:S(2)}, u32[]{:S(2)}) collective-permute-start(bf16[16,1024]{1,0:T(8,128)(2,1)S(1)} %get-tuple-element.74), channel_id=1, source_target_pairs={{0,16},{8,24},{16,0},{24,8},{1,17},{9,25},{17,1},{25,9},{2,18},{10... | collective-permute-start | bytes 98312 | tf_op jit(solution)/shard_map/ppermute | solution.py:371
  (14 other events, 204.4 us)

commit v6 on v4

--- a/solution.py
+++ b/solution.py
@@ -14,6 +14,7 @@
 VDIM = 128
 LATENT = 512
 TOK = 128
+SHARE = TOK // 8
 ROWS = 4 * TOK
 KEYS = 2 * ROWS
 TILE = 256
@@ -44,53 +45,66 @@
     return pltpu.with_memory_space_constraint(x, pltpu.HBM)
 
 
-def pack_kernel(q_ref, g_ref, earlier_ref, own_ref, out_ref):
-    for pair in range(2):
-        rows = slice(pair * TOK, (pair + 1) * TOK)
-        out_ref[0, rows, :384] = q_ref[:, pair * 384 : (pair + 1) * 384]
-        out_ref[0, rows, 384:] = g_ref[:, pair * 256 : (pair + 1) * 256]
-    out_ref[0, 2 * TOK : 2 * TOK + TOK // 2, :] = earlier_ref[...]
-    out_ref[0, 2 * TOK + TOK // 2 :, :] = own_ref[...]
-
-
-def pack_call(queries, out_grad, earlier, own):
-    half = pl.BlockSpec((TOK // 2, PAY), lambda y: (0, 0))
+def pack_kernel(where_ref, q_ref, g_ref, *refs):
+    piece_refs, sems = refs[:4], refs[4]
+    y = where_ref[1]
+    copies = []
+    for k in range(4):
+        to = (y + k) & 3
+        for pair in range(2):
+            left, at = pair * PAY, 4 * k + 2 * pair
+            from_q = q_ref.at[:, pl.ds(pl.multiple_of(to * 768 + pair * 384, 128), 384)]
+            from_g = g_ref.at[:, pl.ds(pl.multiple_of(to * 512 + pair * 256, 128), 256)]
+            to_q = piece_refs[k].at[:, left : left + 384]
+            to_g = piece_refs[k].at[:, left + 384 : left + PAY]
+            copies.append(pltpu.make_async_copy(from_q, to_q, sems.at[at]))
+            copies.append(pltpu.make_async_copy(from_g, to_g, sems.at[at + 1]))
+    for copy in copies:
+        copy.start()
+    for copy in copies:
+        copy.wait()
+
+
+def pack_call(place, queries, out_grad):
+    hbm = pl.BlockSpec(memory_space=pltpu.HBM)
+    vmem = pl.BlockSpec(memory_space=pltpu.VMEM)
     return pl.pallas_call(
         pack_kernel,
-        grid=(4,),
-        in_specs=[
-            pl.BlockSpec((TOK, 768), lambda y: (0, y)),
-            pl.BlockSpec((TOK, 512), lambda y: (0, y)),
-            half,
-            half,
-        ],
-        out_specs=pl.BlockSpec((1, 3 * TOK, PAY), lambda y: (y, 0, 0)),
-        out_shape=pltpu.HBM((4, 3 * TOK, PAY), BF16),
-        cost_estimate=pl.CostEstimate(flops=0, bytes_accessed=3_300_000, transcendentals=0),
+        in_specs=[pl.BlockSpec(memory_space=pltpu.SMEM), hbm, hbm],
+        out_specs=[vmem] * 4,
+        out_shape=[jax.ShapeDtypeStruct((TOK, 2 * PAY), BF16)] * 4,
+        scratch_shapes=[pltpu.SemaphoreType.DMA((16,))],
+        cost_estimate=pl.CostEstimate(flops=0, bytes_accessed=2_600_000, transcendentals=0),
         compiler_params=SMALL,
         name="pack",
-    )(in_hbm(queries), in_hbm(out_grad), earlier, own)
-
-
-def pair_kernel(where_ref, x_ref, mine_ref, other_ref, wk_ref, wv_ref, *refs):
+    )(place, in_hbm(queries), in_hbm(out_grad))
+
+
+def pair_kernel(where_ref, *refs):
+    pieces, mine_refs, other_refs, refs = refs[:4], refs[4:8], refs[8:12], refs[12:]
+    wk_ref, wv_ref, refs = refs[0], refs[1], refs[2:]
     keep_ref, send_ref, out_refs, dw_ref = refs[0], refs[1], refs[2:6], refs[6]
-    l_ref, kcat, vals, bias, dk_acc, dv_acc, grads, attended, dl_acc = refs[7:]
-    group, y, core = where_ref[0], where_ref[1], where_ref[2]
+    x_ref, l_ref, kcat, vals, bias, dk_acc, dv_acc, grads, attended, dl_acc = refs[7:]
+    group, y, core, x = where_ref[0], where_ref[1], where_ref[2], where_ref[3]
     pair = pl.program_id(0)
     half = TOK // 2
     lane = lax.broadcasted_iota(jnp.int32, (KEYS, 128), 1)
     low = lane < ROPE
+    for k in range(4):
+        block = (y - k) & 3
+        x_ref[pl.ds(pl.multiple_of(block * TOK, TOK), TOK), :] = pieces[k][...]
 
     @pl.when(pair == 0)
     def _():
-        for block in range(4):
-            for own in range(2):
-                row = own * ROWS + block * TOK
-                piece = slice(own * half, (own + 1) * half)
-                at = pl.multiple_of(row + core * half, half)
-                l_ref[pl.ds(at, half), :] = mine_ref[block, piece]
-                at = pl.multiple_of(row + (1 - core) * half, half)
-                l_ref[pl.ds(at, half), :] = other_ref[block, piece]
+        for j in range(4):
+            for k in range(4):
+                for own in range(2):
+                    row = own * ROWS + ((y - k) & 3) * TOK + ((x - j) & 3) * SHARE
+                    piece = slice((2 * k + own) * SHARE, (2 * k + own + 1) * SHARE)
+                    at = pl.multiple_of(row + core * half, SHARE)
+                    l_ref[pl.ds(at, SHARE), :] = mine_refs[j][piece]
+                    at = pl.multiple_of(row + (1 - core) * half, SHARE)
+                    l_ref[pl.ds(at, SHARE), :] = other_refs[j][piece]
         ids = l_ref[:, LATENT:].astype(F32)
         key_id = ids[:, ROPE : ROPE + 1]
         key_row = lax.broadcasted_iota(jnp.int32, (KEYS, 1), 0)
@@ -124,9 +138,8 @@
             start = i * TILE
             span = slice(start, start + SPAN)
             rows = slice(start, start + TILE)
-            qc = x_ref[2 * i : 2 * i + 2, :, h * NOPE : h * NOPE + 256].reshape(TILE, 256)
-            og = x_ref[2 * i : 2 * i + 2, :, 384 + h * VDIM : 384 + (h + 1) * VDIM]
-            og = og.reshape(TILE, VDIM)
+            qc = x_ref[rows, h * NOPE : h * NOPE + 256]
+            og = x_ref[rows, 384 + h * VDIM : 384 + (h + 1) * VDIM]
             s = nt(kcat[h, span, :], qc) * (SCALE * LOG2E) + bias[i]
             top = jnp.max(s, axis=0, keepdims=True)
             e = jnp.exp2(s - top)
@@ -180,22 +193,22 @@
                 send_ref[k, piece, :] = dl_acc[pl.ds(at, half), :].astype(BF16)
 
 
-def pair_call(place, x, other, key_weight, value_weight):
+def pair_call(place, pieces, lats, key_weight, value_weight):
     def whole(*shape):
         return pl.BlockSpec(shape, lambda i, w: (0,) * len(shape))
 
     weight_spec = pl.BlockSpec((LATENT, 256), lambda i, w: (0, 2 * w[1] + i))
-    x_spec = pl.BlockSpec((4, TOK, PAY), lambda i, w: (0, i, 0))
-    lat_spec = pl.BlockSpec((4, TOK, PAY), lambda i, w: (0, 2, 0))
+    x_spec = pl.BlockSpec((TOK, PAY), lambda i, w: (0, i))
     dw_spec = pl.BlockSpec((LATENT, 512), lambda i, w: (0, i))
     return pl.pallas_call(
         pair_kernel,
         grid_spec=pltpu.PrefetchScalarGridSpec(
             num_scalar_prefetch=1,
             grid=(2,),
-            in_specs=[x_spec, lat_spec, whole(4, TOK, PAY), weight_spec, weight_spec],
+            in_specs=[x_spec] * 4 + [whole(TOK, PAY)] * 8 + [weight_spec] * 2,
             out_specs=[whole(4, TOK, PAY)] * 2 + [whole(TOK, 512)] * 4 + [dw_spec],
             scratch_shapes=[
+                pltpu.VMEM((ROWS, PAY), BF16),
                 pltpu.VMEM((KEYS, PAY), BF16),
                 pltpu.VMEM((2, KEYS, 256), BF16),
                 pltpu.VMEM((KEYS, 256), BF16),
@@ -215,15 +228,17 @@
             flops=8_000_000_000, bytes_accessed=10_000_000, transcendentals=1_600_000
         ),
         name="pair",
-    )(place, in_hbm(x), in_hbm(x), in_hbm(other), in_hbm(key_weight), in_hbm(value_weight))
+    )(place, *pieces, *lats, in_hbm(key_weight), in_hbm(value_weight))
 
 
 def latent_kernel(where_ref, *refs):
-    terms, out_ref, held = refs[:4], refs[4], refs[5]
+    terms, own_ref, later_ref, held = refs[:4], refs[4], refs[5], refs[6]
     x = where_ref[3]
     for k in range(4):
         held[(x - k) & 3] = terms[k][...].astype(F32)
-    out_ref[...] = (held[0] + held[1]) + (held[2] + held[3])
+    total = (held[0] + held[1]) + (held[2] + held[3])
+    own_ref[...] = total[: TOK // 2]
+    later_ref[...] = total[TOK // 2 :].astype(BF16)
 
 
 def latent_call(place, terms):
@@ -231,9 +246,12 @@
     return pl.pallas_call(
         latent_kernel,
         in_specs=[pl.BlockSpec(memory_space=pltpu.SMEM)] + [vmem] * 4,
-        out_specs=vmem,
-        out_shape=jax.ShapeDtypeStruct((TOK // 2, PAY), F32),
-        scratch_shapes=[pltpu.VMEM((4, TOK // 2, PAY), F32)],
+        out_specs=[vmem] * 2,
+        out_shape=[
+            jax.ShapeDtypeStruct((TOK // 2, PAY), F32),
+            jax.ShapeDtypeStruct((TOK // 2, PAY), BF16),
+        ],
+        scratch_shapes=[pltpu.VMEM((4, TOK, PAY), F32)],
         compiler_params=SMALL,
         name="latent",
     )(place, *terms)
@@ -346,17 +364,24 @@
     place = [lax.axis_index("z"), lax.axis_index("y"), core, lax.axis_index("x")]
     place = jnp.stack(place).astype(jnp.int32)
     half = TOK // 2
-    rows = lax.dynamic_slice_in_dim(latents, core * half, half)
-    ids = lax.dynamic_slice_in_dim(doc_ids, core * half, half)
+    start = (core * 4 + lax.axis_index("x")) * SHARE
+    rows = lax.dynamic_slice_in_dim(latents, start, SHARE)
+    ids = lax.dynamic_slice_in_dim(doc_ids, start, SHARE)
     pay = jnp.concatenate(
-        [rows, ids.astype(BF16)[:, None], jnp.zeros((half, PAY - 577), BF16)], axis=1
+        [rows, ids.astype(BF16)[:, None], jnp.zeros((SHARE, PAY - 577), BF16)], axis=1
     )
     ahead = [(i, i + 1) for i in range(GROUPS - 1)]
     behind = [(i + 1, i) for i in range(GROUPS - 1)]
     earlier = lax.ppermute(pay, "z", ahead)
-    x = exchanged(pack_call(queries, out_grad, earlier, pay), "y")
-    other = swapped(x[:, 2 * TOK :])
-    keep, send, *outs, dw = pair_call(place, x, other, key_weight, value_weight)
+    packed = pack_call(place, queries, out_grad)
+    share = jnp.concatenate([earlier, pay], axis=0)
+    share, packed = lax.optimization_barrier((share, packed))
+    shares = fanned([share] * 4, "y")
+    pieces = fanned(packed, "y")
+    shares, pieces[1], pieces[3] = lax.optimization_barrier((shares, pieces[1], pieces[3]))
+    mine = fanned([jnp.concatenate(shares, axis=0)] * 4, "x")
+    lats = mine + [swapped(piece) for piece in mine]
+    keep, send, *outs, dw = pair_call(place, pieces, lats, key_weight, value_weight)
 
     came = swapped(send)
     dw = half_call(place, exchanged(dw.reshape(8, 64, 1024), "z"))
@@ -365,13 +390,14 @@
     total = parts[0]
     for part in parts[1:]:
         total = total + part.astype(F32)
-    later, outs = lax.optimization_barrier((total[half:].astype(BF16), outs))
-    later = lax.ppermute(later, "z", behind)
-    own = (total[:half] + later.astype(F32)).astype(BF16)
-    part = latent_call(place, fanned([own] * 4, "x"))
+    total, outs = lax.optimization_barrier((total.astype(BF16), outs))
+    terms, outs = lax.optimization_barrier((fanned([total] * 4, "x"), fanned(outs, "y")))
+    own, later = latent_call(place, terms)
+    later, dw = lax.optimization_barrier((lax.ppermute(later, "z", behind), fanned(dw, "y")))
+    part = own + later.astype(F32)
     latent_grad = jnp.transpose(join_call(place, part, swapped(part)))
-    attended = attended_call(place, fanned(outs, "y"))
-    key_grad, value_grad = weight_call(place, fanned(dw, "y"))
+    attended = attended_call(place, outs)
+    key_grad, value_grad = weight_call(place, dw)
     return attended, latent_grad, key_grad, value_grad
 
 

time: 121 us -> 104 us (0.86)
  blocking collectives: 27.3 us -> 0 us
  starting transfers between devices: 33.6 us -> 49.1 us
  waiting for transfers between devices: 30.9 us -> 28.5 us
  Pallas kernels: 25.7 us -> 23.8 us
    all_to_all x1 -> x0, blocking collectives: 27.3 us -> none  [exchanged(): return lax.all_to_all(x, axes, split_axis=0, concat_axis=0, tiled=True)]
    ppermute x1, waiting for transfers between devices: 15.5 us -> 0.01 us  [per_device(): lax.ppermute(later, 'z', behind)]
    ppermute x12 -> x21, waiting for transfers between devices: 12.3 us -> 23.1 us  [moved(): lax.ppermute(value, along, [(i, (i + step) % size) for i in range(size)])]
    ppermute x12 -> x21, starting transfers between devices: 12.1 us -> 21.8 us  [moved(): lax.ppermute(value, along, [(i, (i + step) % size) for i in range(size)])]
    ppermute x3 -> x6, starting transfers between devices: 6.13 us -> 13.3 us  [swapped(): return lax.ppermute(value, 'core', [(0, 1), (1, 0)])]
    all_to_all x1, waiting for transfers between devices: 0.01 us -> 2.59 us  [exchanged(): return lax.all_to_all(x, axes, split_axis=0, concat_axis=0, tiled=True)]
    pallas_call x1, Pallas kernels: 3.7 us -> 2.06 us  [pack_call(): pl.pallas_call(pack_kernel, in_specs=[pl.BlockSpec(memory_space=pltpu.SME...]
    ppermute x1, waiting for transfers between devices: 1.46 us -> 0.01 us  [per_device(): earlier = lax.ppermute(pay, 'z', ahead)]
  transfers between devices with their start and end apart: 18 -> 30, of which waited for: 10 -> 14; matrix products, arithmetic and copies ran while one was open for 0% -> 0% of each run, Pallas kernels for 3% -> 6%
where the time goes in v6:
time: 104 us
  starting transfers between devices  49.1 us (47%)
  waiting for transfers between devices  28.5 us (27%)
  Pallas kernels  23.8 us (23%)
  other arithmetic  1.27 us (1%)
    ppermute x21, waiting for transfers between devices, moved(): lax.ppermute(value, along, [(i, (i + step) % size) for i in range(size)])  23.1 us
    ppermute x21, starting transfers between devices, moved(): lax.ppermute(value, along, [(i, (i + step) % size) for i in range(size)])  21.8 us
    pallas_call x1, Pallas kernels, pair_call(): pl.pallas_call(pair_kernel, grid_spec=pltpu.PrefetchScalarGridSpec(num_sc...  16.3 us
    ppermute x6, starting transfers between devices, swapped(): return lax.ppermute(value, 'core', [(0, 1), (1, 0)])  13.3 us
    all_to_all x1, starting transfers between devices, exchanged(): return lax.all_to_all(x, axes, split_axis=0, concat_axis=0, tiled=True)  8.35 us
    ppermute x1, starting transfers between devices, per_device(): earlier = lax.ppermute(pay, 'z', ahead)  4.37 us
    ppermute x6, waiting for transfers between devices, swapped(): return lax.ppermute(value, 'core', [(0, 1), (1, 0)])  2.74 us
    all_to_all x1, waiting for transfers between devices, exchanged(): return lax.all_to_all(x, axes, split_axis=0, concat_axis=0, tiled=True)  2.59 us
  transfers between devices with their start and end apart: 30, of which 14 were waited for; matrix products, arithmetic and copies ran while one was open for 0% of the time, Pallas kernels for 6%

profile of v6, /device:TPU:1, one launch (start us, length us, event | category | flops | bytes accessed | tf_op | source)
XLA Modules:
  0.0 103.9 jit_solution(13821186203156180750)
XLA Ops:
  1.9 4.4 %collective-permute-start = (bf16[16,640]{1,0:T(8,128)(2,1)S(1)}, bf16[16,640]{1,0:T(8,128)(2,1)S(1)}, u32[]{:S(2)}, u32[]{:S(2)}) collective-permute-start(bf16[16,640]{1,0:T(8,128)(2,1)S(1)} %pad_maximum_fusion), channel_id=1, source_target_pairs={{0,32},{32,64},{64,96},{96,128},{128,160},{160,192},{192,224},{1,3... | collective-permute-start | bytes 61448 | tf_op jit(solution)/shard_map/ppermute | solution.py:375
  6.3 2.1 %pack.1 = (bf16[128,1280]{1,0:T(8,128)(2,1)S(1)}, bf16[128,1280]{1,0:T(8,128)(2,1)S(1)}, bf16[128,1280]{1,0:T(8,128)(2,1)S(1)}, bf16[128,1280]{1,0:T(8,128)(2,1)S(1)}) custom-call(s32[4]{0:T(128)S(1)} %pad_add_fusion.where_ref, bf16[128,3072]{1,0:T(8,128)(2,1)} %q_ref.1, bf16[128,2048]{1,0:T(8,128)(2,1)} %g_ref.1), custom_call_target="tpu_custom_call" | custom-call | bytes 2600000 | tf_op jit(solution)/shard_map/pack/pallas_call | solution.py:71
  9.8 1.5 %collective-permute-start.5 = (bf16[128,1280]{1,0:T(8,128)(2,1)S(1)}, bf16[128,1280]{1,0:T(8,128)(2,1)S(1)}, u32[]{:S(2)}, u32[]{:S(2)}) collective-permute-start(bf16[128,1280]{1,0:T(8,128)(2,1)S(1)} %get-tuple-element.59), channel_id=1, source_target_pairs={{0,24},{8,0},{16,8},{24,16},{1,25},{9,1},{17,9},{25,17},{2,26},{10... | collective-permute-start | bytes 983048 | tf_op jit(solution)/shard_map/ppermute | solution.py:351
  11.3 1.4 %collective-permute-start.3 = (bf16[32,640]{1,0:T(8,128)(2,1)S(1)}, bf16[32,640]{1,0:T(8,128)(2,1)S(1)}, u32[]{:S(2)}, u32[]{:S(2)}) collective-permute-start(bf16[32,640]{1,0:T(8,128)(2,1)S(1)} %maximum_maximum_fusion), channel_id=1, source_target_pairs={{0,24},{8,0},{16,8},{24,16},{1,25},{9,1},{17,9},{25,17},{2,26},{10... | collective-permute-start | bytes 122888 | tf_op jit(solution)/shard_map/ppermute | solution.py:351
  13.8 4.9 %collective-permute-done.3 = bf16[32,640]{1,0:T(8,128)(2,1)S(1)} collective-permute-done((bf16[32,640]{1,0:T(8,128)(2,1)S(1)}, bf16[32,640]{1,0:T(8,128)(2,1)S(1)}, u32[]{:S(2)}, u32[]{:S(2)}) %collective-permute-start.3) | collective-permute-done | bytes 40992 | tf_op jit(solution)/shard_map/ppermute | solution.py:351
  19.9 2.6 %collective-permute-start.9 = (bf16[128,640]{1,0:T(8,128)(2,1)S(1)}, bf16[128,640]{1,0:T(8,128)(2,1)S(1)}, u32[]{:S(2)}, u32[]{:S(2)}) collective-permute-start(bf16[128,640]{1,0:T(8,128)(2,1)S(1)} %constant_dynamic-update-slice_fusion.refs_4_), channel_id=1, source_target_pairs={{0,6},{2,0},{4,2},{6,4},{1,7},{3,1},{5,3},{7,5},{8,14},{10,8},{12,... | collective-permute-start | bytes 491528 | tf_op jit(solution)/shard_map/ppermute | solution.py:351
  22.4 1.5 %collective-permute-start.6 = (bf16[128,1280]{1,0:T(8,128)(2,1)S(1)}, bf16[128,1280]{1,0:T(8,128)(2,1)S(1)}, u32[]{:S(2)}, u32[]{:S(2)}) collective-permute-start(bf16[128,1280]{1,0:T(8,128)(2,1)S(1)} %get-tuple-element.61), channel_id=1, source_target_pairs={{0,16},{8,24},{16,0},{24,8},{1,17},{9,25},{17,1},{25,9},{2,18},{10... | collective-permute-start | bytes 983048 | tf_op jit(solution)/shard_map/ppermute | solution.py:351
  25.1 3.7 %collective-permute-start.10 = (bf16[128,640]{1,0:T(8,128)(2,1)S(1)}, bf16[128,640]{1,0:T(8,128)(2,1)S(1)}, u32[]{:S(2)}, u32[]{:S(2)}) collective-permute-start(bf16[128,640]{1,0:T(8,128)(2,1)S(1)} %constant_dynamic-update-slice_fusion.refs_4_), channel_id=1, source_target_pairs={{0,1},{1,0},{2,3},{3,2},{4,5},{5,4},{6,7},{7,6},{8,9},{9,8},{10,11... | collective-permute-start | bytes 491528 | tf_op jit(solution)/shard_map/ppermute | solution.py:359
  30.0 4.0 %collective-permute-start.12 = (bf16[128,640]{1,0:T(8,128)(2,1)S(1)}, bf16[128,640]{1,0:T(8,128)(2,1)S(1)}, u32[]{:S(2)}, u32[]{:S(2)}) collective-permute-start(bf16[128,640]{1,0:T(8,128)(2,1)S(1)} %collective-permute-done.8.refs_6_), channel_id=1, source_target_pairs={{0,1},{1,0},{2,3},{3,2},{4,5},{5,4},{6,7},{7,6},{8,9},{9,8},{10,11... | collective-permute-start | bytes 491528 | tf_op jit(solution)/shard_map/ppermute | solution.py:359
  34.0 1.6 %collective-permute-start.11 = (bf16[128,640]{1,0:T(8,128)(2,1)S(1)}, bf16[128,640]{1,0:T(8,128)(2,1)S(1)}, u32[]{:S(2)}, u32[]{:S(2)}) collective-permute-start(bf16[128,640]{1,0:T(8,128)(2,1)S(1)} %collective-permute-done.7.refs_5_), channel_id=1, source_target_pairs={{0,1},{1,0},{2,3},{3,2},{4,5},{5,4},{6,7},{7,6},{8,9},{9,8},{10,11... | collective-permute-start | bytes 491528 | tf_op jit(solution)/shard_map/ppermute | solution.py:359
  36.7 16.3 %pair.1 = (bf16[4,128,640]{2,1,0:T(8,128)(2,1)}, bf16[4,128,640]{2,1,0:T(8,128)(2,1)}, bf16[128,512]{1,0:T(8,128)(2,1)}, bf16[128,512]{1,0:T(8,128)(2,1)}, bf16[...) custom-call(s32[4]{0:T(128)S(1)} %pad_add_fusion.where_ref, ...), custom_call_target="tpu_custom_call" | custom-call | flops 8000000000 | bytes 10000000 | tf_op jit(solution)/shard_map/pair/pallas_call | solution.py:203
  53.0 8.4 %all-to-all-start = ((bf16[8,64,1024]{2,1,0:T(8,128)(2,1)}), bf16[8,64,1024]{2,1,0:T(8,128)(2,1)S(1)}, u32[]{:S(2)}, u32[]{:S(2)}) async-start(bf16[8,64,1024]{2,1,0:T(8,128)(2,1)} %bitcast.22), calls=%async_computation | async-start | bytes 2097152 | tf_op jit(solution)/shard_map/all_to_all | solution.py:347
  62.1 1.7 %collective-permute-done.14 = bf16[4,128,640]{2,1,0:T(8,128)(2,1)S(1)} collective-permute-done((bf16[4,128,640]{2,1,0:T(8,128)(2,1)S(1)}, bf16[4,128,640]{2,1,0:T(8,128)(2,1)S(1)}, u32[]{:S(2)}, u32[]{:S(2)}) %collective-permute-start.14) | collective-permute-done | bytes 655392 | tf_op jit(solution)/shard_map/ppermute | solution.py:359
  65.2 1.5 %collective-permute-start.17 = (bf16[128,640]{1,0:T(8,128)(2,1)S(1)}, bf16[128,640]{1,0:T(8,128)(2,1)S(1)}, u32[]{:S(2)}, u32[]{:S(2)}) collective-permute-start(bf16[128,640]{1,0:T(8,128)(2,1)S(1)} %get-tuple-element.101), channel_id=1, source_target_pairs={{0,24},{8,0},{16,8},{24,16},{1,25},{9,1},{17,9},{25,17},{2,26},{10... | collective-permute-start | bytes 491528 | tf_op jit(solution)/shard_map/ppermute | solution.py:351
  67.4 3.2 %collective-permute-done.15 = bf16[128,640]{1,0:T(8,128)(2,1)S(1)} collective-permute-done((bf16[128,640]{1,0:T(8,128)(2,1)S(1)}, bf16[128,640]{1,0:T(8,128)(2,1)S(1)}, u32[]{:S(2)}, u32[]{:S(2)}) %collective-permute-start.15) | collective-permute-done | bytes 163872 | tf_op jit(solution)/shard_map/ppermute | solution.py:351
  70.6 4.2 %collective-permute-done.16 = bf16[128,640]{1,0:T(8,128)(2,1)S(1)} collective-permute-done((bf16[128,640]{1,0:T(8,128)(2,1)S(1)}, bf16[128,640]{1,0:T(8,128)(2,1)S(1)}, u32[]{:S(2)}, u32[]{:S(2)}) %collective-permute-start.16) | collective-permute-done | bytes 163872 | tf_op jit(solution)/shard_map/ppermute | solution.py:351
  77.1 2.0 %collective-permute-start.22 = (bf16[128,512]{1,0:T(8,128)(2,1)S(1)}, bf16[128,512]{1,0:T(8,128)(2,1)S(1)}, u32[]{:S(2)}, u32[]{:S(2)}) collective-permute-start(bf16[128,512]{1,0:T(8,128)(2,1)S(1)} %copy-done.5), channel_id=1, source_target_pairs={{0,16},{8,24},{16,0},{24,8},{1,17},{9,25},{17,1},{25,9},{2,18},{10... | collective-permute-start | bytes 393224 | tf_op jit(solution)/shard_map/ppermute | solution.py:351
  80.5 3.4 %collective-permute-done.22.refs_2_ = bf16[128,512]{1,0:T(8,128)(2,1)S(1)} collective-permute-done((bf16[128,512]{1,0:T(8,128)(2,1)S(1)}, bf16[128,512]{1,0:T(8,128)(2,1)S(1)}, u32[]{:S(2)}, u32[]{:S(2)}) %collective-permute-start.22) | collective-permute-done | bytes 131104 | tf_op jit(solution)/shard_map/ppermute | solution.py:351
  83.9 1.4 %collective-permute-done.23.refs_3_ = bf16[128,512]{1,0:T(8,128)(2,1)S(1)} collective-permute-done((bf16[128,512]{1,0:T(8,128)(2,1)S(1)}, bf16[128,512]{1,0:T(8,128)(2,1)S(1)}, u32[]{:S(2)}, u32[]{:S(2)}) %collective-permute-start.23) | collective-permute-done | bytes 131104 | tf_op jit(solution)/shard_map/ppermute | solution.py:351
  88.0 2.6 %all-to-all-done.sent_ref = bf16[8,64,1024]{2,1,0:T(8,128)(2,1)S(1)} async-done(((bf16[8,64,1024]{2,1,0:T(8,128)(2,1)}), bf16[8,64,1024]{2,1,0:T(8,128)(2,1)S(1)}, u32[]{:S(2)}, u32[]{:S(2)}) %all-to-all-start) | async-done | bytes 1048608 | tf_op jit(solution)/shard_map/all_to_all | solution.py:347
  92.5 2.3 %collective-permute-start.26 = (bf16[16,1024]{1,0:T(8,128)(2,1)S(1)}, bf16[16,1024]{1,0:T(8,128)(2,1)S(1)}, u32[]{:S(2)}, u32[]{:S(2)}) collective-permute-start(bf16[16,1024]{1,0:T(8,128)(2,1)S(1)} %get-tuple-element.91), channel_id=1, source_target_pairs={{0,16},{8,24},{16,0},{24,8},{1,17},{9,25},{17,1},{25,9},{2,18},{10... | collective-permute-start | bytes 98312 | tf_op jit(solution)/shard_map/ppermute | solution.py:351
  95.3 1.5 %collective-permute-done.26.refs_2_ = bf16[16,1024]{1,0:T(8,128)(2,1)S(1)} collective-permute-done((bf16[16,1024]{1,0:T(8,128)(2,1)S(1)}, bf16[16,1024]{1,0:T(8,128)(2,1)S(1)}, u32[]{:S(2)}, u32[]{:S(2)}) %collective-permute-start.26) | collective-permute-done | bytes 32800 | tf_op jit(solution)/shard_map/ppermute | solution.py:351
  97.8 2.0 %collective-permute-start.28 = (f32[64,640]{1,0:T(8,128)S(1)}, f32[64,640]{1,0:T(8,128)S(1)}, u32[]{:S(2)}, u32[]{:S(2)}) collective-permute-start(f32[64,640]{1,0:T(8,128)S(1)} %convert_add_fusion.mine_ref), channel_id=1, source_target_pairs={{0,1},{1,0},{2,3},{3,2},{4,5},{5,4},{6,7},{7,6},{8,9},{9,8},{10,11... | collective-permute-start | bytes 491528 | tf_op jit(solution)/shard_map/ppermute | solution.py:359
  102.4 1.4 %join.1 = f32[576,128]{1,0:T(8,128)} custom-call(s32[4]{0:T(128)S(1)} %pad_add_fusion.where_ref, f32[64,640]{1,0:T(8,128)S(1)} %convert_add_fusion.mine_ref, f32[64,640]{1,0:T(8,128)S(1)} %collective-permute-done.28.other_ref), custom_call_target="tpu_custom_call" | custom-call | tf_op jit(solution)/shard_map/join/pallas_call | solution.py:271
  (72 shorter events, 23.5 us)
Async XLA Ops:
  1.9 6.5 %collective-permute-start = (bf16[16,640]{1,0:T(8,128)(2,1)S(1)}, bf16[16,640]{1,0:T(8,128)(2,1)S(1)}, u32[]{:S(2)}, u32[]{:S(2)}) collective-permute-start(bf16[16,640]{1,0:T(8,128)(2,1)S(1)} %pad_maximum_fusion), channel_id=1, source_target_pairs={{0,32},{32,64},{64,96},{96,128},{128,160},{160,192},{192,224},{1,3... | collective-permute-start | bytes 61448 | tf_op jit(solution)/shard_map/ppermute | solution.py:375
  8.5 11.3 %collective-permute-start.4 = (bf16[128,1280]{1,0:T(8,128)(2,1)S(1)}, bf16[128,1280]{1,0:T(8,128)(2,1)S(1)}, u32[]{:S(2)}, u32[]{:S(2)}) collective-permute-start(bf16[128,1280]{1,0:T(8,128)(2,1)S(1)} %get-tuple-element.58), channel_id=1, source_target_pairs={{0,8},{8,16},{16,24},{24,0},{1,9},{9,17},{17,25},{25,1},{2,10},{10... | collective-permute-start | bytes 983048 | tf_op jit(solution)/shard_map/ppermute | solution.py:351
  9.8 10.0 %collective-permute-start.5 = (bf16[128,1280]{1,0:T(8,128)(2,1)S(1)}, bf16[128,1280]{1,0:T(8,128)(2,1)S(1)}, u32[]{:S(2)}, u32[]{:S(2)}) collective-permute-start(bf16[128,1280]{1,0:T(8,128)(2,1)S(1)} %get-tuple-element.59), channel_id=1, source_target_pairs={{0,24},{8,0},{16,8},{24,16},{1,25},{9,1},{17,9},{25,17},{2,26},{10... | collective-permute-start | bytes 983048 | tf_op jit(solution)/shard_map/ppermute | solution.py:351
  11.3 7.3 %collective-permute-start.3 = (bf16[32,640]{1,0:T(8,128)(2,1)S(1)}, bf16[32,640]{1,0:T(8,128)(2,1)S(1)}, u32[]{:S(2)}, u32[]{:S(2)}) collective-permute-start(bf16[32,640]{1,0:T(8,128)(2,1)S(1)} %maximum_maximum_fusion), channel_id=1, source_target_pairs={{0,24},{8,0},{16,8},{24,16},{1,25},{9,1},{17,9},{25,17},{2,26},{10... | collective-permute-start | bytes 122888 | tf_op jit(solution)/shard_map/ppermute | solution.py:351
  12.7 7.1 %collective-permute-start.2 = (bf16[32,640]{1,0:T(8,128)(2,1)S(1)}, bf16[32,640]{1,0:T(8,128)(2,1)S(1)}, u32[]{:S(2)}, u32[]{:S(2)}) collective-permute-start(bf16[32,640]{1,0:T(8,128)(2,1)S(1)} %maximum_maximum_fusion), channel_id=1, source_target_pairs={{0,16},{8,24},{16,0},{24,8},{1,17},{9,25},{17,1},{25,9},{2,18},{10... | collective-permute-start | bytes 122888 | tf_op jit(solution)/shard_map/ppermute | solution.py:351
  13.1 6.7 %collective-permute-start.1 = (bf16[32,640]{1,0:T(8,128)(2,1)S(1)}, bf16[32,640]{1,0:T(8,128)(2,1)S(1)}, u32[]{:S(2)}, u32[]{:S(2)}) collective-permute-start(bf16[32,640]{1,0:T(8,128)(2,1)S(1)} %maximum_maximum_fusion), channel_id=1, source_target_pairs={{0,8},{8,16},{16,24},{24,0},{1,9},{9,17},{17,25},{25,1},{2,10},{10... | collective-permute-start | bytes 122888 | tf_op jit(solution)/shard_map/ppermute | solution.py:351
  19.9 8.9 %collective-permute-start.9 = (bf16[128,640]{1,0:T(8,128)(2,1)S(1)}, bf16[128,640]{1,0:T(8,128)(2,1)S(1)}, u32[]{:S(2)}, u32[]{:S(2)}) collective-permute-start(bf16[128,640]{1,0:T(8,128)(2,1)S(1)} %constant_dynamic-update-slice_fusion.refs_4_), channel_id=1, source_target_pairs={{0,6},{2,0},{4,2},{6,4},{1,7},{3,1},{5,3},{7,5},{8,14},{10,8},{12,... | collective-permute-start | bytes 491528 | tf_op jit(solution)/shard_map/ppermute | solution.py:351
  22.4 13.2 %collective-permute-start.6 = (bf16[128,1280]{1,0:T(8,128)(2,1)S(1)}, bf16[128,1280]{1,0:T(8,128)(2,1)S(1)}, u32[]{:S(2)}, u32[]{:S(2)}) collective-permute-start(bf16[128,1280]{1,0:T(8,128)(2,1)S(1)} %get-tuple-element.61), channel_id=1, source_target_pairs={{0,16},{8,24},{16,0},{24,8},{1,17},{9,25},{17,1},{25,9},{2,18},{10... | collective-permute-start | bytes 983048 | tf_op jit(solution)/shard_map/ppermute | solution.py:351
  23.9 6.1 %collective-permute-start.8 = (bf16[128,640]{1,0:T(8,128)(2,1)S(1)}, bf16[128,640]{1,0:T(8,128)(2,1)S(1)}, u32[]{:S(2)}, u32[]{:S(2)}) collective-permute-start(bf16[128,640]{1,0:T(8,128)(2,1)S(1)} %constant_dynamic-update-slice_fusion.refs_4_), channel_id=1, source_target_pairs={{0,4},{2,6},{4,0},{6,2},{1,5},{3,7},{5,1},{7,3},{8,12},{10,14},{12... | collective-permute-start | bytes 491528 | tf_op jit(solution)/shard_map/ppermute | solution.py:351
  24.4 9.6 %collective-permute-start.7 = (bf16[128,640]{1,0:T(8,128)(2,1)S(1)}, bf16[128,640]{1,0:T(8,128)(2,1)S(1)}, u32[]{:S(2)}, u32[]{:S(2)}) collective-permute-start(bf16[128,640]{1,0:T(8,128)(2,1)S(1)} %constant_dynamic-update-slice_fusion.refs_4_), channel_id=1, source_target_pairs={{0,2},{2,4},{4,6},{6,0},{1,3},{3,5},{5,7},{7,1},{8,10},{10,12},{12... | collective-permute-start | bytes 491528 | tf_op jit(solution)/shard_map/ppermute | solution.py:351
  25.1 10.6 %collective-permute-start.10 = (bf16[128,640]{1,0:T(8,128)(2,1)S(1)}, bf16[128,640]{1,0:T(8,128)(2,1)S(1)}, u32[]{:S(2)}, u32[]{:S(2)}) collective-permute-start(bf16[128,640]{1,0:T(8,128)(2,1)S(1)} %constant_dynamic-update-slice_fusion.refs_4_), channel_id=1, source_target_pairs={{0,1},{1,0},{2,3},{3,2},{4,5},{5,4},{6,7},{7,6},{8,9},{9,8},{10,11... | collective-permute-start | bytes 491528 | tf_op jit(solution)/shard_map/ppermute | solution.py:359
  28.8 6.9 %collective-permute-start.13 = (bf16[128,640]{1,0:T(8,128)(2,1)S(1)}, bf16[128,640]{1,0:T(8,128)(2,1)S(1)}, u32[]{:S(2)}, u32[]{:S(2)}) collective-permute-start(bf16[128,640]{1,0:T(8,128)(2,1)S(1)} %collective-permute-done.9.refs_7_), channel_id=1, source_target_pairs={{0,1},{1,0},{2,3},{3,2},{4,5},{5,4},{6,7},{7,6},{8,9},{9,8},{10,11... | collective-permute-start | bytes 491528 | tf_op jit(solution)/shard_map/ppermute | solution.py:359
  30.0 5.7 %collective-permute-start.12 = (bf16[128,640]{1,0:T(8,128)(2,1)S(1)}, bf16[128,640]{1,0:T(8,128)(2,1)S(1)}, u32[]{:S(2)}, u32[]{:S(2)}) collective-permute-start(bf16[128,640]{1,0:T(8,128)(2,1)S(1)} %collective-permute-done.8.refs_6_), channel_id=1, source_target_pairs={{0,1},{1,0},{2,3},{3,2},{4,5},{5,4},{6,7},{7,6},{8,9},{9,8},{10,11... | collective-permute-start | bytes 491528 | tf_op jit(solution)/shard_map/ppermute | solution.py:359
  53.0 37.6 %all-to-all-start = ((bf16[8,64,1024]{2,1,0:T(8,128)(2,1)}), bf16[8,64,1024]{2,1,0:T(8,128)(2,1)S(1)}, u32[]{:S(2)}, u32[]{:S(2)}) async-start(bf16[8,64,1024]{2,1,0:T(8,128)(2,1)} %bitcast.22), calls=%async_computation | async-start | bytes 2097152 | tf_op jit(solution)/shard_map/all_to_all | solution.py:347
  63.9 6.7 %collective-permute-start.15 = (bf16[128,640]{1,0:T(8,128)(2,1)S(1)}, bf16[128,640]{1,0:T(8,128)(2,1)S(1)}, u32[]{:S(2)}, u32[]{:S(2)}) collective-permute-start(bf16[128,640]{1,0:T(8,128)(2,1)S(1)} %get-tuple-element.100), channel_id=1, source_target_pairs={{0,8},{8,16},{16,24},{24,0},{1,9},{9,17},{17,25},{25,1},{2,10},{10... | collective-permute-start | bytes 491528 | tf_op jit(solution)/shard_map/ppermute | solution.py:351
  65.2 5.5 %collective-permute-start.17 = (bf16[128,640]{1,0:T(8,128)(2,1)S(1)}, bf16[128,640]{1,0:T(8,128)(2,1)S(1)}, u32[]{:S(2)}, u32[]{:S(2)}) collective-permute-start(bf16[128,640]{1,0:T(8,128)(2,1)S(1)} %get-tuple-element.101), channel_id=1, source_target_pairs={{0,24},{8,0},{16,8},{24,16},{1,25},{9,1},{17,9},{25,17},{2,26},{10... | collective-permute-start | bytes 491528 | tf_op jit(solution)/shard_map/ppermute | solution.py:351
  66.7 8.2 %collective-permute-start.16 = (bf16[128,640]{1,0:T(8,128)(2,1)S(1)}, bf16[128,640]{1,0:T(8,128)(2,1)S(1)}, u32[]{:S(2)}, u32[]{:S(2)}) collective-permute-start(bf16[128,640]{1,0:T(8,128)(2,1)S(1)} %get-tuple-element.102), channel_id=1, source_target_pairs={{0,16},{8,24},{16,0},{24,8},{1,17},{9,25},{17,1},{25,9},{2,18},{10... | collective-permute-start | bytes 491528 | tf_op jit(solution)/shard_map/ppermute | solution.py:351
  75.0 5.4 %collective-permute-start.21 = (bf16[128,512]{1,0:T(8,128)(2,1)S(1)}, bf16[128,512]{1,0:T(8,128)(2,1)S(1)}, u32[]{:S(2)}, u32[]{:S(2)}) collective-permute-start(bf16[128,512]{1,0:T(8,128)(2,1)S(1)} %copy-done.6), channel_id=1, source_target_pairs={{0,8},{8,16},{16,24},{24,0},{1,9},{9,17},{17,25},{25,1},{2,10},{10... | collective-permute-start | bytes 393224 | tf_op jit(solution)/shard_map/ppermute | solution.py:351
  75.6 9.7 %collective-permute-start.20 = (bf16[128,640]{1,0:T(8,128)(2,1)S(1)}, bf16[128,640]{1,0:T(8,128)(2,1)S(1)}, u32[]{:S(2)}, u32[]{:S(2)}) collective-permute-start(bf16[128,640]{1,0:T(8,128)(2,1)S(1)} %fusion.2.refs_0_), channel_id=1, source_target_pairs={{0,6},{2,0},{4,2},{6,4},{1,7},{3,1},{5,3},{7,5},{8,14},{10,8},{12,... | collective-permute-start | bytes 491528 | tf_op jit(solution)/shard_map/ppermute | solution.py:351
  75.9 9.4 %collective-permute-start.19 = (bf16[128,640]{1,0:T(8,128)(2,1)S(1)}, bf16[128,640]{1,0:T(8,128)(2,1)S(1)}, u32[]{:S(2)}, u32[]{:S(2)}) collective-permute-start(bf16[128,640]{1,0:T(8,128)(2,1)S(1)} %fusion.2.refs_0_), channel_id=1, source_target_pairs={{0,4},{2,6},{4,0},{6,2},{1,5},{3,7},{5,1},{7,3},{8,12},{10,14},{12... | collective-permute-start | bytes 491528 | tf_op jit(solution)/shard_map/ppermute | solution.py:351
  76.4 9.6 %collective-permute-start.18 = (bf16[128,640]{1,0:T(8,128)(2,1)S(1)}, bf16[128,640]{1,0:T(8,128)(2,1)S(1)}, u32[]{:S(2)}, u32[]{:S(2)}) collective-permute-start(bf16[128,640]{1,0:T(8,128)(2,1)S(1)} %fusion.2.refs_0_), channel_id=1, source_target_pairs={{0,2},{2,4},{4,6},{6,0},{1,3},{3,5},{5,7},{7,1},{8,10},{10,12},{12... | collective-permute-start | bytes 491528 | tf_op jit(solution)/shard_map/ppermute | solution.py:351
  77.1 6.9 %collective-permute-start.22 = (bf16[128,512]{1,0:T(8,128)(2,1)S(1)}, bf16[128,512]{1,0:T(8,128)(2,1)S(1)}, u32[]{:S(2)}, u32[]{:S(2)}) collective-permute-start(bf16[128,512]{1,0:T(8,128)(2,1)S(1)} %copy-done.5), channel_id=1, source_target_pairs={{0,16},{8,24},{16,0},{24,8},{1,17},{9,25},{17,1},{25,9},{2,18},{10... | collective-permute-start | bytes 393224 | tf_op jit(solution)/shard_map/ppermute | solution.py:351
  80.4 4.9 %collective-permute-start.23 = (bf16[128,512]{1,0:T(8,128)(2,1)S(1)}, bf16[128,512]{1,0:T(8,128)(2,1)S(1)}, u32[]{:S(2)}, u32[]{:S(2)}) collective-permute-start(bf16[128,512]{1,0:T(8,128)(2,1)S(1)} %copy-done.4), channel_id=1, source_target_pairs={{0,24},{8,0},{16,8},{24,16},{1,25},{9,1},{17,9},{25,17},{2,26},{10... | collective-permute-start | bytes 393224 | tf_op jit(solution)/shard_map/ppermute | solution.py:351
  86.7 8.3 %collective-permute-start.24 = (bf16[64,640]{1,0:T(8,128)(2,1)S(1)}, bf16[64,640]{1,0:T(8,128)(2,1)S(1)}, u32[]{:S(2)}, u32[]{:S(2)}) collective-permute-start(bf16[64,640]{1,0:T(8,128)(2,1)S(1)} %get-tuple-element.87), channel_id=1, source_target_pairs={{32,0},{64,32},{96,64},{128,96},{160,128},{192,160},{224,192},{33,... | collective-permute-start | bytes 245768 | tf_op jit(solution)/shard_map/ppermute | solution.py:396
  (13 other events, 151.0 us)

commit v7 on v6

--- a/solution.py
+++ b/solution.py
@@ -393,10 +393,11 @@
     total, outs = lax.optimization_barrier((total.astype(BF16), outs))
     terms, outs = lax.optimization_barrier((fanned([total] * 4, "x"), fanned(outs, "y")))
     own, later = latent_call(place, terms)
-    later, dw = lax.optimization_barrier((lax.ppermute(later, "z", behind), fanned(dw, "y")))
+    attended = attended_call(place, outs)
+    later, attended = lax.optimization_barrier((lax.ppermute(later, "z", behind), attended))
+    dw = fanned(dw, "y")
     part = own + later.astype(F32)
     latent_grad = jnp.transpose(join_call(place, part, swapped(part)))
-    attended = attended_call(place, outs)
     key_grad, value_grad = weight_call(place, dw)
     return attended, latent_grad, key_grad, value_grad
 

time: 104 us -> 102 us (0.981)
  waiting for transfers between devices: 28.5 us -> 25.3 us
    ppermute x1, waiting for transfers between devices: 0.01 us -> 2.8 us  [per_device(): lax.ppermute(later, 'z', behind)]
    all_to_all x1, waiting for transfers between devices: 2.59 us -> 0.01 us  [exchanged(): return lax.all_to_all(x, axes, split_axis=0, concat_axis=0, tiled=True)]
    ppermute x6, waiting for transfers between devices: 2.74 us -> 1.02 us  [swapped(): return lax.ppermute(value, 'core', [(0, 1), (1, 0)])]
    ppermute x21, waiting for transfers between devices: 23.1 us -> 21.5 us  [moved(): lax.ppermute(value, along, [(i, (i + step) % size) for i in range(size)])]
    ppermute x6, starting transfers between devices: 13.3 us -> 14.6 us  [swapped(): return lax.ppermute(value, 'core', [(0, 1), (1, 0)])]
  transfers between devices with their start and end apart: 30 -> 30, of which waited for: 14 -> 12; matrix products, arithmetic and copies ran while one was open for 0% -> 0% of each run, Pallas kernels for 6% -> 6%
where the time goes in v7:
time: 102 us
  starting transfers between devices  50.1 us (49%)
  waiting for transfers between devices  25.3 us (25%)
  Pallas kernels  23.8 us (23%)
  other arithmetic  1.28 us (1%)
    ppermute x21, starting transfers between devices, moved(): lax.ppermute(value, along, [(i, (i + step) % size) for i in range(size)])  21.5 us
    ppermute x21, waiting for transfers between devices, moved(): lax.ppermute(value, along, [(i, (i + step) % size) for i in range(size)])  21.5 us
    pallas_call x1, Pallas kernels, pair_call(): pl.pallas_call(pair_kernel, grid_spec=pltpu.PrefetchScalarGridSpec(num_sc...  16.3 us
    ppermute x6, starting transfers between devices, swapped(): return lax.ppermute(value, 'core', [(0, 1), (1, 0)])  14.6 us
    all_to_all x1, starting transfers between devices, exchanged(): return lax.all_to_all(x, axes, split_axis=0, concat_axis=0, tiled=True)  8.34 us
    ppermute x1, starting transfers between devices, per_device(): earlier = lax.ppermute(pay, 'z', ahead)  4.37 us
    ppermute x1, waiting for transfers between devices, per_device(): lax.ppermute(later, 'z', behind)  2.8 us
    pallas_call x1, Pallas kernels, pack_call(): pl.pallas_call(pack_kernel, in_specs=[pl.BlockSpec(memory_space=pltpu.SME...  2.06 us
  transfers between devices with their start and end apart: 30, of which 12 were waited for; matrix products, arithmetic and copies ran while one was open for 0% of the time, Pallas kernels for 6%

profile of v7, /device:TPU:1, one launch (start us, length us, event | category | flops | bytes accessed | tf_op | source)
XLA Modules:
  0.0 101.8 jit_solution(17369735480662231213)
XLA Ops:
  1.9 4.4 %collective-permute-start = (bf16[16,640]{1,0:T(8,128)(2,1)S(1)}, bf16[16,640]{1,0:T(8,128)(2,1)S(1)}, u32[]{:S(2)}, u32[]{:S(2)}) collective-permute-start(bf16[16,640]{1,0:T(8,128)(2,1)S(1)} %pad_maximum_fusion), channel_id=1, source_target_pairs={{0,32},{32,64},{64,96},{96,128},{128,160},{160,192},{192,224},{1,3... | collective-permute-start | bytes 61448 | tf_op jit(solution)/shard_map/ppermute | solution.py:375
  6.3 2.1 %pack.1 = (bf16[128,1280]{1,0:T(8,128)(2,1)S(1)}, bf16[128,1280]{1,0:T(8,128)(2,1)S(1)}, bf16[128,1280]{1,0:T(8,128)(2,1)S(1)}, bf16[128,1280]{1,0:T(8,128)(2,1)S(1)}) custom-call(s32[4]{0:T(128)S(1)} %pad_add_fusion.where_ref, bf16[128,3072]{1,0:T(8,128)(2,1)} %q_ref.1, bf16[128,2048]{1,0:T(8,128)(2,1)} %g_ref.1), custom_call_target="tpu_custom_call" | custom-call | bytes 2600000 | tf_op jit(solution)/shard_map/pack/pallas_call | solution.py:71
  8.5 1.3 %collective-permute-start.4 = (bf16[128,1280]{1,0:T(8,128)(2,1)S(1)}, bf16[128,1280]{1,0:T(8,128)(2,1)S(1)}, u32[]{:S(2)}, u32[]{:S(2)}) collective-permute-start(bf16[128,1280]{1,0:T(8,128)(2,1)S(1)} %get-tuple-element.55), channel_id=1, source_target_pairs={{0,8},{8,16},{16,24},{24,0},{1,9},{9,17},{17,25},{25,1},{2,10},{10... | collective-permute-start | bytes 983048 | tf_op jit(solution)/shard_map/ppermute | solution.py:351
  9.8 1.5 %collective-permute-start.5 = (bf16[128,1280]{1,0:T(8,128)(2,1)S(1)}, bf16[128,1280]{1,0:T(8,128)(2,1)S(1)}, u32[]{:S(2)}, u32[]{:S(2)}) collective-permute-start(bf16[128,1280]{1,0:T(8,128)(2,1)S(1)} %get-tuple-element.56), channel_id=1, source_target_pairs={{0,24},{8,0},{16,8},{24,16},{1,25},{9,1},{17,9},{25,17},{2,26},{10... | collective-permute-start | bytes 983048 | tf_op jit(solution)/shard_map/ppermute | solution.py:351
  11.3 1.4 %collective-permute-start.3 = (bf16[32,640]{1,0:T(8,128)(2,1)S(1)}, bf16[32,640]{1,0:T(8,128)(2,1)S(1)}, u32[]{:S(2)}, u32[]{:S(2)}) collective-permute-start(bf16[32,640]{1,0:T(8,128)(2,1)S(1)} %maximum_maximum_fusion), channel_id=1, source_target_pairs={{0,24},{8,0},{16,8},{24,16},{1,25},{9,1},{17,9},{25,17},{2,26},{10... | collective-permute-start | bytes 122888 | tf_op jit(solution)/shard_map/ppermute | solution.py:351
  13.8 4.9 %collective-permute-done.3 = bf16[32,640]{1,0:T(8,128)(2,1)S(1)} collective-permute-done((bf16[32,640]{1,0:T(8,128)(2,1)S(1)}, bf16[32,640]{1,0:T(8,128)(2,1)S(1)}, u32[]{:S(2)}, u32[]{:S(2)}) %collective-permute-start.3) | collective-permute-done | bytes 40992 | tf_op jit(solution)/shard_map/ppermute | solution.py:351
  19.9 2.6 %collective-permute-start.9 = (bf16[128,640]{1,0:T(8,128)(2,1)S(1)}, bf16[128,640]{1,0:T(8,128)(2,1)S(1)}, u32[]{:S(2)}, u32[]{:S(2)}) collective-permute-start(bf16[128,640]{1,0:T(8,128)(2,1)S(1)} %constant_dynamic-update-slice_fusion.refs_4_), channel_id=1, source_target_pairs={{0,6},{2,0},{4,2},{6,4},{1,7},{3,1},{5,3},{7,5},{8,14},{10,8},{12,... | collective-permute-start | bytes 491528 | tf_op jit(solution)/shard_map/ppermute | solution.py:351
  22.4 1.5 %collective-permute-start.6 = (bf16[128,1280]{1,0:T(8,128)(2,1)S(1)}, bf16[128,1280]{1,0:T(8,128)(2,1)S(1)}, u32[]{:S(2)}, u32[]{:S(2)}) collective-permute-start(bf16[128,1280]{1,0:T(8,128)(2,1)S(1)} %get-tuple-element.58), channel_id=1, source_target_pairs={{0,16},{8,24},{16,0},{24,8},{1,17},{9,25},{17,1},{25,9},{2,18},{10... | collective-permute-start | bytes 983048 | tf_op jit(solution)/shard_map/ppermute | solution.py:351
  25.1 3.7 %collective-permute-start.10 = (bf16[128,640]{1,0:T(8,128)(2,1)S(1)}, bf16[128,640]{1,0:T(8,128)(2,1)S(1)}, u32[]{:S(2)}, u32[]{:S(2)}) collective-permute-start(bf16[128,640]{1,0:T(8,128)(2,1)S(1)} %constant_dynamic-update-slice_fusion.refs_4_), channel_id=1, source_target_pairs={{0,1},{1,0},{2,3},{3,2},{4,5},{5,4},{6,7},{7,6},{8,9},{9,8},{10,11... | collective-permute-start | bytes 491528 | tf_op jit(solution)/shard_map/ppermute | solution.py:359
  30.0 4.0 %collective-permute-start.12 = (bf16[128,640]{1,0:T(8,128)(2,1)S(1)}, bf16[128,640]{1,0:T(8,128)(2,1)S(1)}, u32[]{:S(2)}, u32[]{:S(2)}) collective-permute-start(bf16[128,640]{1,0:T(8,128)(2,1)S(1)} %collective-permute-done.8.refs_6_), channel_id=1, source_target_pairs={{0,1},{1,0},{2,3},{3,2},{4,5},{5,4},{6,7},{7,6},{8,9},{9,8},{10,11... | collective-permute-start | bytes 491528 | tf_op jit(solution)/shard_map/ppermute | solution.py:359
  34.0 1.6 %collective-permute-start.11 = (bf16[128,640]{1,0:T(8,128)(2,1)S(1)}, bf16[128,640]{1,0:T(8,128)(2,1)S(1)}, u32[]{:S(2)}, u32[]{:S(2)}) collective-permute-start(bf16[128,640]{1,0:T(8,128)(2,1)S(1)} %collective-permute-done.7.refs_5_), channel_id=1, source_target_pairs={{0,1},{1,0},{2,3},{3,2},{4,5},{5,4},{6,7},{7,6},{8,9},{9,8},{10,11... | collective-permute-start | bytes 491528 | tf_op jit(solution)/shard_map/ppermute | solution.py:359
  36.7 16.3 %pair.1 = (bf16[4,128,640]{2,1,0:T(8,128)(2,1)}, bf16[4,128,640]{2,1,0:T(8,128)(2,1)}, bf16[128,512]{1,0:T(8,128)(2,1)}, bf16[128,512]{1,0:T(8,128)(2,1)}, bf16[...) custom-call(s32[4]{0:T(128)S(1)} %pad_add_fusion.where_ref, ...), custom_call_target="tpu_custom_call" | custom-call | flops 8000000000 | bytes 10000000 | tf_op jit(solution)/shard_map/pair/pallas_call | solution.py:203
  53.3 8.3 %all-to-all-start = ((bf16[8,64,1024]{2,1,0:T(8,128)(2,1)}), bf16[8,64,1024]{2,1,0:T(8,128)(2,1)S(1)}, u32[]{:S(2)}, u32[]{:S(2)}) async-start(bf16[8,64,1024]{2,1,0:T(8,128)(2,1)} %bitcast.22), calls=%async_computation | async-start | bytes 2097152 | tf_op jit(solution)/shard_map/all_to_all | solution.py:347
  63.0 1.5 %collective-permute-start.17 = (bf16[128,640]{1,0:T(8,128)(2,1)S(1)}, bf16[128,640]{1,0:T(8,128)(2,1)S(1)}, u32[]{:S(2)}, u32[]{:S(2)}) collective-permute-start(bf16[128,640]{1,0:T(8,128)(2,1)S(1)} %get-tuple-element.95), channel_id=1, source_target_pairs={{0,24},{8,0},{16,8},{24,16},{1,25},{9,1},{17,9},{25,17},{2,26},{10... | collective-permute-start | bytes 491528 | tf_op jit(solution)/shard_map/ppermute | solution.py:351
  65.3 3.2 %collective-permute-done.15 = bf16[128,640]{1,0:T(8,128)(2,1)S(1)} collective-permute-done((bf16[128,640]{1,0:T(8,128)(2,1)S(1)}, bf16[128,640]{1,0:T(8,128)(2,1)S(1)}, u32[]{:S(2)}, u32[]{:S(2)}) %collective-permute-start.15) | collective-permute-done | bytes 163872 | tf_op jit(solution)/shard_map/ppermute | solution.py:351
  68.5 4.2 %collective-permute-done.16 = bf16[128,640]{1,0:T(8,128)(2,1)S(1)} collective-permute-done((bf16[128,640]{1,0:T(8,128)(2,1)S(1)}, bf16[128,640]{1,0:T(8,128)(2,1)S(1)}, u32[]{:S(2)}, u32[]{:S(2)}) %collective-permute-start.16) | collective-permute-done | bytes 163872 | tf_op jit(solution)/shard_map/ppermute | solution.py:351
  74.9 2.0 %collective-permute-start.22 = (bf16[128,512]{1,0:T(8,128)(2,1)S(1)}, bf16[128,512]{1,0:T(8,128)(2,1)S(1)}, u32[]{:S(2)}, u32[]{:S(2)}) collective-permute-start(bf16[128,512]{1,0:T(8,128)(2,1)S(1)} %copy-done.4), channel_id=1, source_target_pairs={{0,16},{8,24},{16,0},{24,8},{1,17},{9,25},{17,1},{25,9},{2,18},{10... | collective-permute-start | bytes 393224 | tf_op jit(solution)/shard_map/ppermute | solution.py:351
  76.9 1.3 %collective-permute-done.21.refs_1_ = bf16[128,512]{1,0:T(8,128)(2,1)S(1)} collective-permute-done((bf16[128,512]{1,0:T(8,128)(2,1)S(1)}, bf16[128,512]{1,0:T(8,128)(2,1)S(1)}, u32[]{:S(2)}, u32[]{:S(2)}) %collective-permute-start.21) | collective-permute-done | bytes 131104 | tf_op jit(solution)/shard_map/ppermute | solution.py:351
  78.3 3.5 %collective-permute-done.22.refs_2_ = bf16[128,512]{1,0:T(8,128)(2,1)S(1)} collective-permute-done((bf16[128,512]{1,0:T(8,128)(2,1)S(1)}, bf16[128,512]{1,0:T(8,128)(2,1)S(1)}, u32[]{:S(2)}, u32[]{:S(2)}) %collective-permute-start.22) | collective-permute-done | bytes 131104 | tf_op jit(solution)/shard_map/ppermute | solution.py:351
  85.8 1.4 %attended.1 = bf16[128,2048]{1,0:T(8,128)(2,1)} custom-call(s32[4]{0:T(128)S(1)} %pad_add_fusion.where_ref, bf16[128,512]{1,0:T(8,128)(2,1)S(1)} %copy-done.1, bf16[128,512]{1,0:T(8,128)(2,1)S(1)} %collective-permute-done.21.refs_1_, bf16[128,512]{1,0:T(8,128)(2,1)S(1)} %collective-permute-done.22.refs_2_, bf16[128,512]{1,0:T(8,128)(2,1)S(1)} %collective-permute-done.23.refs_3_), custom_call_target="tpu_custom_call" | custom-call | tf_op jit(solution)/shard_map/attended/pallas_call | solution.py:291
  87.1 2.8 %collective-permute-done.24 = bf16[64,640]{1,0:T(8,128)(2,1)S(1)} collective-permute-done((bf16[64,640]{1,0:T(8,128)(2,1)S(1)}, bf16[64,640]{1,0:T(8,128)(2,1)S(1)}, u32[]{:S(2)}, u32[]{:S(2)}) %collective-permute-start.24) | collective-permute-done | bytes 81952 | tf_op jit(solution)/shard_map/ppermute | solution.py:397
  89.9 3.6 %collective-permute-start.25 = (f32[64,640]{1,0:T(8,128)S(1)}, f32[64,640]{1,0:T(8,128)S(1)}, u32[]{:S(2)}, u32[]{:S(2)}) collective-permute-start(f32[64,640]{1,0:T(8,128)S(1)} %convert_add_fusion.mine_ref), channel_id=1, source_target_pairs={{0,1},{1,0},{2,3},{3,2},{4,5},{5,4},{6,7},{7,6},{8,9},{9,8},{10,11... | collective-permute-start | bytes 491528 | tf_op jit(solution)/shard_map/ppermute | solution.py:359
  94.4 3.4 %collective-permute-start.27 = (bf16[16,1024]{1,0:T(8,128)(2,1)S(1)}, bf16[16,1024]{1,0:T(8,128)(2,1)S(1)}, u32[]{:S(2)}, u32[]{:S(2)}) collective-permute-start(bf16[16,1024]{1,0:T(8,128)(2,1)S(1)} %get-tuple-element.90), channel_id=1, source_target_pairs={{0,16},{8,24},{16,0},{24,8},{1,17},{9,25},{17,1},{25,9},{2,18},{10... | collective-permute-start | bytes 98312 | tf_op jit(solution)/shard_map/ppermute | solution.py:351
  97.7 1.4 %join.1 = f32[576,128]{1,0:T(8,128)} custom-call(s32[4]{0:T(128)S(1)} %pad_add_fusion.where_ref, f32[64,640]{1,0:T(8,128)S(1)} %convert_add_fusion.mine_ref, f32[64,640]{1,0:T(8,128)S(1)} %collective-permute-done.25.other_ref), custom_call_target="tpu_custom_call" | custom-call | tf_op jit(solution)/shard_map/join/pallas_call | solution.py:271
  (70 shorter events, 19.1 us)
Async XLA Ops:
  1.9 6.5 %collective-permute-start = (bf16[16,640]{1,0:T(8,128)(2,1)S(1)}, bf16[16,640]{1,0:T(8,128)(2,1)S(1)}, u32[]{:S(2)}, u32[]{:S(2)}) collective-permute-start(bf16[16,640]{1,0:T(8,128)(2,1)S(1)} %pad_maximum_fusion), channel_id=1, source_target_pairs={{0,32},{32,64},{64,96},{96,128},{128,160},{160,192},{192,224},{1,3... | collective-permute-start | bytes 61448 | tf_op jit(solution)/shard_map/ppermute | solution.py:375
  8.5 11.3 %collective-permute-start.4 = (bf16[128,1280]{1,0:T(8,128)(2,1)S(1)}, bf16[128,1280]{1,0:T(8,128)(2,1)S(1)}, u32[]{:S(2)}, u32[]{:S(2)}) collective-permute-start(bf16[128,1280]{1,0:T(8,128)(2,1)S(1)} %get-tuple-element.55), channel_id=1, source_target_pairs={{0,8},{8,16},{16,24},{24,0},{1,9},{9,17},{17,25},{25,1},{2,10},{10... | collective-permute-start | bytes 983048 | tf_op jit(solution)/shard_map/ppermute | solution.py:351
  9.8 10.0 %collective-permute-start.5 = (bf16[128,1280]{1,0:T(8,128)(2,1)S(1)}, bf16[128,1280]{1,0:T(8,128)(2,1)S(1)}, u32[]{:S(2)}, u32[]{:S(2)}) collective-permute-start(bf16[128,1280]{1,0:T(8,128)(2,1)S(1)} %get-tuple-element.56), channel_id=1, source_target_pairs={{0,24},{8,0},{16,8},{24,16},{1,25},{9,1},{17,9},{25,17},{2,26},{10... | collective-permute-start | bytes 983048 | tf_op jit(solution)/shard_map/ppermute | solution.py:351
  11.3 7.3 %collective-permute-start.3 = (bf16[32,640]{1,0:T(8,128)(2,1)S(1)}, bf16[32,640]{1,0:T(8,128)(2,1)S(1)}, u32[]{:S(2)}, u32[]{:S(2)}) collective-permute-start(bf16[32,640]{1,0:T(8,128)(2,1)S(1)} %maximum_maximum_fusion), channel_id=1, source_target_pairs={{0,24},{8,0},{16,8},{24,16},{1,25},{9,1},{17,9},{25,17},{2,26},{10... | collective-permute-start | bytes 122888 | tf_op jit(solution)/shard_map/ppermute | solution.py:351
  12.7 7.1 %collective-permute-start.2 = (bf16[32,640]{1,0:T(8,128)(2,1)S(1)}, bf16[32,640]{1,0:T(8,128)(2,1)S(1)}, u32[]{:S(2)}, u32[]{:S(2)}) collective-permute-start(bf16[32,640]{1,0:T(8,128)(2,1)S(1)} %maximum_maximum_fusion), channel_id=1, source_target_pairs={{0,16},{8,24},{16,0},{24,8},{1,17},{9,25},{17,1},{25,9},{2,18},{10... | collective-permute-start | bytes 122888 | tf_op jit(solution)/shard_map/ppermute | solution.py:351
  13.1 6.7 %collective-permute-start.1 = (bf16[32,640]{1,0:T(8,128)(2,1)S(1)}, bf16[32,640]{1,0:T(8,128)(2,1)S(1)}, u32[]{:S(2)}, u32[]{:S(2)}) collective-permute-start(bf16[32,640]{1,0:T(8,128)(2,1)S(1)} %maximum_maximum_fusion), channel_id=1, source_target_pairs={{0,8},{8,16},{16,24},{24,0},{1,9},{9,17},{17,25},{25,1},{2,10},{10... | collective-permute-start | bytes 122888 | tf_op jit(solution)/shard_map/ppermute | solution.py:351
  19.9 8.9 %collective-permute-start.9 = (bf16[128,640]{1,0:T(8,128)(2,1)S(1)}, bf16[128,640]{1,0:T(8,128)(2,1)S(1)}, u32[]{:S(2)}, u32[]{:S(2)}) collective-permute-start(bf16[128,640]{1,0:T(8,128)(2,1)S(1)} %constant_dynamic-update-slice_fusion.refs_4_), channel_id=1, source_target_pairs={{0,6},{2,0},{4,2},{6,4},{1,7},{3,1},{5,3},{7,5},{8,14},{10,8},{12,... | collective-permute-start | bytes 491528 | tf_op jit(solution)/shard_map/ppermute | solution.py:351
  22.4 13.2 %collective-permute-start.6 = (bf16[128,1280]{1,0:T(8,128)(2,1)S(1)}, bf16[128,1280]{1,0:T(8,128)(2,1)S(1)}, u32[]{:S(2)}, u32[]{:S(2)}) collective-permute-start(bf16[128,1280]{1,0:T(8,128)(2,1)S(1)} %get-tuple-element.58), channel_id=1, source_target_pairs={{0,16},{8,24},{16,0},{24,8},{1,17},{9,25},{17,1},{25,9},{2,18},{10... | collective-permute-start | bytes 983048 | tf_op jit(solution)/shard_map/ppermute | solution.py:351
  23.9 6.1 %collective-permute-start.8 = (bf16[128,640]{1,0:T(8,128)(2,1)S(1)}, bf16[128,640]{1,0:T(8,128)(2,1)S(1)}, u32[]{:S(2)}, u32[]{:S(2)}) collective-permute-start(bf16[128,640]{1,0:T(8,128)(2,1)S(1)} %constant_dynamic-update-slice_fusion.refs_4_), channel_id=1, source_target_pairs={{0,4},{2,6},{4,0},{6,2},{1,5},{3,7},{5,1},{7,3},{8,12},{10,14},{12... | collective-permute-start | bytes 491528 | tf_op jit(solution)/shard_map/ppermute | solution.py:351
  24.4 9.6 %collective-permute-start.7 = (bf16[128,640]{1,0:T(8,128)(2,1)S(1)}, bf16[128,640]{1,0:T(8,128)(2,1)S(1)}, u32[]{:S(2)}, u32[]{:S(2)}) collective-permute-start(bf16[128,640]{1,0:T(8,128)(2,1)S(1)} %constant_dynamic-update-slice_fusion.refs_4_), channel_id=1, source_target_pairs={{0,2},{2,4},{4,6},{6,0},{1,3},{3,5},{5,7},{7,1},{8,10},{10,12},{12... | collective-permute-start | bytes 491528 | tf_op jit(solution)/shard_map/ppermute | solution.py:351
  25.1 10.6 %collective-permute-start.10 = (bf16[128,640]{1,0:T(8,128)(2,1)S(1)}, bf16[128,640]{1,0:T(8,128)(2,1)S(1)}, u32[]{:S(2)}, u32[]{:S(2)}) collective-permute-start(bf16[128,640]{1,0:T(8,128)(2,1)S(1)} %constant_dynamic-update-slice_fusion.refs_4_), channel_id=1, source_target_pairs={{0,1},{1,0},{2,3},{3,2},{4,5},{5,4},{6,7},{7,6},{8,9},{9,8},{10,11... | collective-permute-start | bytes 491528 | tf_op jit(solution)/shard_map/ppermute | solution.py:359
  28.8 6.9 %collective-permute-start.13 = (bf16[128,640]{1,0:T(8,128)(2,1)S(1)}, bf16[128,640]{1,0:T(8,128)(2,1)S(1)}, u32[]{:S(2)}, u32[]{:S(2)}) collective-permute-start(bf16[128,640]{1,0:T(8,128)(2,1)S(1)} %collective-permute-done.9.refs_7_), channel_id=1, source_target_pairs={{0,1},{1,0},{2,3},{3,2},{4,5},{5,4},{6,7},{7,6},{8,9},{9,8},{10,11... | collective-permute-start | bytes 491528 | tf_op jit(solution)/shard_map/ppermute | solution.py:359
  30.0 5.7 %collective-permute-start.12 = (bf16[128,640]{1,0:T(8,128)(2,1)S(1)}, bf16[128,640]{1,0:T(8,128)(2,1)S(1)}, u32[]{:S(2)}, u32[]{:S(2)}) collective-permute-start(bf16[128,640]{1,0:T(8,128)(2,1)S(1)} %collective-permute-done.8.refs_6_), channel_id=1, source_target_pairs={{0,1},{1,0},{2,3},{3,2},{4,5},{5,4},{6,7},{7,6},{8,9},{9,8},{10,11... | collective-permute-start | bytes 491528 | tf_op jit(solution)/shard_map/ppermute | solution.py:359
  53.0 8.7 %collective-permute-start.14 = (bf16[4,128,640]{2,1,0:T(8,128)(2,1)}, bf16[4,128,640]{2,1,0:T(8,128)(2,1)S(1)}, u32[]{:S(2)}, u32[]{:S(2)}) collective-permute-start(bf16[4,128,640]{2,1,0:T(8,128)(2,1)} %get-tuple-element.65), channel_id=1, source_target_pairs={{0,1},{1,0},{2,3},{3,2},{4,5},{5,4},{6,7},{7,6},{8,9},{9,8},{10,11... | collective-permute-start | bytes 1966088 | tf_op jit(solution)/shard_map/ppermute | solution.py:359
  53.3 40.2 %all-to-all-start = ((bf16[8,64,1024]{2,1,0:T(8,128)(2,1)}), bf16[8,64,1024]{2,1,0:T(8,128)(2,1)S(1)}, u32[]{:S(2)}, u32[]{:S(2)}) async-start(bf16[8,64,1024]{2,1,0:T(8,128)(2,1)} %bitcast.22), calls=%async_computation | async-start | bytes 2097152 | tf_op jit(solution)/shard_map/all_to_all | solution.py:347
  61.8 6.6 %collective-permute-start.15 = (bf16[128,640]{1,0:T(8,128)(2,1)S(1)}, bf16[128,640]{1,0:T(8,128)(2,1)S(1)}, u32[]{:S(2)}, u32[]{:S(2)}) collective-permute-start(bf16[128,640]{1,0:T(8,128)(2,1)S(1)} %get-tuple-element.94), channel_id=1, source_target_pairs={{0,8},{8,16},{16,24},{24,0},{1,9},{9,17},{17,25},{25,1},{2,10},{10... | collective-permute-start | bytes 491528 | tf_op jit(solution)/shard_map/ppermute | solution.py:351
  63.0 5.4 %collective-permute-start.17 = (bf16[128,640]{1,0:T(8,128)(2,1)S(1)}, bf16[128,640]{1,0:T(8,128)(2,1)S(1)}, u32[]{:S(2)}, u32[]{:S(2)}) collective-permute-start(bf16[128,640]{1,0:T(8,128)(2,1)S(1)} %get-tuple-element.95), channel_id=1, source_target_pairs={{0,24},{8,0},{16,8},{24,16},{1,25},{9,1},{17,9},{25,17},{2,26},{10... | collective-permute-start | bytes 491528 | tf_op jit(solution)/shard_map/ppermute | solution.py:351
  64.6 8.1 %collective-permute-start.16 = (bf16[128,640]{1,0:T(8,128)(2,1)S(1)}, bf16[128,640]{1,0:T(8,128)(2,1)S(1)}, u32[]{:S(2)}, u32[]{:S(2)}) collective-permute-start(bf16[128,640]{1,0:T(8,128)(2,1)S(1)} %get-tuple-element.96), channel_id=1, source_target_pairs={{0,16},{8,24},{16,0},{24,8},{1,17},{9,25},{17,1},{25,9},{2,18},{10... | collective-permute-start | bytes 491528 | tf_op jit(solution)/shard_map/ppermute | solution.py:351
  73.4 9.6 %collective-permute-start.20 = (bf16[128,640]{1,0:T(8,128)(2,1)S(1)}, bf16[128,640]{1,0:T(8,128)(2,1)S(1)}, u32[]{:S(2)}, u32[]{:S(2)}) collective-permute-start(bf16[128,640]{1,0:T(8,128)(2,1)S(1)} %fusion.2.refs_0_), channel_id=1, source_target_pairs={{0,6},{2,0},{4,2},{6,4},{1,7},{3,1},{5,3},{7,5},{8,14},{10,8},{12,... | collective-permute-start | bytes 491528 | tf_op jit(solution)/shard_map/ppermute | solution.py:351
  73.7 9.3 %collective-permute-start.19 = (bf16[128,640]{1,0:T(8,128)(2,1)S(1)}, bf16[128,640]{1,0:T(8,128)(2,1)S(1)}, u32[]{:S(2)}, u32[]{:S(2)}) collective-permute-start(bf16[128,640]{1,0:T(8,128)(2,1)S(1)} %fusion.2.refs_0_), channel_id=1, source_target_pairs={{0,4},{2,6},{4,0},{6,2},{1,5},{3,7},{5,1},{7,3},{8,12},{10,14},{12... | collective-permute-start | bytes 491528 | tf_op jit(solution)/shard_map/ppermute | solution.py:351
  74.2 9.5 %collective-permute-start.18 = (bf16[128,640]{1,0:T(8,128)(2,1)S(1)}, bf16[128,640]{1,0:T(8,128)(2,1)S(1)}, u32[]{:S(2)}, u32[]{:S(2)}) collective-permute-start(bf16[128,640]{1,0:T(8,128)(2,1)S(1)} %fusion.2.refs_0_), channel_id=1, source_target_pairs={{0,2},{2,4},{4,6},{6,0},{1,3},{3,5},{5,7},{7,1},{8,10},{10,12},{12... | collective-permute-start | bytes 491528 | tf_op jit(solution)/shard_map/ppermute | solution.py:351
  74.9 6.9 %collective-permute-start.22 = (bf16[128,512]{1,0:T(8,128)(2,1)S(1)}, bf16[128,512]{1,0:T(8,128)(2,1)S(1)}, u32[]{:S(2)}, u32[]{:S(2)}) collective-permute-start(bf16[128,512]{1,0:T(8,128)(2,1)S(1)} %copy-done.4), channel_id=1, source_target_pairs={{0,16},{8,24},{16,0},{24,8},{1,17},{9,25},{17,1},{25,9},{2,18},{10... | collective-permute-start | bytes 393224 | tf_op jit(solution)/shard_map/ppermute | solution.py:351
  84.4 5.5 %collective-permute-start.24 = (bf16[64,640]{1,0:T(8,128)(2,1)S(1)}, bf16[64,640]{1,0:T(8,128)(2,1)S(1)}, u32[]{:S(2)}, u32[]{:S(2)}) collective-permute-start(bf16[64,640]{1,0:T(8,128)(2,1)S(1)} %get-tuple-element.79), channel_id=1, source_target_pairs={{32,0},{64,32},{96,64},{128,96},{160,128},{192,160},{224,192},{33,... | collective-permute-start | bytes 245768 | tf_op jit(solution)/shard_map/ppermute | solution.py:397
  89.9 7.8 %collective-permute-start.25 = (f32[64,640]{1,0:T(8,128)S(1)}, f32[64,640]{1,0:T(8,128)S(1)}, u32[]{:S(2)}, u32[]{:S(2)}) collective-permute-start(f32[64,640]{1,0:T(8,128)S(1)} %convert_add_fusion.mine_ref), channel_id=1, source_target_pairs={{0,1},{1,0},{2,3},{3,2},{4,5},{5,4},{6,7},{7,6},{8,9},{9,8},{10,11... | collective-permute-start | bytes 491528 | tf_op jit(solution)/shard_map/ppermute | solution.py:359
  (12 other events, 133.8 us)

commit v8 on v7

--- a/solution.py
+++ b/solution.py
@@ -390,7 +390,7 @@
     total = parts[0]
     for part in parts[1:]:
         total = total + part.astype(F32)
-    total, outs = lax.optimization_barrier((total.astype(BF16), outs))
+    total = total.astype(BF16)
     terms, outs = lax.optimization_barrier((fanned([total] * 4, "x"), fanned(outs, "y")))
     own, later = latent_call(place, terms)
     attended = attended_call(place, outs)

time: 102 us -> 101 us (level)
  waiting for transfers between devices: 25.3 us -> 23.5 us
    ppermute x21, waiting for transfers between devices: 21.5 us -> 19.7 us  [moved(): lax.ppermute(value, along, [(i, (i + step) % size) for i in range(size)])]
  transfers between devices with their start and end apart: 30 -> 30, of which waited for: 12 -> 11; matrix products, arithmetic and copies ran while one was open for 0% -> 0% of each run, Pallas kernels for 6% -> 6%
where the time goes in v8:
time: 101 us; the launch traced here: 100 us
  starting transfers between devices  50.1 us (50%)
  Pallas kernels  23.8 us (24%)
  waiting for transfers between devices  23.5 us (23%)
  other arithmetic  1.28 us (1%)
    ppermute x21, starting transfers between devices, moved(): lax.ppermute(value, along, [(i, (i + step) % size) for i in range(size)])  22.2 us
    ppermute x21, waiting for transfers between devices, moved(): lax.ppermute(value, along, [(i, (i + step) % size) for i in range(size)])  19.7 us
    pallas_call x1, Pallas kernels, pair_call(): pl.pallas_call(pair_kernel, grid_spec=pltpu.PrefetchScalarGridSpec(num_sc...  16.3 us
    ppermute x6, starting transfers between devices, swapped(): return lax.ppermute(value, 'core', [(0, 1), (1, 0)])  13.9 us
    all_to_all x1, starting transfers between devices, exchanged(): return lax.all_to_all(x, axes, split_axis=0, concat_axis=0, tiled=True)  8.33 us
    ppermute x1, starting transfers between devices, per_device(): earlier = lax.ppermute(pay, 'z', ahead)  4.37 us
    ppermute x1, waiting for transfers between devices, per_device(): lax.ppermute(later, 'z', behind)  2.8 us
    pallas_call x1, Pallas kernels, pack_call(): pl.pallas_call(pack_kernel, in_specs=[pl.BlockSpec(memory_space=pltpu.SME...  2.06 us
  transfers between devices with their start and end apart: 30, of which 11 were waited for; matrix products, arithmetic and copies ran while one was open for 0% of the time, Pallas kernels for 6%

profile of v8, /device:TPU:1, one launch (start us, length us, event | category | flops | bytes accessed | tf_op | source)
XLA Modules:
  0.0 100.0 jit_solution(10409705095183527439)
XLA Ops:
  1.9 4.4 %collective-permute-start = (bf16[16,640]{1,0:T(8,128)(2,1)S(1)}, bf16[16,640]{1,0:T(8,128)(2,1)S(1)}, u32[]{:S(2)}, u32[]{:S(2)}) collective-permute-start(bf16[16,640]{1,0:T(8,128)(2,1)S(1)} %pad_maximum_fusion), channel_id=1, source_target_pairs={{0,32},{32,64},{64,96},{96,128},{128,160},{160,192},{192,224},{1,3... | collective-permute-start | bytes 61448 | tf_op jit(solution)/shard_map/ppermute | solution.py:375
  6.3 2.1 %pack.1 = (bf16[128,1280]{1,0:T(8,128)(2,1)S(1)}, bf16[128,1280]{1,0:T(8,128)(2,1)S(1)}, bf16[128,1280]{1,0:T(8,128)(2,1)S(1)}, bf16[128,1280]{1,0:T(8,128)(2,1)S(1)}) custom-call(s32[4]{0:T(128)S(1)} %pad_add_fusion.where_ref, bf16[128,3072]{1,0:T(8,128)(2,1)} %q_ref.1, bf16[128,2048]{1,0:T(8,128)(2,1)} %g_ref.1), custom_call_target="tpu_custom_call" | custom-call | bytes 2600000 | tf_op jit(solution)/shard_map/pack/pallas_call | solution.py:71
  8.5 1.3 %collective-permute-start.4 = (bf16[128,1280]{1,0:T(8,128)(2,1)S(1)}, bf16[128,1280]{1,0:T(8,128)(2,1)S(1)}, u32[]{:S(2)}, u32[]{:S(2)}) collective-permute-start(bf16[128,1280]{1,0:T(8,128)(2,1)S(1)} %get-tuple-element.50), channel_id=1, source_target_pairs={{0,8},{8,16},{16,24},{24,0},{1,9},{9,17},{17,25},{25,1},{2,10},{10... | collective-permute-start | bytes 983048 | tf_op jit(solution)/shard_map/ppermute | solution.py:351
  9.8 1.5 %collective-permute-start.5 = (bf16[128,1280]{1,0:T(8,128)(2,1)S(1)}, bf16[128,1280]{1,0:T(8,128)(2,1)S(1)}, u32[]{:S(2)}, u32[]{:S(2)}) collective-permute-start(bf16[128,1280]{1,0:T(8,128)(2,1)S(1)} %get-tuple-element.51), channel_id=1, source_target_pairs={{0,24},{8,0},{16,8},{24,16},{1,25},{9,1},{17,9},{25,17},{2,26},{10... | collective-permute-start | bytes 983048 | tf_op jit(solution)/shard_map/ppermute | solution.py:351
  11.3 1.4 %collective-permute-start.3 = (bf16[32,640]{1,0:T(8,128)(2,1)S(1)}, bf16[32,640]{1,0:T(8,128)(2,1)S(1)}, u32[]{:S(2)}, u32[]{:S(2)}) collective-permute-start(bf16[32,640]{1,0:T(8,128)(2,1)S(1)} %maximum_maximum_fusion), channel_id=1, source_target_pairs={{0,24},{8,0},{16,8},{24,16},{1,25},{9,1},{17,9},{25,17},{2,26},{10... | collective-permute-start | bytes 122888 | tf_op jit(solution)/shard_map/ppermute | solution.py:351
  13.8 4.9 %collective-permute-done.3 = bf16[32,640]{1,0:T(8,128)(2,1)S(1)} collective-permute-done((bf16[32,640]{1,0:T(8,128)(2,1)S(1)}, bf16[32,640]{1,0:T(8,128)(2,1)S(1)}, u32[]{:S(2)}, u32[]{:S(2)}) %collective-permute-start.3) | collective-permute-done | bytes 40992 | tf_op jit(solution)/shard_map/ppermute | solution.py:351
  19.9 2.6 %collective-permute-start.9 = (bf16[128,640]{1,0:T(8,128)(2,1)S(1)}, bf16[128,640]{1,0:T(8,128)(2,1)S(1)}, u32[]{:S(2)}, u32[]{:S(2)}) collective-permute-start(bf16[128,640]{1,0:T(8,128)(2,1)S(1)} %constant_dynamic-update-slice_fusion.refs_4_), channel_id=1, source_target_pairs={{0,6},{2,0},{4,2},{6,4},{1,7},{3,1},{5,3},{7,5},{8,14},{10,8},{12,... | collective-permute-start | bytes 491528 | tf_op jit(solution)/shard_map/ppermute | solution.py:351
  22.4 1.5 %collective-permute-start.6 = (bf16[128,1280]{1,0:T(8,128)(2,1)S(1)}, bf16[128,1280]{1,0:T(8,128)(2,1)S(1)}, u32[]{:S(2)}, u32[]{:S(2)}) collective-permute-start(bf16[128,1280]{1,0:T(8,128)(2,1)S(1)} %get-tuple-element.53), channel_id=1, source_target_pairs={{0,16},{8,24},{16,0},{24,8},{1,17},{9,25},{17,1},{25,9},{2,18},{10... | collective-permute-start | bytes 983048 | tf_op jit(solution)/shard_map/ppermute | solution.py:351
  25.1 3.7 %collective-permute-start.10 = (bf16[128,640]{1,0:T(8,128)(2,1)S(1)}, bf16[128,640]{1,0:T(8,128)(2,1)S(1)}, u32[]{:S(2)}, u32[]{:S(2)}) collective-permute-start(bf16[128,640]{1,0:T(8,128)(2,1)S(1)} %constant_dynamic-update-slice_fusion.refs_4_), channel_id=1, source_target_pairs={{0,1},{1,0},{2,3},{3,2},{4,5},{5,4},{6,7},{7,6},{8,9},{9,8},{10,11... | collective-permute-start | bytes 491528 | tf_op jit(solution)/shard_map/ppermute | solution.py:359
  30.0 4.0 %collective-permute-start.12 = (bf16[128,640]{1,0:T(8,128)(2,1)S(1)}, bf16[128,640]{1,0:T(8,128)(2,1)S(1)}, u32[]{:S(2)}, u32[]{:S(2)}) collective-permute-start(bf16[128,640]{1,0:T(8,128)(2,1)S(1)} %collective-permute-done.8.refs_6_), channel_id=1, source_target_pairs={{0,1},{1,0},{2,3},{3,2},{4,5},{5,4},{6,7},{7,6},{8,9},{9,8},{10,11... | collective-permute-start | bytes 491528 | tf_op jit(solution)/shard_map/ppermute | solution.py:359
  34.0 1.6 %collective-permute-start.11 = (bf16[128,640]{1,0:T(8,128)(2,1)S(1)}, bf16[128,640]{1,0:T(8,128)(2,1)S(1)}, u32[]{:S(2)}, u32[]{:S(2)}) collective-permute-start(bf16[128,640]{1,0:T(8,128)(2,1)S(1)} %collective-permute-done.7.refs_5_), channel_id=1, source_target_pairs={{0,1},{1,0},{2,3},{3,2},{4,5},{5,4},{6,7},{7,6},{8,9},{9,8},{10,11... | collective-permute-start | bytes 491528 | tf_op jit(solution)/shard_map/ppermute | solution.py:359
  36.7 16.3 %pair.1 = (bf16[4,128,640]{2,1,0:T(8,128)(2,1)}, bf16[4,128,640]{2,1,0:T(8,128)(2,1)}, bf16[128,512]{1,0:T(8,128)(2,1)}, bf16[128,512]{1,0:T(8,128)(2,1)}, bf16[...) custom-call(s32[4]{0:T(128)S(1)} %pad_add_fusion.where_ref, ...), custom_call_target="tpu_custom_call" | custom-call | flops 8000000000 | bytes 10000000 | tf_op jit(solution)/shard_map/pair/pallas_call | solution.py:203
  53.4 8.3 %all-to-all-start = ((bf16[8,64,1024]{2,1,0:T(8,128)(2,1)}), bf16[8,64,1024]{2,1,0:T(8,128)(2,1)S(1)}, u32[]{:S(2)}, u32[]{:S(2)}) async-start(bf16[8,64,1024]{2,1,0:T(8,128)(2,1)} %bitcast.22), calls=%async_computation | async-start | bytes 2097152 | tf_op jit(solution)/shard_map/all_to_all | solution.py:347
  63.1 1.5 %collective-permute-start.17 = (bf16[128,640]{1,0:T(8,128)(2,1)S(1)}, bf16[128,640]{1,0:T(8,128)(2,1)S(1)}, u32[]{:S(2)}, u32[]{:S(2)}) collective-permute-start(bf16[128,640]{1,0:T(8,128)(2,1)S(1)} %get-tuple-element.85), channel_id=1, source_target_pairs={{0,24},{8,0},{16,8},{24,16},{1,25},{9,1},{17,9},{25,17},{2,26},{10... | collective-permute-start | bytes 491528 | tf_op jit(solution)/shard_map/ppermute | solution.py:351
  66.2 2.3 %collective-permute-done.15 = bf16[128,640]{1,0:T(8,128)(2,1)S(1)} collective-permute-done((bf16[128,640]{1,0:T(8,128)(2,1)S(1)}, bf16[128,640]{1,0:T(8,128)(2,1)S(1)}, u32[]{:S(2)}, u32[]{:S(2)}) %collective-permute-start.15) | collective-permute-done | bytes 163872 | tf_op jit(solution)/shard_map/ppermute | solution.py:351
  68.5 4.3 %collective-permute-done.16 = bf16[128,640]{1,0:T(8,128)(2,1)S(1)} collective-permute-done((bf16[128,640]{1,0:T(8,128)(2,1)S(1)}, bf16[128,640]{1,0:T(8,128)(2,1)S(1)}, u32[]{:S(2)}, u32[]{:S(2)}) %collective-permute-start.16) | collective-permute-done | bytes 163872 | tf_op jit(solution)/shard_map/ppermute | solution.py:351
  75.2 2.2 %collective-permute-start.23 = (bf16[128,512]{1,0:T(8,128)(2,1)S(1)}, bf16[128,512]{1,0:T(8,128)(2,1)S(1)}, u32[]{:S(2)}, u32[]{:S(2)}) collective-permute-start(bf16[128,512]{1,0:T(8,128)(2,1)S(1)} %copy-done.3), channel_id=1, source_target_pairs={{0,24},{8,0},{16,8},{24,16},{1,25},{9,1},{17,9},{25,17},{2,26},{10... | collective-permute-start | bytes 393224 | tf_op jit(solution)/shard_map/ppermute | solution.py:351
  77.3 2.7 %collective-permute-done.22.refs_2_ = bf16[128,512]{1,0:T(8,128)(2,1)S(1)} collective-permute-done((bf16[128,512]{1,0:T(8,128)(2,1)S(1)}, bf16[128,512]{1,0:T(8,128)(2,1)S(1)}, u32[]{:S(2)}, u32[]{:S(2)}) %collective-permute-start.22) | collective-permute-done | bytes 131104 | tf_op jit(solution)/shard_map/ppermute | solution.py:351
  80.4 2.6 %collective-permute-done.18.refs_1_ = bf16[128,640]{1,0:T(8,128)(2,1)S(1)} collective-permute-done((bf16[128,640]{1,0:T(8,128)(2,1)S(1)}, bf16[128,640]{1,0:T(8,128)(2,1)S(1)}, u32[]{:S(2)}, u32[]{:S(2)}) %collective-permute-start.18) | collective-permute-done | bytes 163872 | tf_op jit(solution)/shard_map/ppermute | solution.py:351
  85.0 1.4 %attended.1 = bf16[128,2048]{1,0:T(8,128)(2,1)} custom-call(s32[4]{0:T(128)S(1)} %pad_add_fusion.where_ref, bf16[128,512]{1,0:T(8,128)(2,1)S(1)} %copy-done.1, bf16[128,512]{1,0:T(8,128)(2,1)S(1)} %collective-permute-done.21.refs_1_, bf16[128,512]{1,0:T(8,128)(2,1)S(1)} %collective-permute-done.22.refs_2_, bf16[128,512]{1,0:T(8,128)(2,1)S(1)} %collective-permute-done.23.refs_3_), custom_call_target="tpu_custom_call" | custom-call | tf_op jit(solution)/shard_map/attended/pallas_call | solution.py:291
  86.4 2.8 %collective-permute-done.24 = bf16[64,640]{1,0:T(8,128)(2,1)S(1)} collective-permute-done((bf16[64,640]{1,0:T(8,128)(2,1)S(1)}, bf16[64,640]{1,0:T(8,128)(2,1)S(1)}, u32[]{:S(2)}, u32[]{:S(2)}) %collective-permute-start.24) | collective-permute-done | bytes 81952 | tf_op jit(solution)/shard_map/ppermute | solution.py:397
  89.2 2.9 %collective-permute-start.25 = (f32[64,640]{1,0:T(8,128)S(1)}, f32[64,640]{1,0:T(8,128)S(1)}, u32[]{:S(2)}, u32[]{:S(2)}) collective-permute-start(f32[64,640]{1,0:T(8,128)S(1)} %convert_add_fusion.mine_ref), channel_id=1, source_target_pairs={{0,1},{1,0},{2,3},{3,2},{4,5},{5,4},{6,7},{7,6},{8,9},{9,8},{10,11... | collective-permute-start | bytes 491528 | tf_op jit(solution)/shard_map/ppermute | solution.py:359
  93.3 2.1 %collective-permute-start.27 = (bf16[16,1024]{1,0:T(8,128)(2,1)S(1)}, bf16[16,1024]{1,0:T(8,128)(2,1)S(1)}, u32[]{:S(2)}, u32[]{:S(2)}) collective-permute-start(bf16[16,1024]{1,0:T(8,128)(2,1)S(1)} %get-tuple-element.80), channel_id=1, source_target_pairs={{0,16},{8,24},{16,0},{24,8},{1,17},{9,25},{17,1},{25,9},{2,18},{10... | collective-permute-start | bytes 98312 | tf_op jit(solution)/shard_map/ppermute | solution.py:351
  95.8 1.4 %join.1 = f32[576,128]{1,0:T(8,128)} custom-call(s32[4]{0:T(128)S(1)} %pad_add_fusion.where_ref, f32[64,640]{1,0:T(8,128)S(1)} %convert_add_fusion.mine_ref, f32[64,640]{1,0:T(8,128)S(1)} %collective-permute-done.25.other_ref), custom_call_target="tpu_custom_call" | custom-call | tf_op jit(solution)/shard_map/join/pallas_call | solution.py:271
  (70 shorter events, 19.5 us)
Async XLA Ops:
  1.9 6.5 %collective-permute-start = (bf16[16,640]{1,0:T(8,128)(2,1)S(1)}, bf16[16,640]{1,0:T(8,128)(2,1)S(1)}, u32[]{:S(2)}, u32[]{:S(2)}) collective-permute-start(bf16[16,640]{1,0:T(8,128)(2,1)S(1)} %pad_maximum_fusion), channel_id=1, source_target_pairs={{0,32},{32,64},{64,96},{96,128},{128,160},{160,192},{192,224},{1,3... | collective-permute-start | bytes 61448 | tf_op jit(solution)/shard_map/ppermute | solution.py:375
  8.5 11.3 %collective-permute-start.4 = (bf16[128,1280]{1,0:T(8,128)(2,1)S(1)}, bf16[128,1280]{1,0:T(8,128)(2,1)S(1)}, u32[]{:S(2)}, u32[]{:S(2)}) collective-permute-start(bf16[128,1280]{1,0:T(8,128)(2,1)S(1)} %get-tuple-element.50), channel_id=1, source_target_pairs={{0,8},{8,16},{16,24},{24,0},{1,9},{9,17},{17,25},{25,1},{2,10},{10... | collective-permute-start | bytes 983048 | tf_op jit(solution)/shard_map/ppermute | solution.py:351
  9.8 10.0 %collective-permute-start.5 = (bf16[128,1280]{1,0:T(8,128)(2,1)S(1)}, bf16[128,1280]{1,0:T(8,128)(2,1)S(1)}, u32[]{:S(2)}, u32[]{:S(2)}) collective-permute-start(bf16[128,1280]{1,0:T(8,128)(2,1)S(1)} %get-tuple-element.51), channel_id=1, source_target_pairs={{0,24},{8,0},{16,8},{24,16},{1,25},{9,1},{17,9},{25,17},{2,26},{10... | collective-permute-start | bytes 983048 | tf_op jit(solution)/shard_map/ppermute | solution.py:351
  11.3 7.3 %collective-permute-start.3 = (bf16[32,640]{1,0:T(8,128)(2,1)S(1)}, bf16[32,640]{1,0:T(8,128)(2,1)S(1)}, u32[]{:S(2)}, u32[]{:S(2)}) collective-permute-start(bf16[32,640]{1,0:T(8,128)(2,1)S(1)} %maximum_maximum_fusion), channel_id=1, source_target_pairs={{0,24},{8,0},{16,8},{24,16},{1,25},{9,1},{17,9},{25,17},{2,26},{10... | collective-permute-start | bytes 122888 | tf_op jit(solution)/shard_map/ppermute | solution.py:351
  12.7 7.1 %collective-permute-start.2 = (bf16[32,640]{1,0:T(8,128)(2,1)S(1)}, bf16[32,640]{1,0:T(8,128)(2,1)S(1)}, u32[]{:S(2)}, u32[]{:S(2)}) collective-permute-start(bf16[32,640]{1,0:T(8,128)(2,1)S(1)} %maximum_maximum_fusion), channel_id=1, source_target_pairs={{0,16},{8,24},{16,0},{24,8},{1,17},{9,25},{17,1},{25,9},{2,18},{10... | collective-permute-start | bytes 122888 | tf_op jit(solution)/shard_map/ppermute | solution.py:351
  13.1 6.7 %collective-permute-start.1 = (bf16[32,640]{1,0:T(8,128)(2,1)S(1)}, bf16[32,640]{1,0:T(8,128)(2,1)S(1)}, u32[]{:S(2)}, u32[]{:S(2)}) collective-permute-start(bf16[32,640]{1,0:T(8,128)(2,1)S(1)} %maximum_maximum_fusion), channel_id=1, source_target_pairs={{0,8},{8,16},{16,24},{24,0},{1,9},{9,17},{17,25},{25,1},{2,10},{10... | collective-permute-start | bytes 122888 | tf_op jit(solution)/shard_map/ppermute | solution.py:351
  19.9 8.9 %collective-permute-start.9 = (bf16[128,640]{1,0:T(8,128)(2,1)S(1)}, bf16[128,640]{1,0:T(8,128)(2,1)S(1)}, u32[]{:S(2)}, u32[]{:S(2)}) collective-permute-start(bf16[128,640]{1,0:T(8,128)(2,1)S(1)} %constant_dynamic-update-slice_fusion.refs_4_), channel_id=1, source_target_pairs={{0,6},{2,0},{4,2},{6,4},{1,7},{3,1},{5,3},{7,5},{8,14},{10,8},{12,... | collective-permute-start | bytes 491528 | tf_op jit(solution)/shard_map/ppermute | solution.py:351
  22.4 13.2 %collective-permute-start.6 = (bf16[128,1280]{1,0:T(8,128)(2,1)S(1)}, bf16[128,1280]{1,0:T(8,128)(2,1)S(1)}, u32[]{:S(2)}, u32[]{:S(2)}) collective-permute-start(bf16[128,1280]{1,0:T(8,128)(2,1)S(1)} %get-tuple-element.53), channel_id=1, source_target_pairs={{0,16},{8,24},{16,0},{24,8},{1,17},{9,25},{17,1},{25,9},{2,18},{10... | collective-permute-start | bytes 983048 | tf_op jit(solution)/shard_map/ppermute | solution.py:351
  23.9 6.1 %collective-permute-start.8 = (bf16[128,640]{1,0:T(8,128)(2,1)S(1)}, bf16[128,640]{1,0:T(8,128)(2,1)S(1)}, u32[]{:S(2)}, u32[]{:S(2)}) collective-permute-start(bf16[128,640]{1,0:T(8,128)(2,1)S(1)} %constant_dynamic-update-slice_fusion.refs_4_), channel_id=1, source_target_pairs={{0,4},{2,6},{4,0},{6,2},{1,5},{3,7},{5,1},{7,3},{8,12},{10,14},{12... | collective-permute-start | bytes 491528 | tf_op jit(solution)/shard_map/ppermute | solution.py:351
  24.4 9.6 %collective-permute-start.7 = (bf16[128,640]{1,0:T(8,128)(2,1)S(1)}, bf16[128,640]{1,0:T(8,128)(2,1)S(1)}, u32[]{:S(2)}, u32[]{:S(2)}) collective-permute-start(bf16[128,640]{1,0:T(8,128)(2,1)S(1)} %constant_dynamic-update-slice_fusion.refs_4_), channel_id=1, source_target_pairs={{0,2},{2,4},{4,6},{6,0},{1,3},{3,5},{5,7},{7,1},{8,10},{10,12},{12... | collective-permute-start | bytes 491528 | tf_op jit(solution)/shard_map/ppermute | solution.py:351
  25.1 10.6 %collective-permute-start.10 = (bf16[128,640]{1,0:T(8,128)(2,1)S(1)}, bf16[128,640]{1,0:T(8,128)(2,1)S(1)}, u32[]{:S(2)}, u32[]{:S(2)}) collective-permute-start(bf16[128,640]{1,0:T(8,128)(2,1)S(1)} %constant_dynamic-update-slice_fusion.refs_4_), channel_id=1, source_target_pairs={{0,1},{1,0},{2,3},{3,2},{4,5},{5,4},{6,7},{7,6},{8,9},{9,8},{10,11... | collective-permute-start | bytes 491528 | tf_op jit(solution)/shard_map/ppermute | solution.py:359
  28.8 6.9 %collective-permute-start.13 = (bf16[128,640]{1,0:T(8,128)(2,1)S(1)}, bf16[128,640]{1,0:T(8,128)(2,1)S(1)}, u32[]{:S(2)}, u32[]{:S(2)}) collective-permute-start(bf16[128,640]{1,0:T(8,128)(2,1)S(1)} %collective-permute-done.9.refs_7_), channel_id=1, source_target_pairs={{0,1},{1,0},{2,3},{3,2},{4,5},{5,4},{6,7},{7,6},{8,9},{9,8},{10,11... | collective-permute-start | bytes 491528 | tf_op jit(solution)/shard_map/ppermute | solution.py:359
  30.0 5.7 %collective-permute-start.12 = (bf16[128,640]{1,0:T(8,128)(2,1)S(1)}, bf16[128,640]{1,0:T(8,128)(2,1)S(1)}, u32[]{:S(2)}, u32[]{:S(2)}) collective-permute-start(bf16[128,640]{1,0:T(8,128)(2,1)S(1)} %collective-permute-done.8.refs_6_), channel_id=1, source_target_pairs={{0,1},{1,0},{2,3},{3,2},{4,5},{5,4},{6,7},{7,6},{8,9},{9,8},{10,11... | collective-permute-start | bytes 491528 | tf_op jit(solution)/shard_map/ppermute | solution.py:359
  53.0 8.8 %collective-permute-start.14 = (bf16[4,128,640]{2,1,0:T(8,128)(2,1)}, bf16[4,128,640]{2,1,0:T(8,128)(2,1)S(1)}, u32[]{:S(2)}, u32[]{:S(2)}) collective-permute-start(bf16[4,128,640]{2,1,0:T(8,128)(2,1)} %get-tuple-element.60), channel_id=1, source_target_pairs={{0,1},{1,0},{2,3},{3,2},{4,5},{5,4},{6,7},{7,6},{8,9},{9,8},{10,11... | collective-permute-start | bytes 1966088 | tf_op jit(solution)/shard_map/ppermute | solution.py:359
  53.4 38.6 %all-to-all-start = ((bf16[8,64,1024]{2,1,0:T(8,128)(2,1)}), bf16[8,64,1024]{2,1,0:T(8,128)(2,1)S(1)}, u32[]{:S(2)}, u32[]{:S(2)}) async-start(bf16[8,64,1024]{2,1,0:T(8,128)(2,1)} %bitcast.22), calls=%async_computation | async-start | bytes 2097152 | tf_op jit(solution)/shard_map/all_to_all | solution.py:347
  61.9 6.6 %collective-permute-start.15 = (bf16[128,640]{1,0:T(8,128)(2,1)S(1)}, bf16[128,640]{1,0:T(8,128)(2,1)S(1)}, u32[]{:S(2)}, u32[]{:S(2)}) collective-permute-start(bf16[128,640]{1,0:T(8,128)(2,1)S(1)} %get-tuple-element.84), channel_id=1, source_target_pairs={{0,8},{8,16},{16,24},{24,0},{1,9},{9,17},{17,25},{25,1},{2,10},{10... | collective-permute-start | bytes 491528 | tf_op jit(solution)/shard_map/ppermute | solution.py:351
  64.7 8.1 %collective-permute-start.16 = (bf16[128,640]{1,0:T(8,128)(2,1)S(1)}, bf16[128,640]{1,0:T(8,128)(2,1)S(1)}, u32[]{:S(2)}, u32[]{:S(2)}) collective-permute-start(bf16[128,640]{1,0:T(8,128)(2,1)S(1)} %get-tuple-element.86), channel_id=1, source_target_pairs={{0,16},{8,24},{16,0},{24,8},{1,17},{9,25},{17,1},{25,9},{2,18},{10... | collective-permute-start | bytes 491528 | tf_op jit(solution)/shard_map/ppermute | solution.py:351
  65.4 9.8 %collective-permute-start.21 = (bf16[128,512]{1,0:T(8,128)(2,1)S(1)}, bf16[128,512]{1,0:T(8,128)(2,1)S(1)}, u32[]{:S(2)}, u32[]{:S(2)}) collective-permute-start(bf16[128,512]{1,0:T(8,128)(2,1)S(1)} %copy-done.5), channel_id=1, source_target_pairs={{0,8},{8,16},{16,24},{24,0},{1,9},{9,17},{17,25},{25,1},{2,10},{10... | collective-permute-start | bytes 393224 | tf_op jit(solution)/shard_map/ppermute | solution.py:351
  72.9 7.5 %collective-permute-start.20 = (bf16[128,640]{1,0:T(8,128)(2,1)S(1)}, bf16[128,640]{1,0:T(8,128)(2,1)S(1)}, u32[]{:S(2)}, u32[]{:S(2)}) collective-permute-start(bf16[128,640]{1,0:T(8,128)(2,1)S(1)} %fusion.2.refs_0_), channel_id=1, source_target_pairs={{0,6},{2,0},{4,2},{6,4},{1,7},{3,1},{5,3},{7,5},{8,14},{10,8},{12,... | collective-permute-start | bytes 491528 | tf_op jit(solution)/shard_map/ppermute | solution.py:351
  73.3 7.1 %collective-permute-start.19 = (bf16[128,640]{1,0:T(8,128)(2,1)S(1)}, bf16[128,640]{1,0:T(8,128)(2,1)S(1)}, u32[]{:S(2)}, u32[]{:S(2)}) collective-permute-start(bf16[128,640]{1,0:T(8,128)(2,1)S(1)} %fusion.2.refs_0_), channel_id=1, source_target_pairs={{0,4},{2,6},{4,0},{6,2},{1,5},{3,7},{5,1},{7,3},{8,12},{10,14},{12... | collective-permute-start | bytes 491528 | tf_op jit(solution)/shard_map/ppermute | solution.py:351
  73.8 9.2 %collective-permute-start.18 = (bf16[128,640]{1,0:T(8,128)(2,1)S(1)}, bf16[128,640]{1,0:T(8,128)(2,1)S(1)}, u32[]{:S(2)}, u32[]{:S(2)}) collective-permute-start(bf16[128,640]{1,0:T(8,128)(2,1)S(1)} %fusion.2.refs_0_), channel_id=1, source_target_pairs={{0,2},{2,4},{4,6},{6,0},{1,3},{3,5},{5,7},{7,1},{8,10},{10,12},{12... | collective-permute-start | bytes 491528 | tf_op jit(solution)/shard_map/ppermute | solution.py:351
  74.5 5.6 %collective-permute-start.22 = (bf16[128,512]{1,0:T(8,128)(2,1)S(1)}, bf16[128,512]{1,0:T(8,128)(2,1)S(1)}, u32[]{:S(2)}, u32[]{:S(2)}) collective-permute-start(bf16[128,512]{1,0:T(8,128)(2,1)S(1)} %copy-done.4), channel_id=1, source_target_pairs={{0,16},{8,24},{16,0},{24,8},{1,17},{9,25},{17,1},{25,9},{2,18},{10... | collective-permute-start | bytes 393224 | tf_op jit(solution)/shard_map/ppermute | solution.py:351
  83.7 5.5 %collective-permute-start.24 = (bf16[64,640]{1,0:T(8,128)(2,1)S(1)}, bf16[64,640]{1,0:T(8,128)(2,1)S(1)}, u32[]{:S(2)}, u32[]{:S(2)}) collective-permute-start(bf16[64,640]{1,0:T(8,128)(2,1)S(1)} %get-tuple-element.69), channel_id=1, source_target_pairs={{32,0},{64,32},{96,64},{128,96},{160,128},{192,160},{224,192},{33,... | collective-permute-start | bytes 245768 | tf_op jit(solution)/shard_map/ppermute | solution.py:397
  89.2 6.6 %collective-permute-start.25 = (f32[64,640]{1,0:T(8,128)S(1)}, f32[64,640]{1,0:T(8,128)S(1)}, u32[]{:S(2)}, u32[]{:S(2)}) collective-permute-start(f32[64,640]{1,0:T(8,128)S(1)} %convert_add_fusion.mine_ref), channel_id=1, source_target_pairs={{0,1},{1,0},{2,3},{3,2},{4,5},{5,4},{6,7},{7,6},{8,9},{9,8},{10,11... | collective-permute-start | bytes 491528 | tf_op jit(solution)/shard_map/ppermute | solution.py:359
  (12 other events, 122.0 us)
